TPU v7x, 32 devices: a whole 2x2x4 slice. The times are simulated.
32 devices in a mesh: dp: 8 (over y, x, core), tensor: 4 (over z).
Axes of the slice: x: 2, y: 2, z: 4, core: 2. Of those that a mesh axis runs over, the one named last changes fastest.
Arguments:
- block_input: bfloat16 [8, 2048, 768], P('dp', 'tensor'), may hold values from -6 to 6
- teacher: bfloat16 [8, 2048, 768], P('dp', 'tensor'), may hold values from -6 to 6
- segment_ids: int32 [8, 2048], P('dp', 'tensor'), may hold values from 0 to 7, never falling along the last dimension, each value on 1 to 800 neighbouring positions
- valid_mask: int32 [8, 2048], P('dp', 'tensor'), may hold values from 0 to 1
- ln1_gain: bfloat16 [768], P('dp'), may hold values from 0.5 to 1.5
- ln1_bias: bfloat16 [768], P('dp'), may hold values from -1.75 to 1.75
- qkv_weight: bfloat16 [3, 768, 768], P(None, 'dp', 'tensor'), may hold values from -0.21875 to 0.21875
- qv_bias: bfloat16 [2, 12, 64], P(None, 'tensor', 'dp'), may hold values from -1.75 to 1.75
- out_weight: bfloat16 [768, 768], P('tensor', 'dp'), may hold values from -0.875 to 0.875
- out_bias: bfloat16 [768], P('dp'), may hold values from -1.75 to 1.75
- ln2_gain: bfloat16 [768], P('dp'), may hold values from 0.5 to 1.5
- ln2_bias: bfloat16 [768], P('dp'), may hold values from -1.75 to 1.75
- fc_weight: bfloat16 [768, 3072], P('dp', 'tensor'), may hold values from -0.21875 to 0.21875
- fc_bias: bfloat16 [48, 64], P('tensor', 'dp'), may hold values from -1.75 to 1.75
- proj_weight: bfloat16 [3072, 768], P('tensor', 'dp'), may hold values from -0.109375 to 0.109375
- proj_bias: bfloat16 [768], P('dp'), may hold values from -1.75 to 1.75
Outputs:
- block_output: bfloat16 [8, 2048, 768], P('dp', 'tensor')
- loss: float32 [], replicated
- input_grad: float32 [8, 2048, 768], P('dp', 'tensor')
- grad_ln1_gain: float32 [768], P('dp')
- grad_ln1_bias: float32 [768], P('dp')
- grad_qkv_weight: float32 [3, 768, 768], P(None, 'dp', 'tensor')
- grad_qv_bias: float32 [2, 12, 64], P(None, 'tensor', 'dp')
- grad_out_weight: float32 [768, 768], P('tensor', 'dp')
- grad_out_bias: float32 [768], P('dp')
- grad_ln2_gain: float32 [768], P('dp')
- grad_ln2_bias: float32 [768], P('dp')
- grad_fc_weight: float32 [768, 3072], P('dp', 'tensor')
- grad_fc_bias: float32 [48, 64], P('tensor', 'dp')
- grad_proj_weight: float32 [3072, 768], P('tensor', 'dp')
- grad_proj_bias: float32 [768], P('dp')
Inputs may be any that keep to these rules, and one draw needn't show every extreme that they name: `segment_ids`: within a sequence segment ids never fall; every document has 1 to 800 tokens, one has exactly 800, and every id of 0 to 7 occurs.
All inputs are finite; a program needn't handle non-finite values.
Results may differ from a plain program's by a relative error of at most 0.014.
Values may be sent and summed in bfloat16 or wider, within the bound.
A program may use at most 128 MiB of HBM per device.

v0:
```python
import functools

import jax
import jax.numpy as jnp
from jax import lax
from jax.experimental import pallas as pl
from jax.experimental.pallas import tpu as pltpu
from jax.sharding import PartitionSpec as P

HD = 64
DOC_MOST = 800
KB = 128
QB = 256
DOCS = 8
WINDOW = -(-(DOC_MOST - 1) // KB) + QB // KB
EPSILON = 1e-05
TANH_SLOPE = 0.7978845608028654
CUBIC_TERM = 0.044715
MESH = pl.DeviceIdType.MESH
F32 = jnp.float32
BF16 = jnp.bfloat16
NN = (((1,), (0,)), ((), ()))
NT = (((1,), (1,)), ((), ()))


def mm(a, b, dims=NN):
    return lax.dot_general(a, b, dims, preferred_element_type=F32)


def halo_parts(tokens, ts):
    parts, left, back = [], DOC_MOST, 1
    while left > 0 and back < ts:
        parts.append((back, min(tokens, left)))
        left -= tokens
        back += 1
    return parts


class Gather:
    def __init__(self, dp, ts, ins, outs, z_send, z_recv, send_sem, recv_sem):
        self.dp, self.ts, self.ins, self.outs = dp, ts, ins, outs
        self.z_send, self.z_recv, self.send_sem, self.recv_sem = z_send, z_recv, send_sem, recv_sem
        self.me, self.mt = lax.axis_index("dp"), lax.axis_index("tensor")
        self.far = [1 << k for k in range(1, dp.bit_length() - 1)]
        self.keys = {}
        self.flight = []
        self.near = [sorted(range(ts), key=lambda t: (abs(t - m), t)) for m in range(ts)]

    @staticmethod
    def copies(dp, ts, parts):
        return parts * ts * (dp - 1)

    def t_of(self, k):
        t = jnp.int32(self.near[0][k])
        for m in range(1, self.ts):
            t = jnp.where(self.mt == m, self.near[m][k], t)
        return t

    def order(self, t):
        flip = t * 2 >= self.ts
        return [jnp.where(flip, b, a) for a, b in zip(self.far, self.far[::-1])]

    def place(self, c, t, dp_index):
        return self.outs[c].at[t, dp_index]

    def along(self, c, t, up):
        src = self.ins[c] if t is None else self.place(c, t, self.me)
        t = self.mt if t is None else t
        return pltpu.make_async_remote_copy(
            src_ref=src,
            dst_ref=self.place(c, t, self.me),
            send_sem=self.z_send.at[c, t, int(up)],
            recv_sem=self.z_recv.at[c, t],
            device_id={"tensor": self.mt + (1 if up else -1)},
            device_id_type=MESH,
        )

    def desc(self, key):
        c, k, known, i = key
        t = self.t_of(k)
        order = self.order(t)
        mask = jnp.int32(0)
        for b in known:
            mask = mask ^ order[b]
        ref = self.place(c, t, self.me ^ mask)
        own = k == 0 and not known
        n = self.keys.setdefault(key, len(self.keys))
        return pltpu.make_async_remote_copy(
            src_ref=self.ins[c] if own else ref,
            dst_ref=ref,
            send_sem=self.send_sem.at[n],
            recv_sem=self.recv_sem.at[n],
            device_id={"dp": self.me ^ (1 if i < 0 else order[i])},
            device_id_type=MESH,
        )

    def here(self, c, k, known):
        first = max(known) + 1 if known else 0
        for i in list(range(first, len(self.far))) + [-1]:
            key = (c, k, known, i)
            self.desc(key).start()
            self.flight.append(key)

    def start(self, c):
        @pl.when(self.mt + 1 < self.ts)
        def _():
            self.along(c, None, True).start()

        @pl.when(self.mt >= 1)
        def _():
            self.along(c, None, False).start()

        self.here(c, 0, ())

    def z_step(self, c, k):
        t = self.t_of(k)
        self.along(c, t, True).wait_recv()

        @pl.when((t < self.mt) & (self.mt + 1 < self.ts))
        def _():
            self.along(c, t, True).start()

        @pl.when((t > self.mt) & (self.mt >= 1))
        def _():
            self.along(c, t, False).start()

        self.here(c, k, ())

    def far_step(self, c, k, i):
        for key in [q for q in self.flight if q[:2] == (c, k) and q[3] == i]:
            self.desc(key).wait_recv()
            self.here(c, k, key[2] + (i,))

    def core_step(self, c, k):
        for key in [q for q in self.flight if q[:2] == (c, k) and q[3] < 0]:
            self.desc(key).wait_recv()

    def finish(self):
        for c in range(len(self.ins)):
            for k in range(self.ts):
                t = self.t_of(k)

                @pl.when((t <= self.mt) & (self.mt + 1 < self.ts))
                def _():
                    self.along(c, t, True).wait_send()

                @pl.when((t >= self.mt) & (self.mt >= 1))
                def _():
                    self.along(c, t, False).wait_send()

        for key in self.flight:
            self.desc(key).wait_send()


def meet(dp, ts):
    me, mt = lax.axis_index("dp"), lax.axis_index("tensor")
    bits = [1 << k for k in range(dp.bit_length() - 1)]
    barrier = pltpu.get_barrier_semaphore()
    for k in range(1, ts):
        pl.semaphore_signal(barrier, inc=1, device_id={"tensor": lax.rem(mt + k, ts)}, device_id_type=MESH)
    for b in bits:
        pl.semaphore_signal(barrier, inc=1, device_id={"dp": me ^ b}, device_id_type=MESH)
    pl.semaphore_wait(barrier, ts - 1 + len(bits))


def keep_lanes(block, head):
    lanes = lax.broadcasted_iota(jnp.int32, block.shape, 1)
    return jnp.where((lanes < HD) == (head == 0), block, jnp.zeros_like(block))


def fold_rows(block, op):
    return op(block.reshape(block.shape[0] // 8, 8, block.shape[1]), axis=0)


def swap_halves(block):
    return jnp.concatenate([block[:, HD:], block[:, :HD]], axis=1)


def lanes_of(low, high):
    lanes = lax.broadcasted_iota(jnp.int32, low.shape, 1)
    return jnp.where(lanes < HD, low, high)


def masked(s, i, doc_row, base):
    key = lax.broadcasted_iota(jnp.int32, s.shape, 0)
    ok = key >= doc_row - (base + i * KB)
    ahead = i - (WINDOW - QB // KB)
    if ahead >= 0:
        query = lax.broadcasted_iota(jnp.int32, s.shape, 1)
        ok = ok & (key + ahead * KB <= query)
    return jnp.where(ok, s, -1e30)


def normalize(values_in):
    center = values_in - jnp.mean(values_in, axis=-1, keepdims=True)
    scaler = lax.rsqrt(jnp.mean(center * center, axis=-1, keepdims=True) + EPSILON)
    return (center * scaler, scaler)


def merge_pairs(w_ref, h2_ref, ts):
    for a in range(ts // 2):
        tiles = []
        for t in (2 * a, 2 * a + 1):
            block = h2_ref[t].reshape(-1, 256)
            tiles.append((block[:, :128], block[:, 128:]))
        (qk0, vo0), (qk1, vo1) = tiles
        merged = [
            lanes_of(qk0, swap_halves(qk1)),
            lanes_of(swap_halves(qk0), qk1),
            lanes_of(vo0, swap_halves(vo1)),
            lanes_of(swap_halves(vo0), vo1),
        ]
        for i, m in enumerate(merged):
            w_ref[ts + a, :, :, i * 128 : (i + 1) * 128] = m.reshape(w_ref.shape[1], w_ref.shape[2], 128)


def weight_loads(qkvo_all, w_ref, h2_ref, sem, ts):
    res = []
    for t in range(ts):
        res.append(pltpu.make_async_copy(qkvo_all.at[t, :, :, pl.ds(0, 512)], w_ref.at[t], sem.at[2 * t]))
        res.append(pltpu.make_async_copy(qkvo_all.at[t, :, :, pl.ds(512, 256)], h2_ref.at[t], sem.at[2 * t + 1]))
    return res


def front_kernel(
    dp,
    ts,
    x_ref,
    seg_ref,
    small_ref,
    qkvo_ref,
    fc_ref,
    proj_ref,
    qkvo_all,
    fc_all,
    proj_all,
    vec_ref,
    doc_ref,
    normed_ref,
    q_ref,
    k_ref,
    v_ref,
    ot_ref,
    lse_ref,
    mixed_ref,
    hidden_ref,
    small_all,
    w_ref,
    h2_ref,
    halo_ref,
    hseg_ref,
    vt_ref,
    s_ref,
    local_sem,
    z_send,
    z_recv,
    send_sem,
    recv_sem,
    halo_send,
    halo_recv,
):
    me, mt = lax.axis_index("dp"), lax.axis_index("tensor")
    tokens, width = x_ref.shape
    halo = halo_ref.shape[0]
    ins = [small_ref, qkvo_ref, fc_ref, proj_ref]
    outs = [small_all, qkvo_all, fc_all, proj_all]
    halo_ref[...] = jnp.zeros_like(halo_ref)
    hseg_ref[...] = jnp.full_like(hseg_ref, -1)
    meet(dp, ts)
    net = Gather(dp, ts, ins, outs, z_send, z_recv, send_sem, recv_sem)
    stages = len(net.far)
    parts = halo_parts(tokens, ts)

    def halo_copies(i):
        back, count = parts[i]
        end = halo - sum(c for _, c in parts[:i])
        pairs = [
            (x_ref.at[pl.ds(tokens - count, count)], halo_ref.at[pl.ds(end - count, count)]),
            (seg_ref, hseg_ref.at[i]),
        ]
        return [
            pltpu.make_async_remote_copy(
                src_ref=src,
                dst_ref=dst,
                send_sem=halo_send.at[2 * i + n],
                recv_sem=halo_recv.at[2 * i + n],
                device_id={"tensor": lax.rem(mt + back, ts)},
                device_id_type=MESH,
            )
            for n, (src, dst) in enumerate(pairs)
        ]

    own = [
        pltpu.make_async_copy(ins[c], outs[c].at[mt, me], local_sem.at[2 * ts + c]) for c in range(4)
    ]
    net.start(0)
    net.start(1)
    for i, (back, _) in enumerate(parts):

        @pl.when(mt + back < ts)
        def _():
            for h in halo_copies(i):
                h.start()

    for c in own:
        c.start()
    for c in (0, 1):
        for k in range(1, ts):
            net.z_step(c, k)
    net.start(2)
    net.start(3)
    for c in (0, 1):
        for i in range(stages):
            for k in range(ts):
                net.far_step(c, k, i)
    own[0].wait()
    for k in range(ts):
        net.core_step(0, k)
    for t in range(ts):
        vec_ref[t] = jnp.sum(small_all[t], axis=0)

    def norm_rows(src, i, at):
        unit, _ = normalize(src[pl.ds(i * KB, KB), :].astype(F32))
        normed_ref[pl.ds(at + i * KB, KB), :] = (unit * vec_ref[0, 0:1, :] + vec_ref[0, 1:2, :]).astype(BF16)

    def own_rows(i, carry):
        norm_rows(x_ref, i, halo)
        return carry

    lax.fori_loop(0, tokens // KB, own_rows, 0)
    own[1].wait()
    for k in range(ts):
        net.core_step(1, k)
    loads = weight_loads(qkvo_all, w_ref, h2_ref, local_sem, ts)
    for load in loads:
        load.start()
    for load in loads:
        load.wait()
    merge_pairs(w_ref, h2_ref, ts)
    for i, (back, _) in enumerate(parts):

        @pl.when(mt >= back)
        def _():
            for h in halo_copies(i):
                h.wait_recv()

    def halo_rows(i, carry):
        norm_rows(halo_ref, i, 0)
        return carry

    lax.fori_loop(0, halo // KB, halo_rows, 0)

    seg_row = seg_ref[0:1, :]
    lanes = lax.broadcasted_iota(jnp.int32, (1, tokens), 1)
    doc = jnp.full((1, tokens), halo, jnp.int32)
    for value in range(DOCS):
        in_halo = jnp.zeros((1, 1), jnp.int32)
        for i, (_, count) in enumerate(parts):
            hit = (hseg_ref[i, 0:1, :] == value) & (lanes >= tokens - count)
            in_halo = in_halo + jnp.sum(hit.astype(jnp.int32), axis=1, keepdims=True)
        here = jnp.sum((seg_row == value).astype(jnp.int32), axis=1, keepdims=True)
        doc = doc - in_halo + jnp.where(seg_row > value, in_halo + here, 0)
    doc_ref[...] = jnp.broadcast_to(doc, doc_ref.shape)

    window = halo + tokens
    half_rows = window // 2

    def steps_at(p):
        work = {1: [(2, "z")], 2: [(2, 0)], 3: [(2, 1), (3, "z")], 4: [(3, 0)], 5: [(3, 1)]}
        for at, items in work.items():

            @pl.when(p == at)
            def _():
                for c, what in items:
                    if what == "z":
                        for k in range(1, ts):
                            net.z_step(c, k)
                    elif what < stages:
                        for k in range(ts):
                            net.far_step(c, k, what)

    def one_pair(p, carry):
        cols = pl.ds(pl.multiple_of(p * 128, 128), 128)
        t = jnp.minimum(p, ts - 1)
        a = jnp.maximum(p - ts, 0)
        low_q, high_q = vec_ref[2 * a, 7:8, 256:384], vec_ref[2 * a + 1, 7:8, 256:384]
        bias_q = jnp.where(p < ts, vec_ref[t, 7:8, 0:128], lanes_of(low_q, swap_halves(high_q)))
        bias_v = jnp.where(p < ts, vec_ref[t, 7:8, 128:256], lanes_of(swap_halves(low_q), high_q))
        w_q = w_ref[p, :, :, 0:128].reshape(width, 128)
        y = mm(normed_ref[pl.ds(halo, tokens), :], w_q) + bias_q
        q_ref[:, cols] = (y.astype(BF16) * 0.125).astype(BF16)

        def project(i, c):
            rows = pl.ds(pl.multiple_of(i * half_rows, 16), half_rows)
            w_kv = w_ref[p, :, :, 128:384].reshape(width, 256)
            kv = mm(normed_ref[rows, :], w_kv)
            k_ref[rows, cols] = kv[:, :128].astype(BF16)
            v_ref[rows, cols] = (kv[:, 128:] + bias_v).astype(BF16)
            return c

        lax.fori_loop(0, 2, project, 0)

        def turn(i, c):
            rows = pl.ds(pl.multiple_of(i * KB, KB), KB)
            vt_ref[:, rows] = v_ref[rows, cols].T
            return c

        lax.fori_loop(0, window // KB, turn, 0)

        def one_block(j, c):
            rows = pl.ds(pl.multiple_of(j * QB, QB), QB)
            q_block = q_ref[rows, cols]
            doc_row = doc_ref[0:1, rows]
            base = j * QB
            for h in range(2):
                query = keep_lanes(q_block, h)
                top = jnp.full((8, QB), -1e30, F32)
                for i in range(WINDOW):
                    span = pl.ds(pl.multiple_of(base + i * KB, KB), KB)
                    s = masked(mm(k_ref[span, cols], query, NT), i, doc_row, base)
                    s_ref[h, i] = s
                    top = jnp.maximum(top, fold_rows(s, jnp.max))
                top = jnp.max(top, axis=0, keepdims=True)
                total = jnp.zeros((8, QB), F32)
                acc = jnp.zeros((HD, QB), F32)
                for i in range(WINDOW):
                    span = pl.ds(pl.multiple_of(base + i * KB, KB), KB)
                    e = jnp.exp(s_ref[h, i] - top)
                    total = total + fold_rows(e, jnp.sum)
                    acc = acc + mm(vt_ref[h * HD : (h + 1) * HD, span], e.astype(BF16))
                total = jnp.sum(total, axis=0, keepdims=True)
                ot_ref[pl.ds(pl.multiple_of(p * 128 + h * HD, HD), HD), rows] = acc / total
                lse_ref[p, h : h + 1, rows] = top + jnp.log(total)
            o = ot_ref[pl.ds(pl.multiple_of(p * 128, 128), 128), rows]
            mixed_ref[rows, cols] = o.T.astype(BF16)
            return c

        lax.fori_loop(0, tokens // QB, one_block, 0)
        w_o = w_ref[p, :, :, 384:512].reshape(width, 128)
        start = jnp.where(p == 0, x_ref[...].astype(F32) + vec_ref[0, 2:3, :], hidden_ref[...])
        hidden_ref[...] = start + mm(mixed_ref[:, cols], w_o, NT)
        steps_at(p)
        return carry

    hidden_ref[...] = jnp.zeros_like(hidden_ref)
    lax.fori_loop(0, width // 128, one_pair, 0)
    for c in (2, 3):
        for k in range(ts):
            net.core_step(c, k)
    for c in own[2:]:
        c.wait()
    for i, (back, _) in enumerate(parts):

        @pl.when(mt + back < ts)
        def _():
            for h in halo_copies(i):
                h.wait_send()

    net.finish()


def front(x, seg, small, qkvo, fc, proj, dp, ts, halo):
    tokens, width = x.shape
    rows = fc.shape[0]
    window = halo + tokens
    pairs = width // 128
    copies = Gather.copies(dp, ts, 4)
    n_halo = len(halo_parts(tokens, ts))
    any_spec = pl.BlockSpec(memory_space=pl.ANY)
    vmem = pl.BlockSpec(memory_space=pltpu.VMEM)
    big = jax.ShapeDtypeStruct((ts, dp, rows, width), BF16)
    s = jax.ShapeDtypeStruct
    dma = pltpu.SemaphoreType.DMA
    return pl.pallas_call(
        functools.partial(front_kernel, dp, ts),
        out_shape=[
            big,
            big,
            big,
            s((ts, 8, width), F32),
            s((8, tokens), jnp.int32),
            s((window, width), BF16),
            s((tokens, width), BF16),
            s((window, width), BF16),
            s((window, width), BF16),
            s((width, tokens), F32),
            s((pairs, 2, tokens), F32),
            s((tokens, width), BF16),
            s((tokens, width), F32),
        ],
        in_specs=[vmem, vmem] + [any_spec] * 4,
        out_specs=[any_spec] * 3 + [vmem] * 10,
        scratch_shapes=[
            pltpu.VMEM((ts, dp, 8, width), F32),
            pltpu.VMEM((pairs, dp, rows, 512), BF16),
            pltpu.VMEM((ts, dp, rows, 256), BF16),
            pltpu.VMEM((halo, width), BF16),
            pltpu.VMEM((n_halo, 8, tokens), jnp.int32),
            pltpu.VMEM((128, window), BF16),
            pltpu.VMEM((2, WINDOW, KB, QB), F32),
            dma((2 * ts + 4,)),
            dma((4, ts, 2)),
            dma((4, ts)),
            dma((copies,)),
            dma((copies,)),
            dma((2 * n_halo,)),
            dma((2 * n_halo,)),
        ],
        compiler_params=pltpu.CompilerParams(
            collective_id=1, has_side_effects=True, vmem_limit_bytes=62 << 20
        ),
        name="front",
    )(x, seg, small, qkvo, fc, proj)


def gather_kernel(dp, ts, tokens, n_in, *refs):
    w_refs, (x_ref, seg_ref) = refs[:n_in], refs[n_in : n_in + 2]
    outs = refs[n_in + 2 : 2 * n_in + 2]
    halo_ref, hseg_ref = refs[2 * n_in + 2 : 2 * n_in + 4]
    local_sem, send_sem, recv_sem, halo_send, halo_recv = refs[2 * n_in + 4 :]
    me = lax.axis_index("dp")
    mt = lax.axis_index("tensor")
    bits = [1 << k for k in range(dp.bit_length() - 1)]
    far = bits[1:]
    halo_ref[...] = jnp.zeros_like(halo_ref)
    hseg_ref[...] = jnp.full_like(hseg_ref, -1)
    barrier = pltpu.get_barrier_semaphore()
    peers_t = [lax.rem(mt + k, ts) for k in range(1, ts)]
    for t in peers_t:
        pl.semaphore_signal(barrier, inc=1, device_id={"tensor": t}, device_id_type=MESH)
    for b in bits:
        pl.semaphore_signal(barrier, inc=1, device_id={"dp": me ^ b}, device_id_type=MESH)
    pl.semaphore_wait(barrier, len(peers_t) + len(bits))
    started = []

    def rcopy(src, dst, dev):
        i = len(started)
        c = pltpu.make_async_remote_copy(
            src_ref=src,
            dst_ref=dst,
            send_sem=send_sem.at[i],
            recv_sem=recv_sem.at[i],
            device_id=dev,
            device_id_type=MESH,
        )
        c.start()
        started.append(c)
        return c

    locals_, over_z = [], []
    for c in range(n_in):
        copy = pltpu.make_async_copy(w_refs[c], outs[c].at[mt, me], local_sem.at[c])
        copy.start()
        locals_.append(copy)
        over_z.append([rcopy(w_refs[c], outs[c].at[mt, me], {"tensor": t}) for t in peers_t])
        if c == min(1, n_in - 1):
            end = halo_ref.shape[0]
            halos = []
            for i, (back, count) in enumerate(halo_parts(tokens, ts)):
                end -= count
                pair = [
                    pltpu.make_async_remote_copy(
                        src_ref=src,
                        dst_ref=dst,
                        send_sem=halo_send.at[2 * i + k],
                        recv_sem=halo_recv.at[2 * i + k],
                        device_id={"tensor": lax.rem(mt + back, ts)},
                        device_id_type=MESH,
                    )
                    for k, (src, dst) in enumerate(
                        [
                            (x_ref.at[pl.ds(tokens - count, count)], halo_ref.at[pl.ds(end, count)]),
                            (seg_ref, hseg_ref.at[i]),
                        ]
                    )
                ]
                halos.append((back, pair))

                @pl.when(mt + back < ts)
                def _():
                    for h in pair:
                        h.start()

    half = max(ts // 2, 1)
    groups = [(0, half, far)] + ([(half, ts - half, far[::-1])] if ts > half else [])

    def spread(c, group, masks, later):
        res = {}
        for b in later + [1]:
            res[b] = []
            for m in masks:
                ref = outs[c].at[pl.ds(group[0], group[1]), me ^ m]
                res[b].append((m, rcopy(ref, ref, {"dp": me ^ b})))
        return res

    stages = len(far) + 1
    pending = {}
    for step in range(n_in + stages - 1):
        for s in range(stages):
            c = step - s
            if not 0 <= c < n_in:
                continue
            if s == 0:
                locals_[c].wait()
                for k in over_z[c]:
                    k.wait_recv()
            for gi, group in enumerate(groups):
                if s == 0:
                    pending[c, gi] = [spread(c, group, [0], group[2])]
                else:
                    b = group[2][s - 1]
                    masks = []
                    for res in pending[c, gi]:
                        for m, k in res.get(b, []):
                            k.wait_recv()
                            masks.append(m ^ b)
                    pending[c, gi].append(spread(c, group, masks, group[2][s:]))
    for c in range(n_in):
        for gi in range(len(groups)):
            for res in pending[c, gi]:
                for m, k in res[1]:
                    k.wait_recv()
    for back, pair in halos:

        @pl.when(mt >= back)
        def _():
            for h in pair:
                h.wait_recv()

        @pl.when(mt + back < ts)
        def _():
            for h in pair:
                h.wait_send()

    for k in started:
        k.wait_send()


def gather(parts, x, seg, dp, ts, halo):
    n_in = len(parts)
    tokens = x.shape[0]
    copies = n_in * ((ts - 1) + (2 if ts > 1 else 1) * (dp - 1))
    n_halo = len(halo_parts(tokens, ts))
    any_spec = pl.BlockSpec(memory_space=pl.ANY)
    vmem = pl.BlockSpec(memory_space=pltpu.VMEM)
    return pl.pallas_call(
        functools.partial(gather_kernel, dp, ts, tokens, n_in),
        out_shape=[jax.ShapeDtypeStruct((ts, dp) + p.shape, p.dtype) for p in parts]
        + [
            jax.ShapeDtypeStruct((halo, x.shape[1]), x.dtype),
            jax.ShapeDtypeStruct((n_halo,) + seg.shape, seg.dtype),
        ],
        in_specs=[any_spec] * (n_in + 2),
        out_specs=[any_spec] * n_in + [vmem, vmem],
        scratch_shapes=[
            pltpu.SemaphoreType.DMA((n_in,)),
            pltpu.SemaphoreType.DMA((copies,)),
            pltpu.SemaphoreType.DMA((copies,)),
            pltpu.SemaphoreType.DMA((2 * n_halo,)),
            pltpu.SemaphoreType.DMA((2 * n_halo,)),
        ],
        compiler_params=pltpu.CompilerParams(collective_id=1, has_side_effects=True),
        name="gather",
    )(*parts, x, seg)


def reduce_kernel(dp, ts, g_ref, out_ref, in_core, in_far, in_z, send_sem, recv_sem):
    n_c = g_ref.shape[0]
    me = lax.axis_index("dp")
    mt = lax.axis_index("tensor")
    bits = [1 << k for k in range(dp.bit_length() - 1)]
    far = bits[1:]
    barrier = pltpu.get_barrier_semaphore()
    peers_t = [lax.rem(mt + k, ts) for k in range(1, ts)]
    for t in peers_t:
        pl.semaphore_signal(barrier, inc=1, device_id={"tensor": t}, device_id_type=MESH)
    for b in bits:
        pl.semaphore_signal(barrier, inc=1, device_id={"dp": me ^ b}, device_id_type=MESH)
    pl.semaphore_wait(barrier, len(peers_t) + len(bits))
    started = []

    def rcopy(src, dst, dev):
        i = len(started)
        c = pltpu.make_async_remote_copy(
            src_ref=src,
            dst_ref=dst,
            send_sem=send_sem.at[i],
            recv_sem=recv_sem.at[i],
            device_id=dev,
            device_id_type=MESH,
        )
        c.start()
        started.append(c)
        return c

    half = max(ts // 2, 1)
    groups = [(0, half, far[::-1])] + ([(half, ts - half, far)] if ts > half else [])
    evens = list(range(0, dp, 2))
    core = []
    for c in range(n_c):
        core.append(
            {
                m: rcopy(g_ref.at[c, :, me ^ 1 ^ m], in_core.at[c, m >> 1], {"dp": me ^ 1})
                for m in evens[::-1]
            }
        )

    def add_into(dst, src, base, count):
        def one(i, carry):
            dst[base + i] = (dst[base + i].astype(F32) + src[i].astype(F32)).astype(BF16)
            return carry

        lax.fori_loop(0, count, one, 0)

    stages = len(far) + 2
    pending = {}
    slots = {}
    for step in range(n_c + stages - 1):
        for s in range(stages):
            c = step - s
            if not 0 <= c < n_c:
                continue
            if s == 0:
                for m in evens[::-1]:
                    core[c][m].wait_recv()

                    def one(i, carry, m=m):
                        in_core[c, m >> 1, i] = (
                            in_core[c, m >> 1, i].astype(F32) + g_ref[c, i, me ^ m].astype(F32)
                        ).astype(BF16)
                        return carry

                    lax.fori_loop(0, ts, one, 0)
            for gi, (t0, tn, order) in enumerate(groups):
                if s > 0:
                    for m, slot, k in pending.pop((c, gi)):
                        k.wait_recv()
                        add_into(in_core.at[c, m >> 1], in_far.at[c, slot, pl.ds(t0, tn)], t0, tn)
                if s < len(far):
                    b = order[s]
                    done = sum(order[:s])
                    masks = [m for m in evens if m & b and not m & done]
                    sent = []
                    for m in masks:
                        slot = slots.get((c, gi), 0)
                        slots[c, gi] = slot + 1
                        k = rcopy(
                            in_core.at[c, m >> 1, pl.ds(t0, tn)],
                            in_far.at[c, slot, pl.ds(t0, tn)],
                            {"dp": me ^ b},
                        )
                        sent.append((m ^ b, slot, k))
                    pending[c, gi] = sent
                elif s == len(far):
                    pending[c, gi] = []
            if s == len(far):
                pending[c, "z"] = [
                    rcopy(in_core.at[c, 0, lax.rem(mt + k, ts)], in_z.at[c, k - 1], {"tensor": lax.rem(mt + k, ts)})
                    for k in range(1, ts)
                ]
            if s == len(far) + 1:
                total = in_core[c, 0, mt].astype(F32)
                for k in pending[c, "z"]:
                    k.wait_recv()
                for k in range(ts - 1):
                    total = total + in_z[c, k].astype(F32)
                out_ref[c] = total
    for k in started:
        k.wait_send()


def reduce(grads, dp, ts):
    n_c, _, _, rows, width = grads.shape
    n_far = dp // 2 - 1
    groups = 2 if ts > 1 else 1
    copies = n_c * (dp // 2 + groups * n_far + ts - 1)
    vmem = pl.BlockSpec(memory_space=pltpu.VMEM)
    return pl.pallas_call(
        functools.partial(reduce_kernel, dp, ts),
        out_shape=jax.ShapeDtypeStruct((n_c, rows, width), F32),
        in_specs=[vmem],
        out_specs=vmem,
        scratch_shapes=[
            pltpu.VMEM((n_c, dp // 2, ts, rows, width), BF16),
            pltpu.VMEM((n_c, n_far, ts, rows, width), BF16),
            pltpu.VMEM((n_c, ts - 1, rows, width), BF16),
            pltpu.SemaphoreType.DMA((copies,)),
            pltpu.SemaphoreType.DMA((copies,)),
        ],
        compiler_params=pltpu.CompilerParams(
            collective_id=2, has_side_effects=True, vmem_limit_bytes=62 << 20
        ),
        name="reduce",
    )(grads)


def allowed_at(chunk, doc_row, first_q):
    key = chunk * KB + lax.broadcasted_iota(jnp.int32, (KB, QB), 0)
    query = first_q + lax.broadcasted_iota(jnp.int32, (KB, QB), 1)
    return (key >= doc_row) & (key <= query)


def attend_kernel(halo, first_ref, doc_ref, q_ref, k_ref, vt_ref, o_ref, lse_ref, s_ref):
    for j in range(q_ref.shape[0] // QB):
        rows = pl.ds(j * QB, QB)
        q_block = q_ref[rows, :]
        queries = [keep_lanes(q_block, h) for h in range(2)]
        doc_row = doc_ref[0:1, rows]
        first_q = halo + j * QB
        begin = first_ref[j]
        end = (first_q + QB) // KB

        def score(c, tops):
            keys = k_ref[pl.ds(pl.multiple_of(c * KB, KB), KB), :]
            ok = allowed_at(c, doc_row, first_q)
            res = []
            for h in range(2):
                s = jnp.where(ok, mm(keys, queries[h], NT), -1e30)
                s_ref[h, c] = s
                res.append(jnp.maximum(tops[h], fold_rows(s, jnp.max)))
            return tuple(res)

        tops = lax.fori_loop(begin, end, score, (jnp.full((8, QB), -1e30, F32),) * 2)
        tops = [jnp.max(t, axis=0, keepdims=True) for t in tops]

        def mix(c, carry):
            res = []
            for h in range(2):
                total, acc = carry[h]
                p = jnp.exp(s_ref[h, c] - tops[h])
                total = total + fold_rows(p, jnp.sum)
                vt = vt_ref[pl.ds(h * HD, HD), pl.ds(pl.multiple_of(c * KB, KB), KB)]
                acc = acc + mm(vt, p.astype(BF16))
                res.append((total, acc))
            return tuple(res)

        carry = lax.fori_loop(
            begin, end, mix, ((jnp.zeros((8, QB), F32), jnp.zeros((HD, QB), F32)),) * 2
        )
        for h in range(2):
            total = jnp.sum(carry[h][0], axis=0, keepdims=True)
            o_ref[pl.ds(h * HD, HD), rows] = carry[h][1] / total
            lse_ref[0, h : h + 1, rows] = tops[h] + jnp.log(total)


def attend(first, doc, q, k, vt, halo):
    tokens, width = q.shape
    keys = k.shape[0]
    pairs = width // 128
    return pl.pallas_call(
        functools.partial(attend_kernel, halo),
        out_shape=[
            jax.ShapeDtypeStruct((width, tokens), F32),
            jax.ShapeDtypeStruct((pairs, 2, tokens), F32),
        ],
        grid_spec=pltpu.PrefetchScalarGridSpec(
            num_scalar_prefetch=1,
            grid=(pairs,),
            in_specs=[
                pl.BlockSpec((1, tokens), lambda p, f: (0, 0)),
                pl.BlockSpec((tokens, 128), lambda p, f: (0, p)),
                pl.BlockSpec((keys, 128), lambda p, f: (0, p)),
                pl.BlockSpec((128, keys), lambda p, f: (p, 0)),
            ],
            out_specs=[
                pl.BlockSpec((128, tokens), lambda p, f: (p, 0)),
                pl.BlockSpec((1, 2, tokens), lambda p, f: (p, 0, 0)),
            ],
            scratch_shapes=[pltpu.VMEM((2, keys // KB, KB, QB), F32)],
        ),
        name="attend",
    )(first, doc, q, k, vt)


def attend_back_kernel(
    halo, first_ref, doc_ref, q_ref, k_ref, kt_ref, v_ref, do_ref, lse_ref, delta_ref, dq_ref, dk_ref, dv_ref
):
    dk_ref[...] = jnp.zeros_like(dk_ref)
    dv_ref[...] = jnp.zeros_like(dv_ref)
    for j in range(q_ref.shape[0] // QB):
        rows = pl.ds(j * QB, QB)
        q_block, do_block = q_ref[rows, :], do_ref[rows, :]
        queries = [keep_lanes(q_block, h) for h in range(2)]
        grads = [keep_lanes(do_block, h) for h in range(2)]
        doc_row = doc_ref[0:1, rows]
        first_q = halo + j * QB

        def step(c, carry):
            span = pl.ds(pl.multiple_of(c * KB, KB), KB)
            keys, values = k_ref[span, :], v_ref[span, :]
            ok = allowed_at(c, doc_row, first_q)
            res = []
            grad_k = grad_v = None
            for h in range(2):
                s = jnp.where(ok, mm(keys, queries[h], NT), -1e30)
                p = jnp.exp(s - lse_ref[0, h : h + 1, rows])
                dp_ = mm(values, grads[h], NT)
                ds = (p * (dp_ - delta_ref[0, h : h + 1, rows])).astype(BF16)
                gv = mm(p.astype(BF16), grads[h])
                gk = mm(ds, queries[h])
                grad_v = gv if grad_v is None else grad_v + gv
                grad_k = gk if grad_k is None else grad_k + gk
                kt = kt_ref[pl.ds(h * HD, HD), span]
                res.append(carry[h] + mm(kt, ds))
            dk_ref[span, :] += grad_k
            dv_ref[span, :] += grad_v
            return tuple(res)

        carry = lax.fori_loop(
            first_ref[j], (first_q + QB) // KB, step, (jnp.zeros((HD, QB), F32),) * 2
        )
        for h in range(2):
            dq_ref[pl.ds(h * HD, HD), rows] = carry[h] * 0.125


def attend_back(first, doc, q, k, kt, v, do, lse, delta, halo):
    tokens, width = q.shape
    keys = k.shape[0]
    pairs = width // 128
    q_spec = pl.BlockSpec((tokens, 128), lambda p, f: (0, p))
    k_spec = pl.BlockSpec((keys, 128), lambda p, f: (0, p))
    stat = pl.BlockSpec((1, 2, tokens), lambda p, f: (p, 0, 0))
    return pl.pallas_call(
        functools.partial(attend_back_kernel, halo),
        out_shape=[
            jax.ShapeDtypeStruct((width, tokens), F32),
            jax.ShapeDtypeStruct((keys, width), F32),
            jax.ShapeDtypeStruct((keys, width), F32),
        ],
        grid_spec=pltpu.PrefetchScalarGridSpec(
            num_scalar_prefetch=1,
            grid=(pairs,),
            in_specs=[
                pl.BlockSpec((1, tokens), lambda p, f: (0, 0)),
                q_spec,
                k_spec,
                pl.BlockSpec((128, keys), lambda p, f: (p, 0)),
                k_spec,
                q_spec,
                stat,
                stat,
            ],
            out_specs=[pl.BlockSpec((128, tokens), lambda p, f: (p, 0)), k_spec, k_spec],
        ),
        name="attend_back",
    )(first, doc, q, k, kt, v, do, lse, delta)


def gelu_tanh(values_in):
    return (
        0.5
        * values_in
        * (
            1.0
            + jnp.tanh(TANH_SLOPE * (values_in + CUBIC_TERM * values_in * values_in * values_in))
        )
    )


def norm_back(grad_in, gain_vec, unit_rows, scaler):
    scaled = grad_in * gain_vec
    return scaler * (
        scaled
        - jnp.mean(scaled, axis=-1, keepdims=True)
        - unit_rows * jnp.mean(scaled * unit_rows, axis=-1, keepdims=True)
    )


def plain_device(
    block_input,
    teacher,
    segment_ids,
    valid_mask,
    ln1_gain,
    ln1_bias,
    qkv_weight,
    qv_bias,
    out_weight,
    out_bias,
    ln2_gain,
    ln2_bias,
    fc_weight,
    fc_bias,
    proj_weight,
    proj_bias,
):
    dp, ts = lax.axis_size("dp"), lax.axis_size("tensor")
    me, mt = lax.axis_index("dp"), lax.axis_index("tensor")
    tokens, width = block_input.shape[1:]
    total_tokens = tokens * ts * dp
    halo = -(-(DOC_MOST - 1) // KB) * KB
    e = qkv_weight.shape[2]
    x = block_input[0]
    valid_rows = valid_mask[0].astype(F32)

    qkvo = jnp.concatenate([qkv_weight[0], qkv_weight[1], qkv_weight[2], out_weight.T], axis=1)
    local_count = jnp.sum(valid_mask[0])
    mine = jnp.arange(dp) == me

    def spread(v):
        return jnp.where(mine[:, None], v[..., None, :], jnp.zeros((), v.dtype))

    vectors = jnp.stack([ln1_gain, ln1_bias, out_bias, ln2_gain, ln2_bias, proj_bias])
    tail = jnp.stack([local_count // 16, local_count % 16]).astype(BF16)
    small = jnp.concatenate(
        [
            spread(vectors).reshape(6, width),
            spread(fc_bias).reshape(1, -1),
            jnp.concatenate(
                [spread(qv_bias).reshape(-1), tail, jnp.zeros((width - 2 * e - 2,), BF16)]
            )[None],
        ]
    )
    seg_rows = jnp.broadcast_to(segment_ids, (8, tokens))
    small_all, w_qkvo, w_fc, w_proj, x_halo, seg_halo = gather(
        [small, qkvo, fc_weight, proj_weight.T], x, seg_rows, dp, ts, halo
    )
    small_all = jnp.sum(small_all.astype(F32), axis=1)
    gain_one, bias_one, b_out, gain_two, bias_two, b_proj = [small_all[0, i] for i in range(6)]
    b_fc = small_all[:, 6].reshape(-1)
    b_q = small_all[:, 7, :e].reshape(-1)
    b_v = small_all[:, 7, e : 2 * e].reshape(-1)
    valid_count = jnp.sum(small_all[:, 7, 2 * e] * 16 + small_all[:, 7, 2 * e + 1])
    w_qkvo = w_qkvo.reshape(ts, width, 4, e)
    wq, wk, wv, wo = [w_qkvo[:, :, i].transpose(1, 0, 2).reshape(width, width) for i in range(4)]
    wf = w_fc.reshape(ts, width, -1)
    wp = w_proj.reshape(ts, width, -1)

    seg = segment_ids[0]
    pieces = []
    for i, (back, count) in enumerate(halo_parts(tokens, ts)):
        pieces.insert(0, seg_halo[i, 0, tokens - count :])
    filled = sum(p.shape[0] for p in pieces)
    seg_window = jnp.concatenate([jnp.full((halo - filled,), -1, jnp.int32)] + pieces)
    position = jnp.sum((seg_window[:, None] < seg[None, :]).astype(jnp.int32), axis=0)
    own = jnp.sum((seg[:, None] < seg[None, :]).astype(jnp.int32), axis=0)
    doc = (position + own)[None]
    first = doc[0, ::QB] // KB

    inputs = x.astype(F32)
    window = jnp.concatenate([x_halo, x]).astype(F32)
    unit_window, scale_window = normalize(window)
    normed_window = (unit_window * gain_one + bias_one).astype(BF16)
    unit_one, scale_one = unit_window[halo:], scale_window[halo:]
    normed_one = normed_window[halo:]
    q = ((mm(normed_one, wq) + b_q).astype(BF16) * 0.125).astype(BF16)
    k = mm(normed_window, wk).astype(BF16)
    v = (mm(normed_window, wv) + b_v).astype(BF16)
    mixed_t, lse = attend(first, doc, q, k, v.T, halo)
    mixed = mixed_t.T.astype(BF16)
    hidden = inputs + mm(mixed, wo, NT) + b_out
    unit_two, scale_two = normalize(hidden)
    normed_two = (unit_two * gain_two + bias_two).astype(BF16)
    pre_act = jnp.einsum("sd,tdf->stf", normed_two, wf, preferred_element_type=F32) + b_fc.reshape(ts, -1)
    activated = gelu_tanh(pre_act).astype(BF16)
    output = hidden + jnp.einsum("stf,tdf->sd", activated, wp, preferred_element_type=F32) + b_proj
    residual_error = output - teacher[0].astype(F32)
    squares = jnp.sum(valid_rows[:, None] * residual_error * residual_error)
    grad_output = valid_rows[:, None] * residual_error * (total_tokens / valid_count)
    low_output = grad_output.astype(BF16)
    grad_act = jnp.einsum("sd,tdf->stf", low_output, wp, preferred_element_type=F32)
    grad_proj_w = jnp.einsum("sd,stf->tdf", low_output, activated, preferred_element_type=F32)
    _, gelu_back = jax.vjp(gelu_tanh, pre_act)
    grad_pre = gelu_back(grad_act)[0].astype(BF16)
    grad_fc_w = jnp.einsum("sd,stf->tdf", normed_two, grad_pre, preferred_element_type=F32)
    grad_fc_b = jnp.sum(grad_pre, axis=0, dtype=F32)
    grad_normed_two = jnp.einsum("stf,tdf->sd", grad_pre, wf, preferred_element_type=F32)
    grad_gain_two = jnp.sum(grad_normed_two * unit_two, axis=0)
    grad_bias_two = jnp.sum(grad_normed_two, axis=0)
    grad_hidden = grad_output + norm_back(grad_normed_two, gain_two, unit_two, scale_two)
    low_hidden = grad_hidden.astype(BF16)
    grad_mixed = mm(low_hidden, wo).astype(BF16)
    grad_out_w = jnp.einsum("sd,se->de", low_hidden, mixed, preferred_element_type=F32)
    heads = width // HD
    delta = jnp.sum((grad_mixed.T.astype(F32) * mixed_t).reshape(heads // 2, 2, HD, tokens), axis=2)
    dq_t, dk, dv = attend_back(first, doc, q, k, k.T, v, grad_mixed, lse, delta, halo)
    dq, dk, dv = dq_t.T.astype(BF16), dk.astype(BF16), dv.astype(BF16)
    sd_se = lambda a, b: jnp.einsum("sd,se->de", a, b, preferred_element_type=F32)
    g_q, g_k, g_v = sd_se(normed_one, dq), sd_se(normed_window, dk), sd_se(normed_window, dv)
    grad_window = mm(dk, wk, NT) + mm(dv, wv, NT)
    grad_normed_one = grad_window[halo:] + mm(dq, wq, NT)
    end = halo
    for back, count in halo_parts(tokens, ts):
        end -= count
        part = lax.ppermute(
            grad_window[end : end + count].astype(BF16), "tensor", [(t, t - back) for t in range(back, ts)]
        )
        grad_normed_one = grad_normed_one.at[tokens - count :].add(part.astype(F32))
    grad_input = grad_hidden + norm_back(grad_normed_one, gain_one, unit_one, scale_one)

    def by_t(g):
        return g.reshape(width, ts, e)

    g_qkvo = jnp.stack([by_t(g_q), by_t(g_k), by_t(g_v), by_t(grad_out_w)], axis=2)
    g_qkvo = g_qkvo.transpose(1, 0, 2, 3).reshape(ts, width, 4 * e)
    grads = jnp.stack([grad_proj_w, grad_fc_w, g_qkvo]).astype(BF16)
    grads = grads.reshape(3, ts, dp, width // dp, -1)
    r_proj, r_fc, r_qkvo = reduce(grads, dp, ts)
    smalls = [
        jnp.sum(grad_normed_one * unit_one, axis=0),
        jnp.sum(grad_normed_one, axis=0),
        jnp.sum(grad_hidden, axis=0),
        grad_gain_two,
        grad_bias_two,
        jnp.sum(grad_output, axis=0),
        grad_fc_b.reshape(-1),
        jnp.sum(dq, axis=0, dtype=F32),
        jnp.sum(dv, axis=0, dtype=F32),
        squares[None],
    ]
    summed = lax.psum(jnp.concatenate(smalls), ("dp", "tensor"))
    rows = width // dp
    own_rows = lambda i: lax.dynamic_slice_in_dim(summed, i * width + me * rows, rows)
    fc_b = summed[6 * width : 6 * width + fc_bias.size * dp * ts].reshape(ts, -1, dp, fc_bias.shape[1])
    qv0 = 6 * width + fc_bias.size * dp * ts
    qv_b = summed[qv0 : qv0 + 2 * width].reshape(2, ts, -1, dp, qv_bias.shape[2])
    loss = summed[-1] / (width * valid_count)
    pick = lambda a, i, ax: lax.dynamic_index_in_dim(a, i, ax, keepdims=False)
    return (
        output.astype(BF16)[None],
        loss,
        grad_input[None],
        own_rows(0),
        own_rows(1),
        jnp.stack([r_qkvo[:, i * e : (i + 1) * e] for i in range(3)]),
        pick(pick(qv_b, mt, 1), me, 2),
        r_qkvo[:, 3 * e :].T,
        own_rows(2),
        own_rows(3),
        own_rows(4),
        r_fc,
        pick(pick(fc_b, mt, 0), me, 1),
        r_proj.T,
        own_rows(5),
    )


def on_device(
    block_input,
    teacher,
    segment_ids,
    valid_mask,
    ln1_gain,
    ln1_bias,
    qkv_weight,
    qv_bias,
    out_weight,
    out_bias,
    ln2_gain,
    ln2_bias,
    fc_weight,
    fc_bias,
    proj_weight,
    proj_bias,
):
    dp, ts = lax.axis_size("dp"), lax.axis_size("tensor")
    me, mt = lax.axis_index("dp"), lax.axis_index("tensor")
    tokens, width = block_input.shape[1:]
    total_tokens = tokens * ts * dp
    halo = -(-(DOC_MOST - 1) // KB) * KB
    e = qkv_weight.shape[2]
    x = block_input[0]
    valid_rows = valid_mask[0].astype(F32)

    out_t = out_weight.T
    cuts = [qkv_weight[0], qkv_weight[1], qkv_weight[2], out_t]
    qkvo = jnp.concatenate([c[:, : 2 * HD] for c in cuts] + [c[:, 2 * HD :] for c in cuts], axis=1)
    local_count = jnp.sum(valid_rows)
    mine = jnp.arange(dp) == me

    def spread(v):
        return jnp.where(mine[:, None], v[..., None, :], jnp.zeros((), v.dtype)).astype(F32)

    vectors = jnp.stack([ln1_gain, ln1_bias, out_bias, ln2_gain, ln2_bias, proj_bias])
    qv = spread(qv_bias).reshape(2, e)
    small = jnp.concatenate(
        [
            spread(vectors).reshape(6, width),
            spread(fc_bias).reshape(1, -1),
            jnp.concatenate(
                [qv[0, : 2 * HD], qv[1, : 2 * HD], qv[0, 2 * HD :], qv[1, 2 * HD :], local_count[None]]
                + [jnp.zeros((width - 2 * e - 1,), F32)]
            )[None],
        ]
    )
    seg_rows = jnp.broadcast_to(segment_ids, (8, tokens))
    qkvo_all, w_fc, w_proj, vec, doc, normed_window, q, k, v, mixed_t, lse, mixed, hidden = front(
        x, seg_rows, small, qkvo, fc_weight, proj_weight.T, dp, ts, halo
    )
    gain_one, bias_one, b_out, gain_two, bias_two, b_proj = [vec[0, i] for i in range(6)]
    b_fc = vec[:, 6].reshape(-1)
    valid_count = jnp.sum(vec[:, 7, 2 * e])
    w_qkvo = qkvo_all.reshape(ts, width, 4 * e)

    def pair_weights(i):
        low = w_qkvo[:, :, i * 128 : (i + 1) * 128]
        last = w_qkvo[:, :, 512 + i * HD : 512 + (i + 1) * HD]
        last = last.reshape(ts // 2, 2, width, HD).transpose(0, 2, 1, 3).reshape(ts // 2, width, 128)
        return jnp.concatenate([low, last]).transpose(1, 0, 2).reshape(width, width)

    wq, wk, wv, wo = [pair_weights(i) for i in range(4)]
    wf = w_fc.reshape(ts, width, -1)
    wp = w_proj.reshape(ts, width, -1)
    doc = doc[0:1]
    first = doc[0, ::QB] // KB

    inputs = x.astype(F32)
    unit_one, scale_one = normalize(inputs)
    normed_one = normed_window[halo:]
    unit_two, scale_two = normalize(hidden)
    normed_two = (unit_two * gain_two + bias_two).astype(BF16)
    pre_act = jnp.einsum("sd,tdf->stf", normed_two, wf, preferred_element_type=F32) + b_fc.reshape(ts, -1)
    activated = gelu_tanh(pre_act).astype(BF16)
    output = hidden + jnp.einsum("stf,tdf->sd", activated, wp, preferred_element_type=F32) + b_proj
    residual_error = output - teacher[0].astype(F32)
    squares = jnp.sum(valid_rows[:, None] * residual_error * residual_error)
    grad_output = valid_rows[:, None] * residual_error * (total_tokens / valid_count)
    low_output = grad_output.astype(BF16)
    grad_act = jnp.einsum("sd,tdf->stf", low_output, wp, preferred_element_type=F32)
    grad_proj_w = jnp.einsum("sd,stf->tdf", low_output, activated, preferred_element_type=F32)
    _, gelu_back = jax.vjp(gelu_tanh, pre_act)
    grad_pre = gelu_back(grad_act)[0].astype(BF16)
    grad_fc_w = jnp.einsum("sd,stf->tdf", normed_two, grad_pre, preferred_element_type=F32)
    grad_fc_b = jnp.sum(grad_pre, axis=0, dtype=F32)
    grad_normed_two = jnp.einsum("stf,tdf->sd", grad_pre, wf, preferred_element_type=F32)
    grad_gain_two = jnp.sum(grad_normed_two * unit_two, axis=0)
    grad_bias_two = jnp.sum(grad_normed_two, axis=0)
    grad_hidden = grad_output + norm_back(grad_normed_two, gain_two, unit_two, scale_two)
    low_hidden = grad_hidden.astype(BF16)
    grad_mixed = mm(low_hidden, wo).astype(BF16)
    grad_out_w = jnp.einsum("sd,se->de", low_hidden, mixed, preferred_element_type=F32)
    heads = width // HD
    delta = jnp.sum((grad_mixed.T.astype(F32) * mixed_t).reshape(heads // 2, 2, HD, tokens), axis=2)
    dq_t, dk, dv = attend_back(first, doc, q, k, k.T, v, grad_mixed, lse, delta, halo)
    dq, dk, dv = dq_t.T.astype(BF16), dk.astype(BF16), dv.astype(BF16)
    sd_se = lambda a, b: jnp.einsum("sd,se->de", a, b, preferred_element_type=F32)
    g_q, g_k, g_v = sd_se(normed_one, dq), sd_se(normed_window, dk), sd_se(normed_window, dv)
    grad_window = mm(dk, wk, NT) + mm(dv, wv, NT)
    grad_normed_one = grad_window[halo:] + mm(dq, wq, NT)
    end = halo
    for back, count in halo_parts(tokens, ts):
        end -= count
        part = lax.ppermute(
            grad_window[end : end + count].astype(BF16), "tensor", [(t, t - back) for t in range(back, ts)]
        )
        grad_normed_one = grad_normed_one.at[tokens - count :].add(part.astype(F32))
    grad_input = grad_hidden + norm_back(grad_normed_one, gain_one, unit_one, scale_one)

    def by_t(gs):
        gs = jnp.stack([g.reshape(width, -1, 128) for g in gs])
        low = gs[:, :, :ts].transpose(2, 1, 0, 3).reshape(ts, width, 512)
        last = gs[:, :, ts:].reshape(4, width, ts, HD).transpose(2, 1, 0, 3).reshape(ts, width, 256)
        return jnp.concatenate([low, last], axis=2)

    g_qkvo = by_t([g_q, g_k, g_v, grad_out_w])
    grads = jnp.stack([grad_proj_w, grad_fc_w, g_qkvo]).astype(BF16)
    grads = grads.reshape(3, ts, dp, width // dp, -1)
    r_proj, r_fc, r_qkvo = reduce(grads, dp, ts)
    def by_head(v):
        return jnp.concatenate([v[: ts * 128].reshape(ts, 128), v[ts * 128 :].reshape(ts, HD)], axis=1).reshape(-1)

    def columns(i):
        return jnp.concatenate([r_qkvo[:, i * 128 : (i + 1) * 128], r_qkvo[:, 512 + i * HD : 512 + (i + 1) * HD]], axis=1)

    smalls = [
        jnp.sum(grad_normed_one * unit_one, axis=0),
        jnp.sum(grad_normed_one, axis=0),
        jnp.sum(grad_hidden, axis=0),
        grad_gain_two,
        grad_bias_two,
        jnp.sum(grad_output, axis=0),
        grad_fc_b.reshape(-1),
        by_head(jnp.sum(dq, axis=0, dtype=F32)),
        by_head(jnp.sum(dv, axis=0, dtype=F32)),
        squares[None],
    ]
    summed = lax.psum(jnp.concatenate(smalls), ("dp", "tensor"))
    rows = width // dp
    own_rows = lambda i: lax.dynamic_slice_in_dim(summed, i * width + me * rows, rows)
    fc_b = summed[6 * width : 6 * width + fc_bias.size * dp * ts].reshape(ts, -1, dp, fc_bias.shape[1])
    qv0 = 6 * width + fc_bias.size * dp * ts
    qv_b = summed[qv0 : qv0 + 2 * width].reshape(2, ts, -1, dp, qv_bias.shape[2])
    loss = summed[-1] / (width * valid_count)
    pick = lambda a, i, ax: lax.dynamic_index_in_dim(a, i, ax, keepdims=False)
    return (
        output.astype(BF16)[None],
        loss,
        grad_input[None],
        own_rows(0),
        own_rows(1),
        jnp.stack([columns(i) for i in range(3)]),
        pick(pick(qv_b, mt, 1), me, 2),
        columns(3).T,
        own_rows(2),
        own_rows(3),
        own_rows(4),
        r_fc,
        pick(pick(fc_b, mt, 0), me, 1),
        r_proj.T,
        own_rows(5),
    )


def solution(mesh):
    placed = (
        P("dp", "tensor", None),
        P("dp", "tensor", None),
        P("dp", "tensor"),
        P("dp", "tensor"),
        P("dp"),
        P("dp"),
        P(None, "dp", "tensor"),
        P(None, "tensor", "dp"),
        P("tensor", "dp"),
        P("dp"),
        P("dp"),
        P("dp"),
        P("dp", "tensor"),
        P("tensor", "dp"),
        P("tensor", "dp"),
        P("dp"),
    )
    def fits(qkv_weight, block_input):
        rows = block_input.shape[2] // mesh.shape["dp"]
        wide = qkv_weight.shape[2] // mesh.shape["tensor"]
        return rows % 16 == 0 and wide == 3 * HD and mesh.shape["tensor"] % 2 == 0

    def step(*args):
        return placed_step(on_device if fits(args[6], args[0]) else plain_device)(*args)

    placed_step = lambda body: jax.shard_map(
        body,
        mesh=mesh,
        in_specs=placed,
        out_specs=(
            P("dp", "tensor", None),
            P(),
            P("dp", "tensor", None),
            P("dp"),
            P("dp"),
            P(None, "dp", "tensor"),
            P(None, "tensor", "dp"),
            P("tensor", "dp"),
            P("dp"),
            P("dp"),
            P("dp"),
            P("dp", "tensor"),
            P("tensor", "dp"),
            P("tensor", "dp"),
            P("dp"),
        ),
        check_vma=False,
    )
    return step
```

profile of v0, /device:TPU:0, one launch (start us, length us, event | category | flops | bytes accessed | tf_op | source)
XLA Modules:
  0.0 516.6 jit_solution(9921016620012526898)
XLA Ops:
  0.6 1.3 convert_reduce_fusion.4
  9.6 1.3 broadcast_in_dim.114.seg_ref
  10.9 144.3 %front.1 = (bf16[4,8,96,768]{3,2,1,0:T(8,128)(2,1)}, bf16[4,8,96,768]{3,2,1,0:T(8,128)(2,1)}, bf16[4,8,96,768]{3,2,1,0:T(8,128)(2,1)}, f32[4,8,768]{2,1,0:T(8,12...) custom-call(bf16[512,768]{1,0:T(8,128)(2,1)} %bitcast.180, ...), custom_call_target="tpu_custom_call" | custom-call | tf_op jit(solution)/shard_map/front/pallas_call | solution.py:474
  155.2 1.3 slice_reduce_fusion.4
  157.4 1.5 slice_reduce_fusion
  158.9 4.1 fusion.48
  163.0 1.9 fusion.47
  167.9 3.0 copy.53
  171.0 4.2 copy.50
  175.2 2.1 copy.58
  177.3 1.4 copy.56
  179.7 2.4 copy.78
  182.1 1.2 copy.77
  184.4 5.2 %fusion.44 = f32[512,4,768]{2,0,1:T(8,128)S(1)} fusion(bf16[4,768,768]{2,1,0:T(8,128)(2,1)} %bitcast.223, f32[512,768]{1,0:T(8,128)S(1)} %copy-done.4, f32[768]{0:T(1024)} %get-tuple-element.121, f32[768]{0:T(1024)S(1)} %get-tuple-element.122, f32[512]{0:T(512)} %add_rsqrt_fusion.1, f32[512]{0:T(512)S(1)} %broadcast_multiply_fusion.5), kind=kOutput, calls=%fused_computation.139 | convolution fusion | flops 2417885184 | bytes 12593152 | tf_op jit(solution)/shard_map/sd,tdf->stf/dot_general | solution.py:1212
  189.6 8.6 %fusion.21 = f32[512,768]{1,0:T(8,128)S(1)} fusion(f32[512,768]{1,0:T(8,128)S(1)} %copy-done.4, bf16[4,768,768]{2,1,0:T(8,128)(2,1)} %bitcast.227, f32[768]{0:T(1024)S(1)} %copy-done.29, f32[512,4,768]{2,0,1:T(8,128)S(1)} %fusion.44, f32[4,768]{1,0:T(4,128)S(1)} %bitcast.211), kind=kOutput, calls=%fused_computation.46 | convolution fusion | flops 2432434176 | bytes 14171136 | tf_op jit(solution)/shard_map/stf,tdf->sd/dot_general | solution.py:1214
  198.6 8.1 %convert_reduce_fusion = (f32[4,768]{1,0:T(4,128)}, bf16[512,4,768]{2,0,1:T(8,128)(2,1)S(1)}) fusion(bf16[512,768,1]{1,0,2:T(8,128)(2,1)S(1)} %fusion.30, bf16[4,768,768]{2,1,0:T(8,128)(2,1)S(1)} %bitcast.230, f32[512,4,768]{2,0,1:T(8,128)S(1)} %fusion.44, f32[4,768]{1,0:T(4,128)S(1)} %bitcast.212), kind=kOutput, calls=%fused_computation.12 | convolution fusion | flops 2458383360 | bytes 14966784 | tf_op jit(solution)/shard_map/sd,tdf->stf/dot_general | solution.py:1219
  206.7 3.4 fusion.20
  210.2 1.3 copy-done.5
  211.5 2.8 fusion.18
  214.3 2.3 bitcast_multiply_fusion
  216.6 3.0 copy.54
  219.6 2.2 reduce_sum.195.delta_ref
  221.9 1.4 pad_maximum_fusion.2
  224.4 21.9 %attend_back.1 = (f32[768,512]{1,0:T(8,128)}, f32[1408,768]{1,0:T(8,128)}, f32[1408,768]{1,0:T(8,128)}) custom-call(s32[2]{0:T(128)} %and_select_fusion.first_ref, s32[1,512]{1,0:T(1,128)} %copy-done.25, bf16[512,768]{1,0:T(8,128)(2,1)} %get-tuple-element.68.q_ref, bf16[1408,768]{1,0:T(8,128)(2,1)} %get-tuple-element.69.k_ref, bf16[768,1408]{1,0:T(8,128)(2,1)} %bitcast.187, ...), custom_call_target="tpu_custom_call" | custom-call | tf_op jit(solution)/shard_map/attend_back/pallas_call | solution.py:923
  246.4 4.6 fusion.27
  251.0 4.0 fusion.52
  255.1 1.4 collective-permute-start.1
  257.5 1.3 collective-permute-start
  259.6 13.7 %convolution_convert_fusion.1 = bf16[4,768,768]{1,2,0:T(8,128)(2,1)} fusion(bf16[512,768,1]{1,0,2:T(8,128)(2,1)S(1)} %copy-done.16, f32[512,4,768]{2,0,1:T(8,128)S(1)} %bitcast.234, f32[4,768]{1,0:T(4,128)S(1)} %bitcast.213), kind=kOutput, calls=%fused_computation.19 | convolution fusion | flops 2434007040 | bytes 11808768 | tf_op jit(solution)/shard_map/sd,stf->tdf/dot_general | solution.py:1220
  273.3 4.6 convolution_convert_fusion
  279.5 2.1 fusion.25
  281.7 2.1 fusion.40
  286.0 1.3 maximum_convert_fusion.1
  288.0 2.0 slice_bitcast_fusion
  289.9 6.0 %copy.63 = bf16[4,768,4,128]{3,2,1,0:T(4,128)(2,1)} copy(bf16[4,768,4,128]{1,3,0,2:T(8,128)(2,1)} %slice_bitcast_fusion) | data formatting | bytes 6291456 | tf_op jit(solution)/shard_map/transpose | solution.py:1251
  295.9 5.7 %concatenate.68 = bf16[1,4,8,96,512]{4,3,2,1,0:T(8,128)(2,1)} reshape(bf16[4,768,4,128]{3,2,1,0:T(4,128)(2,1)} %copy.63) | data formatting | bytes 6291456 | tf_op jit(solution)/shard_map/concatenate | solution.py:1253
  301.6 5.5 %copy.73 = bf16[4,768,4,64]{3,2,1,0:T(4,128)(2,1)} copy(bf16[4,768,4,64]{1,3,0,2:T(8,128)(2,1)} %bitcast.191) | data formatting | bytes 3145728 | tf_op jit(solution)/shard_map/concatenate | solution.py:1253
  307.1 5.7 %reshape.332 = bf16[1,4,8,96,256]{4,3,2,1,0:T(8,128)(2,1)} reshape(bf16[4,768,4,64]{3,2,1,0:T(4,128)(2,1)} %copy.73) | data formatting | bytes 3145728 | tf_op jit(solution)/shard_map/concatenate | solution.py:1253
  312.8 10.5 %maximum_maximum_fusion.g_ref = bf16[3,4,8,96,768]{4,3,2,1,0:T(8,128)(2,1)} fusion(bf16[1,4,8,96,256]{4,3,2,1,0:T(8,128)(2,1)} %reshape.332, bf16[1,4,8,96,512]{4,3,2,1,0:T(8,128)(2,1)} %concatenate.68, bf16[1,4,8,96,768]{4,3,2,1,0:T(8,128)(2,1)} %bitcast.194, bf16[1,4,8,96,768]{4,3,2,1,0:T(8,128)(2,1)} %bitcast.193), kind=kLoop, calls=%fused_computation | loop fusion | flops 56623104 | bytes 28311552 | tf_op jit(solution)/shard_map/stack | solution.py:1256
  323.3 125.3 %reduce.17 = f32[3,96,768]{2,1,0:T(8,128)} custom-call(bf16[3,4,8,96,768]{4,3,2,1,0:T(8,128)(2,1)} %maximum_maximum_fusion.g_ref), custom_call_target="tpu_custom_call" | custom-call | tf_op jit(solution)/shard_map/reduce/pallas_call | solution.py:778
  448.6 2.0 slice_bitcast_fusion.1
  451.4 2.3 copy.79
  453.9 1.3 reshape.319
  455.3 2.3 pad_maximum_fusion.3
  461.2 3.3 fusion.19
  464.5 1.2 fusion.29
  468.5 40.3 %psum.7 = f32[9217]{0:T(1024)S(1)} all-reduce(f32[9217]{0:T(1024)S(1)} %constant_dynamic-update-slice_fusion), channel_id=1, replica_groups=mesh['dp'=8,'tensor'=4] {'dp','tensor'}, use_global_device_ids=true, to_apply=%region_19.20 | all-reduce | flops 9217 | bytes 73736 | tf_op jit(solution)/shard_map/psum | solution.py:1277
  511.5 3.1 fusion.16
  (199 shorter events, 29.7 us)
Async XLA Ops:
  158.9 4.1 copy-start.7
  163.0 3.2 copy-start.4
  165.7 0.6 copy-start.25
  179.7 2.4 copy-start.10
  184.3 5.3 %copy-start.21 = (f32[4,1,768]{2,0,1:T(4,128)S(1)}, f32[4,1,768]{2,0,1:T(4,128)}, u32[]{:S(2)}) copy-start(f32[4,1,768]{2,0,1:T(4,128)} %copy.82) | copy-start | bytes 36868
  184.3 5.3 %copy-start.29 = (f32[768]{0:T(1024)S(1)}, f32[768]{0:T(1024)}, u32[]{:S(2)}) copy-start(f32[768]{0:T(1024)} %get-tuple-element.120) | copy-start | bytes 9220
  184.4 14.2 %slice-start.4 = ((s8[4718592]{0:T(1024)(128)(4,1)}), s8[4194304]{0:T(1024)(128)(4,1)S(1)}, s32[]{:S(2)}) async-start(s8[4718592]{0:T(1024)(128)(4,1)} %bitcast.228), calls=%async_computation.4 | async-start | bytes 8388608
  189.6 8.9 %copy-start.32 = (f32[512,4,768]{2,0,1:T(8,128)}, f32[512,4,768]{2,0,1:T(8,128)S(1)}, u32[]{:S(2)}) copy-start(f32[512,4,768]{2,0,1:T(8,128)S(1)} %fusion.44) | copy-start | bytes 18874372
  189.6 8.6 %copy-start.11 = (bf16[1,512,768]{2,1,0:T(8,128)(2,1)S(1)}, bf16[1,512,768]{2,1,0:T(8,128)(2,1)}, u32[]{:S(2)}) copy-start(bf16[1,512,768]{2,1,0:T(8,128)(2,1)} %param.23) | copy-start | bytes 2359300
  189.6 8.9 %slice-start.5 = ((s8[4718592]{0:T(1024)(128)(4,1)}), s8[524288]{0:T(1024)(128)(4,1)S(1)}, s32[]{:S(2)}) async-start(s8[4718592]{0:T(1024)(128)(4,1)} %bitcast.228), calls=%async_computation.5 | async-start | bytes 1048576
  198.2 8.4 %slice-start.2 = ((s8[4718592]{0:T(1024)(128)(4,1)}), s8[4194304]{0:T(1024)(128)(4,1)S(1)}, s32[]{:S(2)}) async-start(s8[4718592]{0:T(1024)(128)(4,1)} %bitcast.224), calls=%async_computation.2 | async-start | bytes 8388608
  198.5 8.1 %copy-start.15 = (bf16[512,768,1]{1,0,2:T(8,128)(2,1)}, bf16[512,768,1]{1,0,2:T(8,128)(2,1)S(1)}, u32[]{:S(2)}) copy-start(bf16[512,768,1]{1,0,2:T(8,128)(2,1)S(1)} %fusion.30) | copy-start | bytes 2359300
  198.5 8.1 %copy-start.23 = (f32[512]{0:T(512)S(1)}, f32[512]{0:T(512)}, u32[]{:S(2)}) copy-start(f32[512]{0:T(512)} %add_rsqrt_fusion.1) | copy-start | bytes 6148
  198.6 8.1 %slice-start.3 = ((s8[4718592]{0:T(1024)(128)(4,1)}), s8[524288]{0:T(1024)(128)(4,1)S(1)}, s32[]{:S(2)}) async-start(s8[4718592]{0:T(1024)(128)(4,1)} %bitcast.224), calls=%async_computation.3 | async-start | bytes 1048576
  206.6 3.5 copy-start.33
  206.7 3.5 copy-start.13
  210.1 1.4 copy-start.5
  211.5 2.8 copy-start.8
  221.9 1.5 copy-start.12
  246.4 4.6 slice-start
  246.4 4.6 slice-start.1
  246.4 13.1 %slice-start.8 = ((s8[6291456]{0:T(1024)(128)(4,1)}), s8[4194304]{0:T(1024)(128)(4,1)S(1)}, s32[]{:S(2)}) async-start(s8[6291456]{0:T(1024)(128)(4,1)} %bitcast.233), calls=%async_computation.8 | async-start | bytes 8388608
  251.0 8.5 %slice-start.9 = ((s8[6291456]{0:T(1024)(128)(4,1)}), s8[2097152]{0:T(1024)(128)(4,1)S(1)}, s32[]{:S(2)}) async-start(s8[6291456]{0:T(1024)(128)(4,1)} %bitcast.233), calls=%async_computation.9 | async-start | bytes 4194304
  255.0 3.7 copy-start.1
  255.0 4.5 copy-start.16
  255.0 4.5 copy-start.22
  255.1 209.4 %collective-permute-start.1 = (bf16[288,768]{1,0:T(8,128)(2,1)S(1)}, bf16[288,768]{1,0:T(8,128)(2,1)}, u32[]{:S(2)}, u32[]{:S(2)}) collective-permute-start(bf16[288,768]{1,0:T(8,128)(2,1)S(1)} %slice.307), channel_id=1, source_target_pairs={{2,0},{3,1},{6,4},{7,5},{10,8},{11,9},{14,12},{15,13},{18,16},{19,... | collective-permute-start | bytes 1327112 | tf_op jit(solution)/shard_map/ppermute | solution.py:1243
  257.5 203.7 %collective-permute-start = (bf16[512,768]{1,0:T(8,128)(2,1)}, bf16[512,768]{1,0:T(8,128)(2,1)}, u32[]{:S(2)}, u32[]{:S(2)}) collective-permute-start(bf16[512,768]{1,0:T(8,128)(2,1)} %slice.305), channel_id=1, source_target_pairs={{1,0},{2,1},{3,2},{5,4},{6,5},{7,6},{9,8},{10,9},{11,10},{13,12},{... | collective-permute-start | bytes 2359304 | tf_op jit(solution)/shard_map/ppermute | solution.py:1243
  259.5 13.7 %copy-start.6 = (f32[512,768]{1,0:T(8,128)S(1)}, f32[512,768]{1,0:T(8,128)}, u32[]{:S(2)}) copy-start(f32[512,768]{1,0:T(8,128)} %get-tuple-element.63) | copy-start | bytes 4718596
  259.5 13.7 %copy-start.24 = (f32[512]{0:T(512)S(1)}, f32[512]{0:T(512)}, u32[]{:S(2)}) copy-start(f32[512]{0:T(512)} %add_rsqrt_fusion.1) | copy-start | bytes 6148
  259.5 13.7 %copy-start.28 = (f32[768]{0:T(1024)S(1)}, f32[768]{0:T(1024)}, u32[]{:S(2)}) copy-start(f32[768]{0:T(1024)} %get-tuple-element.121) | copy-start | bytes 9220
  259.6 13.7 %copy-start.34 = (bf16[512,4,768]{2,0,1:T(8,128)(2,1)S(1)}, bf16[512,4,768]{2,0,1:T(8,128)(2,1)}, u32[]{:S(2)}) copy-start(bf16[512,4,768]{2,0,1:T(8,128)(2,1)} %copy-done.33) | copy-start | bytes 9437188
  259.6 19.2 %slice-start.6 = ((s8[4325376]{0:T(1024)(128)(4,1)}), s8[4194304]{0:T(1024)(128)(4,1)S(1)}, s32[]{:S(2)}) async-start(s8[4325376]{0:T(1024)(128)(4,1)} %bitcast.231), calls=%async_computation.6 | async-start | bytes 8388608
  273.3 5.5 %slice-start.7 = ((s8[4325376]{0:T(1024)(128)(4,1)}), s8[131072]{0:T(1024)(128)(4,1)S(1)}, s32[]{:S(2)}) async-start(s8[4325376]{0:T(1024)(128)(4,1)} %bitcast.231), calls=%async_computation.7 | async-start | bytes 262144
  277.9 1.6 copy-start.17
  281.7 2.2 copy-start.3
  284.0 1.1 copy-start.14
  448.6 2.8 copy-start.26
  450.6 3.0 copy-start.9
  455.3 2.3 copy-start.18
  455.3 3.1 copy-start.27
  455.3 3.2 copy-start.2
  465.7 1.1 copy-start
  465.7 2.0 copy-start.20
  465.7 2.1 copy-start.31
  465.7 2.1 copy-start.30
  465.7 2.1 copy-start.19
where the time goes:
time: 520 us; the launch traced here: 517 us
  Pallas kernels  292 us (56%)
  local copies, waits for them, and re-layouts  77.7 us (15%)
  matrix products  63.6 us (12%)
  blocking collectives  40.3 us (8%)
  other arithmetic  35.8 us (7%)
    pallas_call x1, Pallas kernels, front(): pl.pallas_call(functools.partial(front_kernel, dp, ts), out_shape=[big, b...  144 us
    pallas_call x1, Pallas kernels, reduce(): pl.pallas_call(functools.partial(reduce_kernel, dp, ts), out_shape=jax.Sh...  125 us
    psum x1, blocking collectives, on_device(): summed = lax.psum(jnp.concatenate(smalls), ('dp', 'tensor'))  40.3 us
    pallas_call x1, Pallas kernels, attend_back(): pl.pallas_call(functools.partial(attend_back_kernel, halo), out_shape=[ja...  21.9 us
    concatenate x3, local copies, waits for them, and re-layouts, by_t(): return jnp.concatenate([low, last], axis=2)  16.9 us
    dot_general x4, matrix products, mm(): return lax.dot_general(a, b, dims, preferred_element_type=F32)  14.1 us
    dot_general x1, matrix products, on_device(): jnp.einsum('sd,stf->tdf', low_output, activated, preferred_element_type=F32)  13.7 us
    unnamed x108, local copies, waits for them, and re-layouts  13.6 us
  transfers between devices with their start and end apart: 2, of which 0 were waited for; matrix products, arithmetic and copies ran while one was open for 15% of the time, Pallas kernels for 24%

commit v1 on v0

--- a/solution.py
+++ b/solution.py
@@ -12,7 +12,10 @@
 KB = 128
 QB = 256
 DOCS = 8
-WINDOW = -(-(DOC_MOST - 1) // KB) + QB // KB
+HALO = -(-(DOC_MOST - 1) // KB) * KB
+LEAD = (HALO - DOC_MOST + 1) // 32 * 32
+CHUNKS = ([(LEAD, KB - LEAD)] if LEAD else [(0, KB)]) + [(r, KB) for r in range(KB, HALO + QB, KB)]
+Q_SCALE = 0.125 * 1.4426950408889634
 EPSILON = 1e-05
 TANH_SLOPE = 0.7978845608028654
 CUBIC_TERM = 0.044715
@@ -154,13 +157,12 @@
 
 def meet(dp, ts):
     me, mt = lax.axis_index("dp"), lax.axis_index("tensor")
-    bits = [1 << k for k in range(dp.bit_length() - 1)]
     barrier = pltpu.get_barrier_semaphore()
     for k in range(1, ts):
         pl.semaphore_signal(barrier, inc=1, device_id={"tensor": lax.rem(mt + k, ts)}, device_id_type=MESH)
-    for b in bits:
+    for b in range(1, dp):
         pl.semaphore_signal(barrier, inc=1, device_id={"dp": me ^ b}, device_id_type=MESH)
-    pl.semaphore_wait(barrier, ts - 1 + len(bits))
+    pl.semaphore_wait(barrier, ts - 1 + dp - 1)
 
 
 def keep_lanes(block, head):
@@ -181,14 +183,21 @@
     return jnp.where(lanes < HD, low, high)
 
 
-def masked(s, i, doc_row, base):
+def causal(s, row):
+    ahead = row - HALO
+    if ahead < 0:
+        return s
     key = lax.broadcasted_iota(jnp.int32, s.shape, 0)
-    ok = key >= doc_row - (base + i * KB)
-    ahead = i - (WINDOW - QB // KB)
-    if ahead >= 0:
-        query = lax.broadcasted_iota(jnp.int32, s.shape, 1)
-        ok = ok & (key + ahead * KB <= query)
-    return jnp.where(ok, s, -1e30)
+    query = lax.broadcasted_iota(jnp.int32, s.shape, 1)
+    return jnp.where(key + ahead <= query, s, -1e30)
+
+
+def segment_lanes(seg_row, same):
+    shape = (128, seg_row.shape[1])
+    value = lax.rem(lax.broadcasted_iota(jnp.int32, shape, 0), HD)
+    hit = (seg_row == value) if same else (seg_row != value)
+    level = -1e30 if same else 1.0
+    return jnp.where(hit & (value < DOCS), level, 0.0).T.astype(BF16)
 
 
 def normalize(values_in):
@@ -201,7 +210,7 @@
     for a in range(ts // 2):
         tiles = []
         for t in (2 * a, 2 * a + 1):
-            block = h2_ref[t].reshape(-1, 256)
+            block = h2_ref[t, :, :, 0:256].reshape(-1, 256)
             tiles.append((block[:, :128], block[:, 128:]))
         (qk0, vo0), (qk1, vo1) = tiles
         merged = [
@@ -218,7 +227,7 @@
     res = []
     for t in range(ts):
         res.append(pltpu.make_async_copy(qkvo_all.at[t, :, :, pl.ds(0, 512)], w_ref.at[t], sem.at[2 * t]))
-        res.append(pltpu.make_async_copy(qkvo_all.at[t, :, :, pl.ds(512, 256)], h2_ref.at[t], sem.at[2 * t + 1]))
+        res.append(pltpu.make_async_copy(qkvo_all.at[t, :, :, pl.ds(512, 256)], h2_ref.at[t, :, :, pl.ds(0, 256)], sem.at[2 * t + 1]))
     return res
 
 
@@ -235,8 +244,10 @@
     fc_all,
     proj_all,
     vec_ref,
-    doc_ref,
-    normed_ref,
+    kseg_ref,
+    qseg_ref,
+    normed_t_ref,
+    halo_ref,
     q_ref,
     k_ref,
     v_ref,
@@ -247,8 +258,9 @@
     small_all,
     w_ref,
     h2_ref,
-    halo_ref,
     hseg_ref,
+    normed_ref,
+    ka_ref,
     vt_ref,
     s_ref,
     local_sem,
@@ -295,6 +307,12 @@
     ]
     net.start(0)
     net.start(1)
+    for c in own:
+        c.start()
+    for k in range(1, ts):
+        net.z_step(0, k)
+    for k in range(1, ts - 1):
+        net.z_step(1, k)
     for i, (back, _) in enumerate(parts):
 
         @pl.when(mt + back < ts)
@@ -302,17 +320,14 @@
             for h in halo_copies(i):
                 h.start()
 
-    for c in own:
-        c.start()
-    for c in (0, 1):
-        for k in range(1, ts):
-            net.z_step(c, k)
+    net.z_step(1, ts - 1)
+    for i in range(stages):
+        for k in range(ts):
+            net.far_step(0, k, i)
+    for k in range(ts):
+        net.far_step(1, k, 0)
     net.start(2)
     net.start(3)
-    for c in (0, 1):
-        for i in range(stages):
-            for k in range(ts):
-                net.far_step(c, k, i)
     own[0].wait()
     for k in range(ts):
         net.core_step(0, k)
@@ -321,13 +336,22 @@
 
     def norm_rows(src, i, at):
         unit, _ = normalize(src[pl.ds(i * KB, KB), :].astype(F32))
-        normed_ref[pl.ds(at + i * KB, KB), :] = (unit * vec_ref[0, 0:1, :] + vec_ref[0, 1:2, :]).astype(BF16)
+        rows = pl.ds(pl.multiple_of(at + i * KB, KB), KB)
+        normed = (unit * vec_ref[0, 0:1, :] + vec_ref[0, 1:2, :]).astype(BF16)
+        normed_ref[rows, :] = normed
+        for n in range(width // KB):
+            normed_t_ref[n * KB : (n + 1) * KB, rows] = normed[:, n * KB : (n + 1) * KB].T
 
     def own_rows(i, carry):
         norm_rows(x_ref, i, halo)
         return carry
 
     lax.fori_loop(0, tokens // KB, own_rows, 0)
+    qseg_ref[...] = segment_lanes(seg_ref[0:1, :], True)
+    kseg_ref[pl.ds(halo, tokens), :] = segment_lanes(seg_ref[0:1, :], False)
+    for i in range(1, stages):
+        for k in range(ts):
+            net.far_step(1, k, i)
     own[1].wait()
     for k in range(ts):
         net.core_step(1, k)
@@ -337,6 +361,28 @@
     for load in loads:
         load.wait()
     merge_pairs(w_ref, h2_ref, ts)
+
+    def biases(p):
+        t = jnp.minimum(p, ts - 1)
+        a = jnp.maximum(p - ts, 0)
+        low, high = vec_ref[2 * a, 7:8, 256:384], vec_ref[2 * a + 1, 7:8, 256:384]
+        bias_q = jnp.where(p < ts, vec_ref[t, 7:8, 0:128], lanes_of(low, swap_halves(high)))
+        bias_v = jnp.where(p < ts, vec_ref[t, 7:8, 128:256], lanes_of(swap_halves(low), high))
+        return bias_q, bias_v
+
+    own_span = pl.ds(halo, tokens)
+
+    def project_own(p, carry):
+        cols = pl.ds(pl.multiple_of(p * 128, 128), 128)
+        bias_q, bias_v = biases(p)
+        y = mm(normed_ref[own_span, :], w_ref[p, :, :, 0:384].reshape(width, 384))
+        q_ref[:, cols] = ((y[:, :128] + bias_q) * Q_SCALE).astype(BF16)
+        k_ref[own_span, cols] = y[:, 128:256].astype(BF16)
+        v_ref[own_span, cols] = (y[:, 256:] + bias_v).astype(BF16)
+        return carry
+
+    lax.fori_loop(0, width // 128, project_own, 0)
+    net.far_step(2, 0, 0)
     for i, (back, _) in enumerate(parts):
 
         @pl.when(mt >= back)
@@ -349,51 +395,41 @@
         return carry
 
     lax.fori_loop(0, halo // KB, halo_rows, 0)
-
-    seg_row = seg_ref[0:1, :]
-    lanes = lax.broadcasted_iota(jnp.int32, (1, tokens), 1)
-    doc = jnp.full((1, tokens), halo, jnp.int32)
-    for value in range(DOCS):
-        in_halo = jnp.zeros((1, 1), jnp.int32)
-        for i, (_, count) in enumerate(parts):
-            hit = (hseg_ref[i, 0:1, :] == value) & (lanes >= tokens - count)
-            in_halo = in_halo + jnp.sum(hit.astype(jnp.int32), axis=1, keepdims=True)
-        here = jnp.sum((seg_row == value).astype(jnp.int32), axis=1, keepdims=True)
-        doc = doc - in_halo + jnp.where(seg_row > value, in_halo + here, 0)
-    doc_ref[...] = jnp.broadcast_to(doc, doc_ref.shape)
-
-    window = halo + tokens
-    half_rows = window // 2
-
-    def steps_at(p):
-        work = {1: [(2, "z")], 2: [(2, 0)], 3: [(2, 1), (3, "z")], 4: [(3, 0)], 5: [(3, 1)]}
-        for at, items in work.items():
-
-            @pl.when(p == at)
+    lanes = lax.rem(lax.broadcasted_iota(jnp.int32, (halo, 128), 1), HD)
+    kseg_ref[pl.ds(0, halo), :] = jnp.where(lanes < DOCS, 1.0, 0.0).astype(BF16)
+    end = halo
+    for i, (_, count) in enumerate(parts):
+        kseg_ref[pl.ds(end - count, count), :] = segment_lanes(hseg_ref[i, 0:1, :], False)[tokens - count :]
+        end -= count
+
+    plan = {0: [(3, 0, 0)]}
+    for n, (k, c) in enumerate((k, c) for k in range(1, ts) for c in (2, 3)):
+        plan.setdefault(n, []).append((c, k, "z"))
+        plan.setdefault(n + 2, []).append((c, k, 0))
+        plan.setdefault(n + 4, []).append((c, k, 1))
+    plan.setdefault(2, []).extend([(2, 0, 1), (3, 0, 1)])
+
+    def steps_at(p, place):
+        for slot, items in plan.items():
+            if slot % 2 != place:
+                continue
+
+            @pl.when(p == slot // 2)
             def _():
-                for c, what in items:
+                for item in items:
+                    c, k, what = item
                     if what == "z":
-                        for k in range(1, ts):
-                            net.z_step(c, k)
+                        net.z_step(c, k)
                     elif what < stages:
-                        for k in range(ts):
-                            net.far_step(c, k, what)
+                        net.far_step(c, k, what)
 
     def one_pair(p, carry):
         cols = pl.ds(pl.multiple_of(p * 128, 128), 128)
-        t = jnp.minimum(p, ts - 1)
-        a = jnp.maximum(p - ts, 0)
-        low_q, high_q = vec_ref[2 * a, 7:8, 256:384], vec_ref[2 * a + 1, 7:8, 256:384]
-        bias_q = jnp.where(p < ts, vec_ref[t, 7:8, 0:128], lanes_of(low_q, swap_halves(high_q)))
-        bias_v = jnp.where(p < ts, vec_ref[t, 7:8, 128:256], lanes_of(swap_halves(low_q), high_q))
-        w_q = w_ref[p, :, :, 0:128].reshape(width, 128)
-        y = mm(normed_ref[pl.ds(halo, tokens), :], w_q) + bias_q
-        q_ref[:, cols] = (y.astype(BF16) * 0.125).astype(BF16)
+        _, bias_v = biases(p)
 
         def project(i, c):
-            rows = pl.ds(pl.multiple_of(i * half_rows, 16), half_rows)
-            w_kv = w_ref[p, :, :, 128:384].reshape(width, 256)
-            kv = mm(normed_ref[rows, :], w_kv)
+            rows = pl.ds(pl.multiple_of(i * (halo // 2), 16), halo // 2)
+            kv = mm(normed_ref[rows, :], w_ref[p, :, :, 128:384].reshape(width, 256))
             k_ref[rows, cols] = kv[:, :128].astype(BF16)
             v_ref[rows, cols] = (kv[:, 128:] + bias_v).astype(BF16)
             return c
@@ -403,34 +439,41 @@
         def turn(i, c):
             rows = pl.ds(pl.multiple_of(i * KB, KB), KB)
             vt_ref[:, rows] = v_ref[rows, cols].T
+            k, aux = k_ref[rows, cols], kseg_ref[rows, :]
+            ka_ref[0, rows, :] = lanes_of(k, aux)
+            ka_ref[1, rows, :] = lanes_of(aux, k)
             return c
 
-        lax.fori_loop(0, window // KB, turn, 0)
+        lax.fori_loop(0, (halo + tokens) // KB, turn, 0)
+        steps_at(p, 0)
 
         def one_block(j, c):
             rows = pl.ds(pl.multiple_of(j * QB, QB), QB)
-            q_block = q_ref[rows, cols]
-            doc_row = doc_ref[0:1, rows]
+            q_block, aux = q_ref[rows, cols], qseg_ref[rows, :]
             base = j * QB
+            spans = [(row, size, pl.ds(pl.multiple_of(base + row, 16), size)) for row, size in CHUNKS]
             for h in range(2):
-                query = keep_lanes(q_block, h)
+                query = lanes_of(q_block, aux) if h == 0 else lanes_of(aux, q_block)
                 top = jnp.full((8, QB), -1e30, F32)
-                for i in range(WINDOW):
-                    span = pl.ds(pl.multiple_of(base + i * KB, KB), KB)
-                    s = masked(mm(k_ref[span, cols], query, NT), i, doc_row, base)
-                    s_ref[h, i] = s
+                for row, size, span in spans:
+                    s = causal(mm(ka_ref[h, span, :], query, NT), row)
+                    s_ref[h, row : row + size, :] = s
                     top = jnp.maximum(top, fold_rows(s, jnp.max))
                 top = jnp.max(top, axis=0, keepdims=True)
                 total = jnp.zeros((8, QB), F32)
                 acc = jnp.zeros((HD, QB), F32)
-                for i in range(WINDOW):
-                    span = pl.ds(pl.multiple_of(base + i * KB, KB), KB)
-                    e = jnp.exp(s_ref[h, i] - top)
+                for row, size, span in spans:
+                    e = jnp.exp2(s_ref[h, row : row + size, :] - top)
                     total = total + fold_rows(e, jnp.sum)
-                    acc = acc + mm(vt_ref[h * HD : (h + 1) * HD, span], e.astype(BF16))
+                    if size < KB:
+                        wide = pl.ds(pl.multiple_of(base + row // KB * KB, KB), KB)
+                        e = jnp.concatenate([jnp.zeros((KB - size, QB), F32), e], axis=0)
+                    else:
+                        wide = pl.ds(pl.multiple_of(base + row, KB), KB)
+                    acc = acc + mm(vt_ref[h * HD : (h + 1) * HD, wide], e.astype(BF16))
                 total = jnp.sum(total, axis=0, keepdims=True)
                 ot_ref[pl.ds(pl.multiple_of(p * 128 + h * HD, HD), HD), rows] = acc / total
-                lse_ref[p, h : h + 1, rows] = top + jnp.log(total)
+                lse_ref[p, h : h + 1, rows] = top + jnp.log2(total)
             o = ot_ref[pl.ds(pl.multiple_of(p * 128, 128), 128), rows]
             mixed_ref[rows, cols] = o.T.astype(BF16)
             return c
@@ -439,7 +482,7 @@
         w_o = w_ref[p, :, :, 384:512].reshape(width, 128)
         start = jnp.where(p == 0, x_ref[...].astype(F32) + vec_ref[0, 2:3, :], hidden_ref[...])
         hidden_ref[...] = start + mm(mixed_ref[:, cols], w_o, NT)
-        steps_at(p)
+        steps_at(p, 1)
         return carry
 
     hidden_ref[...] = jnp.zeros_like(hidden_ref)
@@ -478,8 +521,10 @@
             big,
             big,
             s((ts, 8, width), F32),
-            s((8, tokens), jnp.int32),
-            s((window, width), BF16),
+            s((window, 128), BF16),
+            s((tokens, 128), BF16),
+            s((width, window), BF16),
+            s((halo, width), BF16),
             s((tokens, width), BF16),
             s((window, width), BF16),
             s((window, width), BF16),
@@ -489,15 +534,16 @@
             s((tokens, width), F32),
         ],
         in_specs=[vmem, vmem] + [any_spec] * 4,
-        out_specs=[any_spec] * 3 + [vmem] * 10,
+        out_specs=[any_spec] * 3 + [vmem] * 12,
         scratch_shapes=[
             pltpu.VMEM((ts, dp, 8, width), F32),
             pltpu.VMEM((pairs, dp, rows, 512), BF16),
             pltpu.VMEM((ts, dp, rows, 256), BF16),
-            pltpu.VMEM((halo, width), BF16),
             pltpu.VMEM((n_halo, 8, tokens), jnp.int32),
+            pltpu.VMEM((window, width), BF16),
+            pltpu.VMEM((2, window, 128), BF16),
             pltpu.VMEM((128, window), BF16),
-            pltpu.VMEM((2, WINDOW, KB, QB), F32),
+            pltpu.VMEM((2, HALO + QB, QB), F32),
             dma((2 * ts + 4,)),
             dma((4, ts, 2)),
             dma((4, ts)),
@@ -511,6 +557,563 @@
         ),
         name="front",
     )(x, seg, small, qkvo, fc, proj)
+
+
+class Scatter:
+    def __init__(self, dp, ts, srcs, local, in_core, in_far, in_z, sems):
+        self.dp, self.ts, self.srcs, self.local = dp, ts, srcs, local
+        self.in_core, self.in_far, self.in_z = in_core, in_far, in_z
+        self.core_send, self.core_recv, self.far_send, self.far_recv, self.z_send, self.z_recv = sems
+        self.me, self.mt = lax.axis_index("dp"), lax.axis_index("tensor")
+        self.far = [1 << k for k in range(1, dp.bit_length() - 1)]
+        self.evens = list(range(0, dp, 2))
+
+    def block(self, c, t, to):
+        if c < 2:
+            return self.srcs[c].at[t, to // 2, lax.rem(to, 2)]
+        return self.srcs[c].at[t, to]
+
+    def order(self, t):
+        return self.far[::-1] if 2 * t < self.ts else self.far
+
+    def core(self, c, t, m):
+        return pltpu.make_async_remote_copy(
+            src_ref=self.block(c, t, self.me ^ 1 ^ m),
+            dst_ref=self.in_core.at[c, t, m >> 1],
+            send_sem=self.core_send.at[c, t, m >> 1],
+            recv_sem=self.core_recv.at[c, t, m >> 1],
+            device_id={"dp": self.me ^ 1},
+            device_id_type=MESH,
+        )
+
+    def far_moves(self, t, s):
+        order = self.order(t)
+        done = sum(order[:s])
+        first = sum(len(self.evens) >> (i + 1) for i in range(s))
+        masks = [m for m in self.evens if m & order[s] and not m & done]
+        return [(m, first + i) for i, m in enumerate(masks)]
+
+    def far_copy(self, c, t, s, m, slot):
+        return pltpu.make_async_remote_copy(
+            src_ref=self.in_core.at[c, t, m >> 1],
+            dst_ref=self.in_far.at[c, t, slot],
+            send_sem=self.far_send.at[c, t, slot],
+            recv_sem=self.far_recv.at[c, t, slot],
+            device_id={"dp": self.me ^ self.order(t)[s]},
+            device_id_type=MESH,
+        )
+
+    def z_copy(self, c, t):
+        back = lax.rem(self.mt + self.ts - t, self.ts) - 1
+        return pltpu.make_async_remote_copy(
+            src_ref=self.in_core.at[c, t, 0],
+            dst_ref=self.in_z.at[c, back],
+            send_sem=self.z_send.at[c, t],
+            recv_sem=self.z_recv.at[c, back],
+            device_id={"tensor": t},
+            device_id_type=MESH,
+        )
+
+    def start(self, c, t):
+        for m in self.evens[::-1]:
+            self.core(c, t, m).start()
+
+    def step(self, c, t, s):
+        if s == 0:
+            for m in self.evens[::-1]:
+                self.core(c, t, m).wait_recv()
+                to = self.me ^ m
+                mine = self.local[c, t, to // 2] if c < 2 else self.srcs[c][t, to]
+                self.in_core[c, t, m >> 1] = self.in_core[c, t, m >> 1] + mine
+        else:
+            bit = self.order(t)[s - 1]
+            for m, slot in self.far_moves(t, s - 1):
+                self.far_copy(c, t, s - 1, m, slot).wait_recv()
+                to = (m ^ bit) >> 1
+                self.in_core[c, t, to] = self.in_core[c, t, to] + self.in_far[c, t, slot]
+        if s < len(self.far):
+            for m, slot in self.far_moves(t, s):
+                self.far_copy(c, t, s, m, slot).start()
+        else:
+
+            @pl.when(self.mt != t)
+            def _():
+                self.z_copy(c, t).start()
+
+    def final(self, c, out_ref):
+        total = self.in_core[c, self.mt, 0].astype(F32)
+        for k in range(self.ts - 1):
+            pltpu.make_async_remote_copy(
+                src_ref=self.in_core.at[c, 0, 0],
+                dst_ref=self.in_z.at[c, k],
+                send_sem=self.z_send.at[c, 0],
+                recv_sem=self.z_recv.at[c, k],
+                device_id={"tensor": self.mt},
+                device_id_type=MESH,
+            ).wait_recv()
+            total = total + self.in_z[c, k].astype(F32)
+        out_ref[c] = total
+
+    def finish(self):
+        for c in range(len(self.srcs)):
+            for t in range(self.ts):
+                for m in self.evens:
+                    self.core(c, t, m).wait_send()
+                for s in range(len(self.far)):
+                    for m, slot in self.far_moves(t, s):
+                        self.far_copy(c, t, s, m, slot).wait_send()
+
+                @pl.when(self.mt != t)
+                def _():
+                    self.z_copy(c, t).wait_send()
+
+
+def norm_back(grad_in, gain_vec, unit_rows, scaler):
+    scaled = grad_in * gain_vec
+    return scaler * (
+        scaled
+        - jnp.mean(scaled, axis=-1, keepdims=True)
+        - unit_rows * jnp.mean(scaled * unit_rows, axis=-1, keepdims=True)
+    )
+
+
+class Total:
+    def __init__(self, dp, ts, mine, dp_in, z_in, sends, recvs):
+        self.dp, self.ts, self.mine, self.dp_in, self.z_in = dp, ts, mine, dp_in, z_in
+        self.sends, self.recvs = sends, recvs
+        self.me, self.mt = lax.axis_index("dp"), lax.axis_index("tensor")
+
+    def over_dp(self, m):
+        return pltpu.make_async_remote_copy(
+            src_ref=self.mine,
+            dst_ref=self.dp_in.at[m],
+            send_sem=self.sends.at[m],
+            recv_sem=self.recvs.at[m],
+            device_id={"dp": self.me ^ m},
+            device_id_type=MESH,
+        )
+
+    def over_z(self, k):
+        return pltpu.make_async_remote_copy(
+            src_ref=self.z_in.at[0],
+            dst_ref=self.z_in.at[self.ts - k],
+            send_sem=self.sends.at[self.dp + k],
+            recv_sem=self.recvs.at[self.dp + self.ts - k],
+            device_id={"tensor": lax.rem(self.mt + k, self.ts)},
+            device_id_type=MESH,
+        )
+
+    def start(self):
+        for m in range(1, self.dp):
+            self.over_dp(m).start()
+
+    def turn(self):
+        total = self.mine[...]
+        for m in range(1, self.dp):
+            self.over_dp(m).wait_recv()
+            total = total + self.dp_in[m]
+        self.z_in[0] = total
+        for k in range(1, self.ts):
+            self.over_z(k).start()
+
+    def end(self, out_ref):
+        total = self.z_in[0]
+        for k in range(1, self.ts):
+            self.over_z(k).wait_recv()
+            total = total + self.z_in[self.ts - k]
+        out_ref[...] = total
+
+    def finish(self):
+        for m in range(1, self.dp):
+            self.over_dp(m).wait_send()
+        for k in range(1, self.ts):
+            self.over_z(k).wait_send()
+
+
+def back_kernel(
+    dp,
+    ts,
+    x_ref,
+    halo_ref,
+    vec_ref,
+    kseg_ref,
+    qseg_ref,
+    normed_t_ref,
+    q_ref,
+    k_ref,
+    v_ref,
+    ot_ref,
+    lse_ref,
+    mixed_ref,
+    grad_hidden_ref,
+    small_ref,
+    g_proj,
+    g_fc,
+    qkvo_all,
+    input_grad_ref,
+    sums_ref,
+    small_out,
+    late_out,
+    w_ref,
+    g_qkvo,
+    low_ref,
+    low_t_ref,
+    ka_ref,
+    kt_ref,
+    dk_ref,
+    dv_ref,
+    gm_ref,
+    delta_ref,
+    dqkv_ref,
+    dkv_ref,
+    give_ref,
+    take_ref,
+    gh_ref,
+    gw_ref,
+    g_local,
+    small_in,
+    small_z,
+    late_own,
+    late_in,
+    late_z,
+    in_core,
+    in_far,
+    in_z,
+    local_sem,
+    core_send,
+    core_recv,
+    far_send,
+    far_recv,
+    z_send,
+    z_recv,
+    halo_send,
+    halo_recv,
+    small_send,
+    small_recv,
+    late_send,
+    late_recv,
+):
+    me, mt = lax.axis_index("dp"), lax.axis_index("tensor")
+    tokens, width = x_ref.shape
+    halo = halo_ref.shape[0]
+    pairs = width // 128
+    parts = halo_parts(tokens, ts)
+    meet(dp, ts)
+    sems = (core_send, core_recv, far_send, far_recv, z_send, z_recv)
+    net = Scatter(dp, ts, [g_proj, g_fc, g_qkvo], g_local, in_core, in_far, in_z, sems)
+    early = Total(dp, ts, small_ref, small_in, small_z, small_send, small_recv)
+    late = Total(dp, ts, late_own, late_in, late_z, late_send, late_recv)
+    stages = len(net.far) + 1
+    zigzag = [t for pair in zip(range(ts // 2), range(ts // 2, ts)) for t in pair]
+    for c in (0, 1):
+        for t in zigzag:
+            net.start(c, t)
+    early.start()
+    loads = weight_loads(qkvo_all, w_ref, g_qkvo, local_sem, ts)
+    loads += [
+        pltpu.make_async_copy(g.at[:, :, lax.rem(me, 2)], g_local.at[c], local_sem.at[2 * ts + c])
+        for c, g in enumerate((g_proj, g_fc))
+    ]
+    for load in loads:
+        load.start()
+
+    def low_rows(i, c):
+        rows = pl.ds(pl.multiple_of(i * KB, KB), KB)
+        low = grad_hidden_ref[rows, :].astype(BF16)
+        low_ref[rows, :] = low
+        for n in range(pairs):
+            low_t_ref[n * KB : (n + 1) * KB, rows] = low[:, n * KB : (n + 1) * KB].T
+        return c
+
+    lax.fori_loop(0, tokens // KB, low_rows, 0)
+    for load in loads:
+        load.wait()
+    merge_pairs(w_ref, g_qkvo, ts)
+    late_own[...] = jnp.zeros_like(late_own)
+    gw_ref[...] = jnp.zeros_like(gw_ref)
+    gh_ref[...] = jnp.zeros_like(gh_ref)
+
+    plan = {5: ["turn"], 9: ["end"]}
+    units = [(c, t) for c in (0, 1) for t in zigzag]
+    for n, (c, t) in enumerate(units):
+        for s in range(stages):
+            plan.setdefault(2 * n + 1 + 3 * s, []).append((c, t, s))
+    plan.setdefault(4 * pairs, []).extend(["final0", "final1"])
+    for t in range(ts):
+        at = 4 * pairs + pairs - ts + t
+        plan.setdefault(at, []).append((2, t, "start"))
+        for s in range(stages):
+            plan.setdefault(at + 1 + s, []).append((2, t, s))
+
+    def run(items):
+        for item in items:
+            if item == "turn":
+                early.turn()
+            elif item == "end":
+                early.end(small_out)
+            elif item in ("final0", "final1"):
+                net.final(int(item[-1]), sums_ref)
+            elif item[2] == "start":
+                net.start(item[0], item[1])
+            else:
+                net.step(*item)
+
+    def steps_at(n, place):
+        for slot, items in sorted(plan.items()):
+            if slot % 4 == place and slot < 4 * pairs:
+
+                @pl.when(n == slot // 4)
+                def _():
+                    run(items)
+
+    def give(i):
+        back, count = parts[i]
+        end = halo - sum(c for _, c in parts[:i])
+        return pltpu.make_async_remote_copy(
+            src_ref=give_ref.at[pl.ds(end - count, count)],
+            dst_ref=take_ref.at[pl.ds(end - count, count)],
+            send_sem=halo_send.at[i],
+            recv_sem=halo_recv.at[i],
+            device_id={"tensor": lax.rem(mt + ts - back, ts)},
+            device_id_type=MESH,
+        )
+
+    def attend_back(n, carry):
+        p = lax.rem(n + ts, pairs)
+        cols = pl.ds(pl.multiple_of(p * 128, 128), 128)
+        w_o = w_ref[p, :, :, 384:512].reshape(width, 128)
+        rounded = mm(low_ref[...], w_o).astype(BF16)
+        gm_ref[...] = rounded
+        weighted = rounded.astype(F32).T * ot_ref[pl.ds(pl.multiple_of(p * 128, 128), 128), :]
+        for h in range(2):
+            delta_ref[h : h + 1, :] = jnp.sum(weighted[h * HD : (h + 1) * HD], axis=0, keepdims=True)
+
+        def turn(i, c):
+            rows = pl.ds(pl.multiple_of(i * KB, KB), KB)
+            k, aux = k_ref[rows, cols], kseg_ref[rows, :]
+            kt_ref[:, rows] = k.T
+            ka_ref[0, rows, :] = lanes_of(k, aux)
+            ka_ref[1, rows, :] = lanes_of(aux, k)
+            dk_ref[rows, :] = jnp.zeros((KB, 128), F32)
+            dv_ref[rows, :] = jnp.zeros((KB, 128), F32)
+            return c
+
+        lax.fori_loop(0, (halo + tokens) // KB, turn, 0)
+        steps_at(n, 0)
+
+        def one_block(j, c):
+            base = j * QB
+            at = pl.ds(pl.multiple_of(base, QB), QB)
+            q_block, aux, do_block = q_ref[at, cols], qseg_ref[at, :], gm_ref[at, :]
+            asks = [lanes_of(q_block, aux), lanes_of(aux, q_block)]
+            q_cat = jnp.concatenate([keep_lanes(q_block, h) for h in range(2)], axis=0)
+            do_cat = jnp.concatenate([keep_lanes(do_block, h) for h in range(2)], axis=0)
+            lse = [lse_ref[p, h : h + 1, at] for h in range(2)]
+            delta = [delta_ref[h : h + 1, at] for h in range(2)]
+            dq_t = [jnp.zeros((HD, QB), F32) for h in range(2)]
+            for row, size in CHUNKS:
+                span = pl.ds(pl.multiple_of(base + row, 16), size)
+                values = v_ref[span, cols]
+                ps, dss = [], []
+                for h in range(2):
+                    s = causal(mm(ka_ref[h, span, :], asks[h], NT), row)
+                    e = jnp.exp2(s - lse[h])
+                    grad_e = mm(values, do_cat[h * QB : (h + 1) * QB], NT)
+                    ds = (e * (grad_e - delta[h])).astype(BF16)
+                    wide = pl.ds(pl.multiple_of(base + row // KB * KB, KB), KB)
+                    tall = ds
+                    if size < KB:
+                        tall = jnp.concatenate([jnp.zeros((KB - size, QB), BF16), ds], axis=0)
+                    dq_t[h] = dq_t[h] + mm(kt_ref[h * HD : (h + 1) * HD, wide], tall)
+                    ps.append(e.astype(BF16))
+                    dss.append(ds)
+                dv_ref[span, :] += mm(jnp.concatenate(ps, axis=1), do_cat)
+                dk_ref[span, :] += mm(jnp.concatenate(dss, axis=1), q_cat)
+            dqkv_ref[n, at, 0:128] = (jnp.concatenate(dq_t, axis=0) * 0.125).T.astype(BF16)
+            for place in range(tokens // QB):
+
+                @pl.when(j == place)
+                def _():
+                    steps_at(n, 1 + place)
+            return c
+
+        lax.fori_loop(0, tokens // QB, one_block, 0)
+
+        dkv_ref[n, :, 0:128] = (dk_ref[:halo, :] * (0.125 / Q_SCALE)).astype(BF16)
+        dkv_ref[n, :, 128:256] = dv_ref[:halo, :].astype(BF16)
+        dqkv_ref[n, :, 128:256] = (dk_ref[halo:, :] * (0.125 / Q_SCALE)).astype(BF16)
+        dqkv_ref[n, :, 256:384] = dv_ref[halo:, :].astype(BF16)
+
+        def halo_grad(i, c):
+            rows = pl.ds(pl.multiple_of(i * (halo // 2), 16), halo // 2)
+            gh_ref[rows, :] += mm(dkv_ref[n, rows, :], w_ref[p, :, :, 128:384].reshape(width, 256), NT)
+            return c
+
+        lax.fori_loop(0, 2, halo_grad, 0)
+        steps_at(n, 3)
+        return carry
+
+    def store(tile, value, t):
+        g_qkvo[t, :, :, tile * 128 : (tile + 1) * 128] = value.astype(BF16).reshape(dp, -1, 128)
+
+    def weights_back(n, carry):
+        p = lax.rem(n + ts, pairs)
+        cols = pl.ds(pl.multiple_of(p * 128, 128), 128)
+        grad_o = mm(low_t_ref[...], mixed_ref[:, cols])
+        dqkv = dqkv_ref[n]
+        own = mm(normed_t_ref[:, halo:], dqkv)
+        far = mm(normed_t_ref[:, :halo], dkv_ref[n])
+        four = [own[:, 0:128], own[:, 128:256] + far[:, 0:128], own[:, 256:384] + far[:, 128:256], grad_o]
+
+        @pl.when(p < ts)
+        def _():
+            for i, g in enumerate(four):
+                store(i, g, p)
+
+        for a in range(pairs - ts):
+
+            @pl.when(p == ts + a)
+            def _():
+                for i in range(2):
+                    low_half, high_half = four[2 * i], four[2 * i + 1]
+                    store(4 + i, lanes_of(low_half, swap_halves(high_half)), 2 * a)
+                    store(4 + i, lanes_of(swap_halves(low_half), high_half), 2 * a + 1)
+
+        gw_ref[...] += mm(dqkv, w_ref[p, :, :, 0:384].reshape(width, 384), NT)
+        grad_v = jnp.sum(dqkv[:, 256:384].astype(F32), axis=0, keepdims=True)
+        late_own[2:3, cols] = jnp.sum(dqkv[:, 0:128].astype(F32), axis=0, keepdims=True)
+        late_own[3:4, cols] = grad_v + jnp.sum(dkv_ref[n, :, 128:256].astype(F32), axis=0, keepdims=True)
+        for slot, items in sorted(plan.items()):
+            if 4 * pairs <= slot < 5 * pairs:
+
+                @pl.when(n == slot - 4 * pairs)
+                def _():
+                    run(items)
+        return carry
+
+    lax.fori_loop(0, pairs, attend_back, 0)
+    give_ref[...] = gh_ref[...].astype(BF16)
+    for i, (back, _) in enumerate(parts):
+
+        @pl.when(mt >= back)
+        def _():
+            give(i).start()
+
+    def halo_sums(i, carry):
+        rows = pl.ds(pl.multiple_of(i * KB, KB), KB)
+        unit, _ = normalize(halo_ref[rows, :].astype(F32))
+        g = gh_ref[rows, :]
+        return carry[0] + fold_rows(g * unit, jnp.sum), carry[1] + fold_rows(g, jnp.sum)
+
+    def own_sums(i, carry):
+        rows = pl.ds(pl.multiple_of(i * KB, KB), KB)
+        unit, _ = normalize(x_ref[rows, :].astype(F32))
+        g = gw_ref[rows, :]
+        return carry[0] + fold_rows(g * unit, jnp.sum), carry[1] + fold_rows(g, jnp.sum)
+
+    zero = jnp.zeros((8, width), F32)
+    carry = lax.fori_loop(0, halo // KB, halo_sums, (zero, zero))
+    lax.fori_loop(0, pairs, weights_back, 0)
+    tail = [items for slot, items in sorted(plan.items()) if slot >= 5 * pairs]
+    run(tail[0])
+    gains, shifts = lax.fori_loop(0, tokens // KB, own_sums, carry)
+    late_own[0:1, :] = jnp.sum(gains, axis=0, keepdims=True)
+    late_own[1:2, :] = jnp.sum(shifts, axis=0, keepdims=True)
+    late.start()
+    for items in tail[1:]:
+        run(items)
+    late.turn()
+    for i, (back, count) in enumerate(parts):
+
+        @pl.when(mt + back < ts)
+        def _():
+            give(i).wait_recv()
+            end = halo - sum(c for _, c in parts[:i])
+            gw_ref[tokens - count :, :] += take_ref[end - count : end, :].astype(F32)
+
+    def own_grad(i, carry):
+        rows = pl.ds(pl.multiple_of(i * KB, KB), KB)
+        unit, scaler = normalize(x_ref[rows, :].astype(F32))
+        g = gw_ref[rows, :]
+        input_grad_ref[rows, :] = grad_hidden_ref[rows, :] + norm_back(g, vec_ref[0, 0:1, :], unit, scaler)
+        return carry
+
+    lax.fori_loop(0, tokens // KB, own_grad, 0)
+    late.end(late_out)
+    net.final(2, sums_ref)
+    early.finish()
+    late.finish()
+    for i, (back, _) in enumerate(parts):
+
+        @pl.when(mt >= back)
+        def _():
+            give(i).wait_send()
+
+    net.finish()
+
+
+def back(x, halo_x, vec, kseg, qseg, normed_t, q, k, v, ot, lse, mixed, grad_hidden, small, g_proj, g_fc, qkvo_all):
+    tokens, width = x.shape
+    halo = halo_x.shape[0]
+    window = halo + tokens
+    ts, dp, rows = qkvo_all.shape[:3]
+    pairs = width // 128
+    n_halo = len(halo_parts(tokens, ts))
+    n_far = dp // 2 - 1
+    any_spec = pl.BlockSpec(memory_space=pl.ANY)
+    vmem = pl.BlockSpec(memory_space=pltpu.VMEM)
+    s = jax.ShapeDtypeStruct
+    dma = pltpu.SemaphoreType.DMA
+    return pl.pallas_call(
+        functools.partial(back_kernel, dp, ts),
+        out_shape=[s((tokens, width), F32), s((3, rows, width), F32), s(small.shape, F32), s((8, width), F32)],
+        in_specs=[vmem] * 14 + [any_spec] * 3,
+        out_specs=[vmem] * 4,
+        scratch_shapes=[
+            pltpu.VMEM((pairs, dp, rows, 512), BF16),
+            pltpu.VMEM((ts, dp, rows, width), BF16),
+            pltpu.VMEM((tokens, width), BF16),
+            pltpu.VMEM((width, tokens), BF16),
+            pltpu.VMEM((2, window, 128), BF16),
+            pltpu.VMEM((128, window), BF16),
+            pltpu.VMEM((window, 128), F32),
+            pltpu.VMEM((window, 128), F32),
+            pltpu.VMEM((tokens, 128), BF16),
+            pltpu.VMEM((8, tokens), F32),
+            pltpu.VMEM((pairs, tokens, 384), BF16),
+            pltpu.VMEM((pairs, halo, 256), BF16),
+            pltpu.VMEM((halo, width), BF16),
+            pltpu.VMEM((halo, width), BF16),
+            pltpu.VMEM((halo, width), F32),
+            pltpu.VMEM((tokens, width), F32),
+            pltpu.VMEM((2, ts, dp // 2, rows, width), BF16),
+            pltpu.VMEM((dp,) + small.shape, F32),
+            pltpu.VMEM((ts,) + small.shape, F32),
+            pltpu.VMEM((8, width), F32),
+            pltpu.VMEM((dp, 8, width), F32),
+            pltpu.VMEM((ts, 8, width), F32),
+            pltpu.VMEM((3, ts, dp // 2, rows, width), BF16),
+            pltpu.VMEM((3, ts, n_far, rows, width), BF16),
+            pltpu.VMEM((3, ts - 1, rows, width), BF16),
+            dma((2 * ts + 2,)),
+            dma((3, ts, dp // 2)),
+            dma((3, ts, dp // 2)),
+            dma((3, ts, n_far)),
+            dma((3, ts, n_far)),
+            dma((3, ts)),
+            dma((3, ts - 1)),
+            dma((n_halo,)),
+            dma((n_halo,)),
+            dma((dp + ts,)),
+            dma((dp + ts,)),
+            dma((dp + ts,)),
+            dma((dp + ts,)),
+        ],
+        compiler_params=pltpu.CompilerParams(
+            collective_id=2, has_side_effects=True, vmem_limit_bytes=63 << 20
+        ),
+        name="back",
+    )(x, halo_x, vec, kseg, qseg, normed_t, q, k, v, ot, lse, mixed, grad_hidden, small, g_proj, g_fc, qkvo_all)
 
 
 def gather_kernel(dp, ts, tokens, n_in, *refs):
@@ -954,15 +1557,6 @@
             1.0
             + jnp.tanh(TANH_SLOPE * (values_in + CUBIC_TERM * values_in * values_in * values_in))
         )
-    )
-
-
-def norm_back(grad_in, gain_vec, unit_rows, scaler):
-    scaled = grad_in * gain_vec
-    return scaler * (
-        scaled
-        - jnp.mean(scaled, axis=-1, keepdims=True)
-        - unit_rows * jnp.mean(scaled * unit_rows, axis=-1, keepdims=True)
     )
 
 
@@ -1157,15 +1751,12 @@
     me, mt = lax.axis_index("dp"), lax.axis_index("tensor")
     tokens, width = block_input.shape[1:]
     total_tokens = tokens * ts * dp
-    halo = -(-(DOC_MOST - 1) // KB) * KB
     e = qkv_weight.shape[2]
     x = block_input[0]
     valid_rows = valid_mask[0].astype(F32)
 
-    out_t = out_weight.T
-    cuts = [qkv_weight[0], qkv_weight[1], qkv_weight[2], out_t]
+    cuts = [qkv_weight[0], qkv_weight[1], qkv_weight[2], out_weight.T]
     qkvo = jnp.concatenate([c[:, : 2 * HD] for c in cuts] + [c[:, 2 * HD :] for c in cuts], axis=1)
-    local_count = jnp.sum(valid_rows)
     mine = jnp.arange(dp) == me
 
     def spread(v):
@@ -1178,38 +1769,24 @@
             spread(vectors).reshape(6, width),
             spread(fc_bias).reshape(1, -1),
             jnp.concatenate(
-                [qv[0, : 2 * HD], qv[1, : 2 * HD], qv[0, 2 * HD :], qv[1, 2 * HD :], local_count[None]]
+                [qv[0, : 2 * HD], qv[1, : 2 * HD], qv[0, 2 * HD :], qv[1, 2 * HD :], jnp.sum(valid_rows)[None]]
                 + [jnp.zeros((width - 2 * e - 1,), F32)]
             )[None],
         ]
     )
     seg_rows = jnp.broadcast_to(segment_ids, (8, tokens))
-    qkvo_all, w_fc, w_proj, vec, doc, normed_window, q, k, v, mixed_t, lse, mixed, hidden = front(
-        x, seg_rows, small, qkvo, fc_weight, proj_weight.T, dp, ts, halo
+    qkvo_all, w_fc, w_proj, vec, kseg, qseg, normed_t, halo_x, q, k, v, ot, lse, mixed, hidden = front(
+        x, seg_rows, small, qkvo, fc_weight, proj_weight.T, dp, ts, HALO
     )
-    gain_one, bias_one, b_out, gain_two, bias_two, b_proj = [vec[0, i] for i in range(6)]
-    b_fc = vec[:, 6].reshape(-1)
+    gain_two, bias_two, b_proj = [vec[0, i] for i in (3, 4, 5)]
+    b_fc = vec[:, 6]
     valid_count = jnp.sum(vec[:, 7, 2 * e])
-    w_qkvo = qkvo_all.reshape(ts, width, 4 * e)
-
-    def pair_weights(i):
-        low = w_qkvo[:, :, i * 128 : (i + 1) * 128]
-        last = w_qkvo[:, :, 512 + i * HD : 512 + (i + 1) * HD]
-        last = last.reshape(ts // 2, 2, width, HD).transpose(0, 2, 1, 3).reshape(ts // 2, width, 128)
-        return jnp.concatenate([low, last]).transpose(1, 0, 2).reshape(width, width)
-
-    wq, wk, wv, wo = [pair_weights(i) for i in range(4)]
     wf = w_fc.reshape(ts, width, -1)
     wp = w_proj.reshape(ts, width, -1)
-    doc = doc[0:1]
-    first = doc[0, ::QB] // KB
-
-    inputs = x.astype(F32)
-    unit_one, scale_one = normalize(inputs)
-    normed_one = normed_window[halo:]
+
     unit_two, scale_two = normalize(hidden)
     normed_two = (unit_two * gain_two + bias_two).astype(BF16)
-    pre_act = jnp.einsum("sd,tdf->stf", normed_two, wf, preferred_element_type=F32) + b_fc.reshape(ts, -1)
+    pre_act = jnp.einsum("sd,tdf->stf", normed_two, wf, preferred_element_type=F32) + b_fc
     activated = gelu_tanh(pre_act).astype(BF16)
     output = hidden + jnp.einsum("stf,tdf->sd", activated, wp, preferred_element_type=F32) + b_proj
     residual_error = output - teacher[0].astype(F32)
@@ -1221,83 +1798,57 @@
     _, gelu_back = jax.vjp(gelu_tanh, pre_act)
     grad_pre = gelu_back(grad_act)[0].astype(BF16)
     grad_fc_w = jnp.einsum("sd,stf->tdf", normed_two, grad_pre, preferred_element_type=F32)
-    grad_fc_b = jnp.sum(grad_pre, axis=0, dtype=F32)
     grad_normed_two = jnp.einsum("stf,tdf->sd", grad_pre, wf, preferred_element_type=F32)
-    grad_gain_two = jnp.sum(grad_normed_two * unit_two, axis=0)
-    grad_bias_two = jnp.sum(grad_normed_two, axis=0)
     grad_hidden = grad_output + norm_back(grad_normed_two, gain_two, unit_two, scale_two)
-    low_hidden = grad_hidden.astype(BF16)
-    grad_mixed = mm(low_hidden, wo).astype(BF16)
-    grad_out_w = jnp.einsum("sd,se->de", low_hidden, mixed, preferred_element_type=F32)
-    heads = width // HD
-    delta = jnp.sum((grad_mixed.T.astype(F32) * mixed_t).reshape(heads // 2, 2, HD, tokens), axis=2)
-    dq_t, dk, dv = attend_back(first, doc, q, k, k.T, v, grad_mixed, lse, delta, halo)
-    dq, dk, dv = dq_t.T.astype(BF16), dk.astype(BF16), dv.astype(BF16)
-    sd_se = lambda a, b: jnp.einsum("sd,se->de", a, b, preferred_element_type=F32)
-    g_q, g_k, g_v = sd_se(normed_one, dq), sd_se(normed_window, dk), sd_se(normed_window, dv)
-    grad_window = mm(dk, wk, NT) + mm(dv, wv, NT)
-    grad_normed_one = grad_window[halo:] + mm(dq, wq, NT)
-    end = halo
-    for back, count in halo_parts(tokens, ts):
-        end -= count
-        part = lax.ppermute(
-            grad_window[end : end + count].astype(BF16), "tensor", [(t, t - back) for t in range(back, ts)]
+    small_grads = jnp.concatenate(
+        [
+            jnp.sum(grad_hidden, axis=0)[None],
+            jnp.sum(grad_normed_two * unit_two, axis=0)[None],
+            jnp.sum(grad_normed_two, axis=0)[None],
+            jnp.sum(grad_output, axis=0)[None],
+            jnp.sum(grad_pre, axis=0, dtype=F32),
+            jnp.full((1, width), squares),
+            jnp.zeros((-(5 + ts) % 8, width), F32),
+        ]
+    )
+    blocks = lambda g: g.astype(BF16).reshape(ts, dp // 2, 2, width // dp, width)
+    input_grad, sums, small_sums, late_sums = back(
+        x, halo_x, vec, kseg, qseg, normed_t, q, k, v, ot, lse, mixed, grad_hidden, small_grads,
+        blocks(grad_proj_w), blocks(grad_fc_w), qkvo_all,
+    )
+    r_proj, r_fc, r_qkvo = sums
+    own = lambda a: lax.dynamic_slice_in_dim(a, me * (width // dp), width // dp, 1)
+    own_late, own_small = own(late_sums), own(small_sums)
+    fc_b = small_sums[4 : 4 + ts].reshape(ts, -1, dp, fc_bias.shape[1])
+    fc_b = lax.dynamic_index_in_dim(lax.dynamic_index_in_dim(fc_b, mt, 0, False), me, 1, False)
+
+    def by_head(v):
+        low = lax.dynamic_slice_in_dim(v, mt * 2 * HD, 2 * HD, 1)
+        last = lax.dynamic_slice_in_dim(v, ts * 2 * HD + mt * HD, HD, 1)
+        v = jnp.concatenate([low, last], axis=1).reshape(2, -1, dp, qv_bias.shape[2])
+        return lax.dynamic_index_in_dim(v, me, 2, False)
+
+    def columns(i):
+        return jnp.concatenate(
+            [r_qkvo[:, i * 128 : (i + 1) * 128], r_qkvo[:, 512 + i * HD : 512 + (i + 1) * HD]], axis=1
         )
-        grad_normed_one = grad_normed_one.at[tokens - count :].add(part.astype(F32))
-    grad_input = grad_hidden + norm_back(grad_normed_one, gain_one, unit_one, scale_one)
-
-    def by_t(gs):
-        gs = jnp.stack([g.reshape(width, -1, 128) for g in gs])
-        low = gs[:, :, :ts].transpose(2, 1, 0, 3).reshape(ts, width, 512)
-        last = gs[:, :, ts:].reshape(4, width, ts, HD).transpose(2, 1, 0, 3).reshape(ts, width, 256)
-        return jnp.concatenate([low, last], axis=2)
-
-    g_qkvo = by_t([g_q, g_k, g_v, grad_out_w])
-    grads = jnp.stack([grad_proj_w, grad_fc_w, g_qkvo]).astype(BF16)
-    grads = grads.reshape(3, ts, dp, width // dp, -1)
-    r_proj, r_fc, r_qkvo = reduce(grads, dp, ts)
-    def by_head(v):
-        return jnp.concatenate([v[: ts * 128].reshape(ts, 128), v[ts * 128 :].reshape(ts, HD)], axis=1).reshape(-1)
-
-    def columns(i):
-        return jnp.concatenate([r_qkvo[:, i * 128 : (i + 1) * 128], r_qkvo[:, 512 + i * HD : 512 + (i + 1) * HD]], axis=1)
-
-    smalls = [
-        jnp.sum(grad_normed_one * unit_one, axis=0),
-        jnp.sum(grad_normed_one, axis=0),
-        jnp.sum(grad_hidden, axis=0),
-        grad_gain_two,
-        grad_bias_two,
-        jnp.sum(grad_output, axis=0),
-        grad_fc_b.reshape(-1),
-        by_head(jnp.sum(dq, axis=0, dtype=F32)),
-        by_head(jnp.sum(dv, axis=0, dtype=F32)),
-        squares[None],
-    ]
-    summed = lax.psum(jnp.concatenate(smalls), ("dp", "tensor"))
-    rows = width // dp
-    own_rows = lambda i: lax.dynamic_slice_in_dim(summed, i * width + me * rows, rows)
-    fc_b = summed[6 * width : 6 * width + fc_bias.size * dp * ts].reshape(ts, -1, dp, fc_bias.shape[1])
-    qv0 = 6 * width + fc_bias.size * dp * ts
-    qv_b = summed[qv0 : qv0 + 2 * width].reshape(2, ts, -1, dp, qv_bias.shape[2])
-    loss = summed[-1] / (width * valid_count)
-    pick = lambda a, i, ax: lax.dynamic_index_in_dim(a, i, ax, keepdims=False)
+
     return (
         output.astype(BF16)[None],
-        loss,
-        grad_input[None],
-        own_rows(0),
-        own_rows(1),
+        small_sums[4 + ts, 0] / (width * valid_count),
+        input_grad[None],
+        own_late[0],
+        own_late[1],
         jnp.stack([columns(i) for i in range(3)]),
-        pick(pick(qv_b, mt, 1), me, 2),
+        by_head(late_sums[2:4]),
         columns(3).T,
-        own_rows(2),
-        own_rows(3),
-        own_rows(4),
+        own_small[0],
+        own_small[1],
+        own_small[2],
         r_fc,
-        pick(pick(fc_b, mt, 0), me, 1),
+        fc_b,
         r_proj.T,
-        own_rows(5),
+        own_small[3],
     )
 
 

time: 520 us -> 327 us (0.63)
  local copies, waits for them, and re-layouts: 77.7 us -> 22.4 us
  Pallas kernels: 292 us -> 249 us
  blocking collectives: 40.3 us -> 0 us
  matrix products: 63.6 us -> 35.6 us
  other arithmetic: 35.8 us -> 12.8 us
    pallas_call x1, Pallas kernels: 144 us -> 104 us  [front(): pl.pallas_call(functools.partial(front_kernel, dp, ts), out_shape=[big, b...]
    psum x1 -> x0, blocking collectives: 40.3 us -> none  [on_device(): summed = lax.psum(jnp.concatenate(smalls), ('dp', 'tensor'))]
    dot_general x9 -> x1, matrix products: 25.2 us -> 4.83 us  [on_device(): jnp.einsum('sd,tdf->stf', normed_two, wf, preferred_element_type=F32) + b_fc]
    concatenate x4 -> x1, local copies, waits for them, and re-layouts: 17.6 us -> 1.26 us  [on_device(): jnp.concatenate([jnp.sum(grad_hidden, axis=0)[None], jnp.sum(grad_normed_...]
    slice x19 -> x5, local copies, waits for them, and re-layouts: 16.1 us -> 4.71 us  [the longest x1 1.31 us: on_device(): small_sums[4 + ts, 0] / (width * valid_count)]
    another operation x2 -> x0, other arithmetic: 11.1 us -> none  [the longest x1 10.5 us: on_device(): grads = jnp.stack([grad_proj_w, grad_fc_w, g_qkvo]).astype(BF16)]
    unnamed x108 -> x29, local copies, waits for them, and re-layouts: 13.6 us -> 4.85 us
    transpose x3 -> x1, local copies, waits for them, and re-layouts: 9.95 us -> 2.01 us  [on_device(): return (output.astype(BF16)[None], small_sums[4 + ts, 0] / (width * valid...]
  transfers between devices with their start and end apart: 2 -> 0, of which waited for: 0 -> 0; matrix products, arithmetic and copies ran while one was open for 15% -> 0% of each run, Pallas kernels for 24% -> 0%
where the time goes in v1:
time: 327 us; the launch traced here: 324 us
  Pallas kernels  249 us (76%)
  matrix products  35.6 us (11%)
  local copies, waits for them, and re-layouts  22.4 us (7%)
  other arithmetic  12.8 us (4%)
  between operations  4.24 us (1%)
    pallas_call x1, Pallas kernels, back(): pl.pallas_call(functools.partial(back_kernel, dp, ts), out_shape=[s((toke...  145 us
    pallas_call x1, Pallas kernels, front(): pl.pallas_call(functools.partial(front_kernel, dp, ts), out_shape=[big, b...  104 us
    dot_general x1, matrix products, on_device(): jnp.einsum('sd,tdf->stf', low_output, wp, preferred_element_type=F32)  10.6 us
    dot_general x1, matrix products, on_device(): jnp.einsum('sd,stf->tdf', low_output, activated, preferred_element_type=F32)  8.57 us

profile of v1, /device:TPU:0, one launch (start us, length us, event | category | flops | bytes accessed | tf_op | source)
XLA Modules:
  0.0 323.6 jit_solution(14552736526766389281)
XLA Ops:
  0.6 0.7 convert_element_type.71
  1.3 1.3 broadcast_in_dim.125.seg_ref
  2.6 0.7 copy.40
  3.3 0.1 broadcast_in_dim.139
  3.5 0.1 broadcast_in_dim.136
  3.6 1.3 convert_reduce_fusion.1
  4.9 0.7 concatenate.27
  5.7 0.8 copy.39
  6.5 0.1 reshape.126
  6.6 0.8 stack.39
  7.4 0.1 broadcast_in_dim.130
  7.5 0.1 broadcast_in_dim.127
  7.6 0.6 pad_maximum_fusion.1.small_ref
  8.3 0.9 slice_bitcast_fusion.3
  9.2 0.9 copy.41
  10.1 0.8 concatenate.29.qkvo_ref
  10.9 103.6 %front.1 = (bf16[4,8,96,768]{3,2,1,0:T(8,128)(2,1)}, bf16[4,8,96,768]{3,2,1,0:T(8,128)(2,1)}, bf16[4,8,96,768]{3,2,1,0:T(8,128)(2,1)}, f32[4,8,768]{2,1,0:T(8,12...) custom-call(bf16[512,768]{1,0:T(8,128)(2,1)} %bitcast.122, ...), custom_call_target="tpu_custom_call" | custom-call | tf_op jit(solution)/shard_map/front/pallas_call | solution.py:517
  114.5 0.9 slice_reduce_fusion.2
  115.4 1.6 reduce_sum.109
  117.0 1.9 multiply_reduce_fusion.1
  118.9 4.8 %fusion.17 = f32[512,4,768]{2,0,1:T(8,128)S(1)} fusion(bf16[4,768,768]{2,1,0:T(8,128)(2,1)} %bitcast.142, f32[512,768]{1,0:T(8,128)S(1)} %copy-done, f32[768]{0:T(1024)S(1)} %get-tuple-element.91, f32[768]{0:T(1024)S(1)} %get-tuple-element.89, f32[512]{0:T(512)S(1)} %add_rsqrt_fusion, f32[512]{0:T(512)S(1)} %broadcast_multiply_fusion.2), kind=kOutput, calls=%fused_computation.80 | convolution fusion | flops 2417885184 | bytes 12593152 | tf_op jit(solution)/shard_map/sd,tdf->stf/dot_general | solution.py:1789
  123.7 1.0 slice.128
  124.8 4.0 %fusion.8 = f32[512,768]{1,0:T(8,128)S(1)} fusion(f32[512,768]{1,0:T(8,128)S(1)} %copy-done, bf16[4,768,768]{2,1,0:T(8,128)(2,1)S(1)} %bitcast.149, f32[768]{0:T(1024)S(1)} %get-tuple-element.90, f32[512,4,768]{2,0,1:T(8,128)S(1)} %fusion.17, f32[4,768]{1,0:T(4,128)S(1)} %bitcast.130), kind=kOutput, calls=%fused_computation.23 | convolution fusion | flops 2432434176 | bytes 14171136 | tf_op jit(solution)/shard_map/stf,tdf->sd/dot_general | solution.py:1791
  128.7 1.3 slice_reduce_fusion.3
  130.8 1.5 fusion.12
  132.3 10.6 %convert_reduce_fusion = (f32[4,768]{1,0:T(4,128)S(1)}, bf16[512,4,768]{2,0,1:T(8,128)(2,1)S(1)}) fusion(bf16[512,768,1]{1,0,2:T(8,128)(2,1)S(1)} %fusion.12, bf16[4,768,768]{2,1,0:T(8,128)(2,1)} %bitcast.146, f32[512,4,768]{2,0,1:T(8,128)} %copy-done.4, f32[4,768]{1,0:T(4,128)S(1)} %bitcast.131), kind=kOutput, calls=%fused_computation.10 | convolution fusion | flops 2458383360 | bytes 14966784 | tf_op jit(solution)/shard_map/sd,tdf->stf/dot_general | solution.py:1796
  143.0 3.0 fusion.7
  146.1 3.0 fusion.6
  149.0 0.7 broadcast_in_dim.149
  149.7 1.3 concatenate.30.small_ref
  151.0 8.6 %convolution_convert_fusion.1 = bf16[4,768,768]{1,2,0:T(8,128)(2,1)} fusion(bf16[512,768,1]{1,0,2:T(8,128)(2,1)} %copy-done.3, f32[512,4,768]{2,0,1:T(8,128)} %copy-done.4, f32[4,768]{1,0:T(4,128)S(1)} %bitcast.132), kind=kOutput, calls=%fused_computation.13 | convolution fusion | flops 2434007040 | bytes 11808768 | tf_op jit(solution)/shard_map/sd,stf->tdf/dot_general | solution.py:1797
  159.6 4.6 %convolution_convert_fusion = bf16[4,768,768]{1,2,0:T(8,128)(2,1)} fusion(bf16[512,4,768]{2,0,1:T(8,128)(2,1)S(1)} %copy-done.6, f32[512,768]{1,0:T(8,128)S(1)} %copy-done, f32[768]{0:T(1024)S(1)} %get-tuple-element.91, f32[768]{0:T(1024)S(1)} %get-tuple-element.89, f32[512]{0:T(512)S(1)} %add_rsqrt_fusion, f32[512]{0:T(512)S(1)} %broadcast_multiply_fusion.2), kind=kOutput, calls=%fused_computation.12 | convolution fusion | flops 2420244480 | bytes 9447424 | tf_op jit(solution)/shard_map/sd,stf->tdf/dot_general | solution.py:1800
  164.2 145.0 %back.1 = (f32[512,768]{1,0:T(8,128)}, f32[3,96,768]{2,1,0:T(8,128)}, f32[16,768]{1,0:T(8,128)}, f32[8,768]{1,0:T(8,128)}) custom-call(bf16[512,768]{1,0:T(8,128)(2,1)} %bitcast.123, bf16[896,768]{1,0:T(8,128)(2,1)} %get-tuple-element.38.halo_ref, f32[4,8,768]{2,1,0:T(8,128)} %get-tuple-element.35.vec_ref, bf16[1408,128]{1,0:T(8,128)(2,1)} %get-tuple-element.39.kseg_ref, ...), custom_call_target="tpu_custom_call" | custom-call | tf_op jit(solution)/shard_map/back/pallas_call | solution.py:1067
  309.2 1.3 slice.131
  311.8 0.8 constant_dynamic-slice_fusion.5
  312.6 0.5 slice_bitcast_fusion.10
  313.1 2.0 slice_bitcast_fusion
  315.1 0.1 fusion.21
  315.3 0.7 pad_maximum_fusion
  316.0 0.7 slice.140
  316.8 0.1 reshape.124
  316.9 0.6 copy.56
  317.5 0.7 copy.46
  318.3 1.4 dynamic-slice_bitcast_fusion
  319.7 0.7 slice.146
  320.4 0.1 reshape.125
  320.6 0.7 copy.45
  321.3 1.1 copy.58
  (63 shorter events, 0.6 us)
Async XLA Ops:
  114.5 4.4 %copy-start = (f32[512,768]{1,0:T(8,128)S(1)}, f32[512,768]{1,0:T(8,128)}, u32[]{:S(2)}) copy-start(f32[512,768]{1,0:T(8,128)} %get-tuple-element.34) | copy-start | bytes 4718596
  117.0 7.8 %slice-start.2 = ((s8[4718592]{0:T(1024)(128)(4,1)}), s8[4194304]{0:T(1024)(128)(4,1)S(1)}, s32[]{:S(2)}) async-start(s8[4718592]{0:T(1024)(128)(4,1)} %bitcast.147), calls=%async_computation.2 | async-start | bytes 8388608
  118.9 5.9 %slice-start.3 = ((s8[4718592]{0:T(1024)(128)(4,1)}), s8[524288]{0:T(1024)(128)(4,1)S(1)}, s32[]{:S(2)}) async-start(s8[4718592]{0:T(1024)(128)(4,1)} %bitcast.147), calls=%async_computation.3 | async-start | bytes 1048576
  123.7 5.0 %copy-start.4 = (f32[512,4,768]{2,0,1:T(8,128)}, f32[512,4,768]{2,0,1:T(8,128)S(1)}, u32[]{:S(2)}) copy-start(f32[512,4,768]{2,0,1:T(8,128)S(1)} %fusion.17) | copy-start | bytes 18874372
  130.8 12.2 %slice-start = ((s8[4718592]{0:T(1024)(128)(4,1)}), s8[4194304]{0:T(1024)(128)(4,1)S(1)}, s32[]{:S(2)}) async-start(s8[4718592]{0:T(1024)(128)(4,1)} %bitcast.143), calls=%async_computation | async-start | bytes 8388608
  132.3 10.7 %copy-start.3 = (bf16[512,768,1]{1,0,2:T(8,128)(2,1)}, bf16[512,768,1]{1,0,2:T(8,128)(2,1)S(1)}, u32[]{:S(2)}) copy-start(bf16[512,768,1]{1,0,2:T(8,128)(2,1)S(1)} %fusion.12) | copy-start | bytes 2359300
  132.3 10.7 %slice-start.1 = ((s8[4718592]{0:T(1024)(128)(4,1)}), s8[524288]{0:T(1024)(128)(4,1)S(1)}, s32[]{:S(2)}) async-start(s8[4718592]{0:T(1024)(128)(4,1)} %bitcast.143), calls=%async_computation.1 | async-start | bytes 1048576
  143.0 3.1 copy-start.5
  143.0 3.0 copy-start.1
  151.0 8.6 %copy-start.6 = (bf16[512,4,768]{2,0,1:T(8,128)(2,1)S(1)}, bf16[512,4,768]{2,0,1:T(8,128)(2,1)}, u32[]{:S(2)}) copy-start(bf16[512,4,768]{2,0,1:T(8,128)(2,1)} %copy-done.5) | copy-start | bytes 9437188
  309.2 12.1 %copy-start.2 = (f32[512,768]{1,0:T(8,128)S(1)}, f32[512,768]{1,0:T(8,128)}, u32[]{:S(2)}) copy-start(f32[512,768]{1,0:T(8,128)} %get-tuple-element.50) | copy-start | bytes 4718596

commit v2 on v1

--- a/solution.py
+++ b/solution.py
@@ -17,6 +17,7 @@
 CHUNKS = ([(LEAD, KB - LEAD)] if LEAD else [(0, KB)]) + [(r, KB) for r in range(KB, HALO + QB, KB)]
 Q_SCALE = 0.125 * 1.4426950408889634
 EPSILON = 1e-05
+LAG = 2
 TANH_SLOPE = 0.7978845608028654
 CUBIC_TERM = 0.044715
 MESH = pl.DeviceIdType.MESH
@@ -283,24 +284,23 @@
     stages = len(net.far)
     parts = halo_parts(tokens, ts)
 
-    def halo_copies(i):
-        back, count = parts[i]
-        end = halo - sum(c for _, c in parts[:i])
-        pairs = [
-            (x_ref.at[pl.ds(tokens - count, count)], halo_ref.at[pl.ds(end - count, count)]),
-            (seg_ref, hseg_ref.at[i]),
-        ]
-        return [
-            pltpu.make_async_remote_copy(
-                src_ref=src,
-                dst_ref=dst,
-                send_sem=halo_send.at[2 * i + n],
-                recv_sem=halo_recv.at[2 * i + n],
-                device_id={"tensor": lax.rem(mt + back, ts)},
-                device_id_type=MESH,
-            )
-            for n, (src, dst) in enumerate(pairs)
-        ]
+    far = parts[1][1]
+    near_at, cut = halo - tokens, tokens - far
+
+    def hop(src, dst, n, back):
+        return pltpu.make_async_remote_copy(
+            src_ref=src,
+            dst_ref=dst,
+            send_sem=halo_send.at[n],
+            recv_sem=halo_recv.at[n],
+            device_id={"tensor": lax.rem(mt + back, ts)},
+            device_id_type=MESH,
+        )
+
+    late_rows = hop(x_ref.at[pl.ds(cut, far)], halo_ref.at[pl.ds(near_at + cut, far)], 0, 1)
+    early_rows = hop(x_ref.at[pl.ds(0, cut)], halo_ref.at[pl.ds(near_at, cut)], 1, 1)
+    passed_rows = hop(halo_ref.at[pl.ds(near_at + cut, far)], halo_ref.at[pl.ds(near_at - far, far)], 2, 1)
+    segs = [hop(seg_ref, hseg_ref.at[i], 3 + i, back) for i, (back, _) in enumerate(parts)]
 
     own = [
         pltpu.make_async_copy(ins[c], outs[c].at[mt, me], local_sem.at[2 * ts + c]) for c in range(4)
@@ -317,8 +317,12 @@
 
         @pl.when(mt + back < ts)
         def _():
-            for h in halo_copies(i):
-                h.start()
+            segs[i].start()
+
+    @pl.when(mt + 1 < ts)
+    def _():
+        late_rows.start()
+        early_rows.start()
 
     net.z_step(1, ts - 1)
     for i in range(stages):
@@ -326,6 +330,15 @@
             net.far_step(0, k, i)
     for k in range(ts):
         net.far_step(1, k, 0)
+
+    @pl.when(mt >= 1)
+    def _():
+        late_rows.wait_recv()
+
+    @pl.when((mt >= 1) & (mt + 1 < ts))
+    def _():
+        passed_rows.start()
+
     net.start(2)
     net.start(3)
     own[0].wait()
@@ -387,8 +400,15 @@
 
         @pl.when(mt >= back)
         def _():
-            for h in halo_copies(i):
-                h.wait_recv()
+            segs[i].wait_recv()
+
+    @pl.when(mt >= 1)
+    def _():
+        early_rows.wait_recv()
+
+    @pl.when(mt >= 2)
+    def _():
+        passed_rows.wait_recv()
 
     def halo_rows(i, carry):
         norm_rows(halo_ref, i, 0)
@@ -496,8 +516,16 @@
 
         @pl.when(mt + back < ts)
         def _():
-            for h in halo_copies(i):
-                h.wait_send()
+            segs[i].wait_send()
+
+    @pl.when(mt + 1 < ts)
+    def _():
+        late_rows.wait_send()
+        early_rows.wait_send()
+
+    @pl.when((mt >= 1) & (mt + 1 < ts))
+    def _():
+        passed_rows.wait_send()
 
     net.finish()
 
@@ -549,8 +577,8 @@
             dma((4, ts)),
             dma((copies,)),
             dma((copies,)),
-            dma((2 * n_halo,)),
-            dma((2 * n_halo,)),
+            dma((3 + n_halo,)),
+            dma((3 + n_halo,)),
         ],
         compiler_params=pltpu.CompilerParams(
             collective_id=1, has_side_effects=True, vmem_limit_bytes=62 << 20
@@ -640,7 +668,7 @@
             def _():
                 self.z_copy(c, t).start()
 
-    def final(self, c, out_ref):
+    def final(self, c):
         total = self.in_core[c, self.mt, 0].astype(F32)
         for k in range(self.ts - 1):
             pltpu.make_async_remote_copy(
@@ -652,7 +680,7 @@
                 device_id_type=MESH,
             ).wait_recv()
             total = total + self.in_z[c, k].astype(F32)
-        out_ref[c] = total
+        return total
 
     def finish(self):
         for c in range(len(self.srcs)):
@@ -716,12 +744,12 @@
         for k in range(1, self.ts):
             self.over_z(k).start()
 
-    def end(self, out_ref):
+    def end(self):
         total = self.z_in[0]
         for k in range(1, self.ts):
             self.over_z(k).wait_recv()
             total = total + self.z_in[self.ts - k]
-        out_ref[...] = total
+        return total
 
     def finish(self):
         for m in range(1, self.dp):
@@ -751,9 +779,19 @@
     g_fc,
     qkvo_all,
     input_grad_ref,
-    sums_ref,
-    small_out,
-    late_out,
+    loss_out,
+    gain_one_out,
+    bias_one_out,
+    qkv_out,
+    qv_bias_out,
+    out_out,
+    out_bias_out,
+    gain_two_out,
+    bias_two_out,
+    fc_out,
+    fc_bias_out,
+    proj_out,
+    proj_bias_out,
     w_ref,
     g_qkvo,
     low_ref,
@@ -768,6 +806,7 @@
     dkv_ref,
     give_ref,
     take_ref,
+    far_ref,
     gh_ref,
     gw_ref,
     g_local,
@@ -804,7 +843,7 @@
     early = Total(dp, ts, small_ref, small_in, small_z, small_send, small_recv)
     late = Total(dp, ts, late_own, late_in, late_z, late_send, late_recv)
     stages = len(net.far) + 1
-    zigzag = [t for pair in zip(range(ts // 2), range(ts // 2, ts)) for t in pair]
+    zigzag = [t for pair in zip(range(ts // 2), range(ts - 1, ts // 2 - 1, -1)) for t in pair]
     for c in (0, 1):
         for t in zigzag:
             net.start(c, t)
@@ -833,26 +872,90 @@
     gw_ref[...] = jnp.zeros_like(gw_ref)
     gh_ref[...] = jnp.zeros_like(gh_ref)
 
-    plan = {5: ["turn"], 9: ["end"]}
+    turns = pairs + LAG
+    order = list(range(ts, pairs)) + zigzag
+
+    def pair_of(n):
+        p = jnp.int32(order[0])
+        for i in range(1, pairs):
+            p = jnp.where(n == i, order[i], p)
+        return p
+
+    last = 4 * turns
+    plan = {5: ["turn"], 9: ["end"], 4 * pairs + 3: ["final0", "final1"]}
     units = [(c, t) for c in (0, 1) for t in zigzag]
     for n, (c, t) in enumerate(units):
         for s in range(stages):
             plan.setdefault(2 * n + 1 + 3 * s, []).append((c, t, s))
-    plan.setdefault(4 * pairs, []).extend(["final0", "final1"])
-    for t in range(ts):
-        at = 4 * pairs + pairs - ts + t
-        plan.setdefault(at, []).append((2, t, "start"))
+
+    def after(slot):
+        slot += 2
+        return slot if slot < 4 * pairs else -(-(slot - 3) // 4) * 4 + 3 if slot < last else slot
+
+    for i, t in enumerate(zigzag):
+        at = 4 * (pairs - ts + i + LAG) + 3
+        plan.setdefault(at, []).insert(0, (2, t, "start"))
         for s in range(stages):
-            plan.setdefault(at + 1 + s, []).append((2, t, s))
+            at = after(at) if at < last - 1 else max(at, last - 1) + 1
+            plan.setdefault(at, []).append((2, t, s))
+
+    def turned(block):
+        pad = jnp.zeros((128 - block.shape[0], 128), F32)
+        return jnp.concatenate([block, pad], axis=0).T[:, : block.shape[0]]
+
+    def write_final(c):
+        total = net.final(c)
+        if c == 0:
+            proj_out[...] = total
+        elif c == 1:
+            fc_out[...] = total
+        else:
+            for i in range(3):
+                qkv_out[i, :, 0:128] = total[:, i * 128 : (i + 1) * 128]
+                qkv_out[i, :, 128:192] = total[:, 512 + i * HD : 512 + (i + 1) * HD]
+            out_out[0:128, :] = turned(total[:, 384:512])
+            out_out[128:192, :] = turned(total[:, 640:768])[HD:, :]
+
+    def at_lane(block, lane):
+        return pltpu.roll(block, lax.rem(width - lane, width), 1)
+
+    def write_small(block):
+        rows = at_lane(block[0:8, :], me * (width // dp))
+        for i, ref in enumerate((out_bias_out, gain_two_out, bias_two_out, proj_bias_out)):
+            ref[...] = rows[i : i + 1, : width // dp]
+        mine = block[4:5, :]
+        for t in range(1, ts):
+            mine = jnp.where(mt == t, block[4 + t : 5 + t, :], mine)
+        mine = at_lane(jnp.broadcast_to(mine, (8, width)), me * (HD // dp))
+        for i in range(width // HD):
+            fc_bias_out[i : i + 1, :] = mine[0:1, i * HD : i * HD + HD // dp]
+        count = vec_ref[0, 7:8, 384:385]
+        for t in range(1, ts):
+            count = count + vec_ref[t, 7:8, 384:385]
+        loss_out[...] = block[4 + ts : 5 + ts, 0:1] / (width * count)
+
+    def write_late(block):
+        rows = at_lane(block, me * (width // dp))
+        gain_one_out[...] = rows[0:1, : width // dp]
+        bias_one_out[...] = rows[1:2, : width // dp]
+        rows = at_lane(block, me * (HD // dp))
+        for h in range(3):
+            for i in range(2):
+                value = None
+                for t in range(ts):
+                    lane = t * 128 + h * HD if h < 2 else ts * 128 + t * HD
+                    here = rows[2 + i : 3 + i, lane : lane + HD // dp]
+                    value = here if value is None else jnp.where(mt == t, here, value)
+                qv_bias_out[h, i : i + 1, :] = value
 
     def run(items):
         for item in items:
             if item == "turn":
                 early.turn()
             elif item == "end":
-                early.end(small_out)
+                write_small(early.end())
             elif item in ("final0", "final1"):
-                net.final(int(item[-1]), sums_ref)
+                write_final(int(item[-1]))
             elif item[2] == "start":
                 net.start(item[0], item[1])
             else:
@@ -860,26 +963,31 @@
 
     def steps_at(n, place):
         for slot, items in sorted(plan.items()):
-            if slot % 4 == place and slot < 4 * pairs:
+            if slot % 4 == place and slot < (last if place == 3 else 4 * pairs):
 
                 @pl.when(n == slot // 4)
                 def _():
                     run(items)
 
-    def give(i):
-        back, count = parts[i]
-        end = halo - sum(c for _, c in parts[:i])
+    far = parts[1][1]
+    near_at, cut = halo - tokens, tokens - far
+
+    def hop(src, dst, n):
         return pltpu.make_async_remote_copy(
-            src_ref=give_ref.at[pl.ds(end - count, count)],
-            dst_ref=take_ref.at[pl.ds(end - count, count)],
-            send_sem=halo_send.at[i],
-            recv_sem=halo_recv.at[i],
-            device_id={"tensor": lax.rem(mt + ts - back, ts)},
+            src_ref=src,
+            dst_ref=dst,
+            send_sem=halo_send.at[n],
+            recv_sem=halo_recv.at[n],
+            device_id={"tensor": lax.rem(mt + ts - 1, ts)},
             device_id_type=MESH,
         )
 
-    def attend_back(n, carry):
-        p = lax.rem(n + ts, pairs)
+    far_rows = hop(give_ref.at[pl.ds(near_at - far, far)], far_ref, 0)
+    early_rows = hop(give_ref.at[pl.ds(near_at, cut)], take_ref.at[pl.ds(0, cut)], 1)
+    late_rows = hop(give_ref.at[pl.ds(near_at + cut, far)], take_ref.at[pl.ds(cut, far)], 2)
+
+    def attend_back(n):
+        p = pair_of(n)
         cols = pl.ds(pl.multiple_of(p * 128, 128), 128)
         w_o = w_ref[p, :, :, 384:512].reshape(width, 128)
         rounded = mm(low_ref[...], w_o).astype(BF16)
@@ -950,14 +1058,24 @@
             return c
 
         lax.fori_loop(0, 2, halo_grad, 0)
-        steps_at(n, 3)
-        return carry
+
+        @pl.when(n == pairs - 1)
+        def _():
+            give_ref[: near_at + cut, :] = gh_ref[: near_at + cut, :].astype(BF16)
+
+            @pl.when(mt >= 2)
+            def _():
+                far_rows.start()
+
+            @pl.when(mt >= 1)
+            def _():
+                early_rows.start()
 
     def store(tile, value, t):
         g_qkvo[t, :, :, tile * 128 : (tile + 1) * 128] = value.astype(BF16).reshape(dp, -1, 128)
 
-    def weights_back(n, carry):
-        p = lax.rem(n + ts, pairs)
+    def weights_back(n):
+        p = pair_of(n)
         cols = pl.ds(pl.multiple_of(p * 128, 128), 128)
         grad_o = mm(low_t_ref[...], mixed_ref[:, cols])
         dqkv = dqkv_ref[n]
@@ -983,21 +1101,20 @@
         grad_v = jnp.sum(dqkv[:, 256:384].astype(F32), axis=0, keepdims=True)
         late_own[2:3, cols] = jnp.sum(dqkv[:, 0:128].astype(F32), axis=0, keepdims=True)
         late_own[3:4, cols] = grad_v + jnp.sum(dkv_ref[n, :, 128:256].astype(F32), axis=0, keepdims=True)
-        for slot, items in sorted(plan.items()):
-            if 4 * pairs <= slot < 5 * pairs:
-
-                @pl.when(n == slot - 4 * pairs)
-                def _():
-                    run(items)
+
+    def one_turn(n, carry):
+        @pl.when(n < pairs)
+        def _():
+            attend_back(n)
+
+        @pl.when(n >= LAG)
+        def _():
+            weights_back(n - LAG)
+
+        steps_at(n, 3)
         return carry
 
-    lax.fori_loop(0, pairs, attend_back, 0)
-    give_ref[...] = gh_ref[...].astype(BF16)
-    for i, (back, _) in enumerate(parts):
-
-        @pl.when(mt >= back)
-        def _():
-            give(i).start()
+    lax.fori_loop(0, turns, one_turn, 0)
 
     def halo_sums(i, carry):
         rows = pl.ds(pl.multiple_of(i * KB, KB), KB)
@@ -1013,23 +1130,36 @@
 
     zero = jnp.zeros((8, width), F32)
     carry = lax.fori_loop(0, halo // KB, halo_sums, (zero, zero))
-    lax.fori_loop(0, pairs, weights_back, 0)
-    tail = [items for slot, items in sorted(plan.items()) if slot >= 5 * pairs]
-    run(tail[0])
+    passed = (mt >= 1) & (mt + 1 < ts)
+
+    @pl.when(passed)
+    def _():
+        far_rows.wait_recv()
+        gh_ref[near_at + cut :, :] += far_ref[...].astype(F32)
+
+    @pl.when(mt >= 1)
+    def _():
+        give_ref[near_at + cut :, :] = gh_ref[near_at + cut :, :].astype(BF16)
+        late_rows.start()
+
+    tail = [item for slot, items in sorted(plan.items()) if slot >= last for item in items]
+    first = [item for item in tail if item[2] == 0] + [item for item in tail if item[1] == zigzag[-3]]
+    tail = [item for item in tail if item not in first]
+    run(first)
     gains, shifts = lax.fori_loop(0, tokens // KB, own_sums, carry)
     late_own[0:1, :] = jnp.sum(gains, axis=0, keepdims=True)
     late_own[1:2, :] = jnp.sum(shifts, axis=0, keepdims=True)
     late.start()
-    for items in tail[1:]:
-        run(items)
+    tail.sort(key=lambda item: (item[2], -zigzag.index(item[1])))
+    run(tail[:1])
     late.turn()
-    for i, (back, count) in enumerate(parts):
-
-        @pl.when(mt + back < ts)
-        def _():
-            give(i).wait_recv()
-            end = halo - sum(c for _, c in parts[:i])
-            gw_ref[tokens - count :, :] += take_ref[end - count : end, :].astype(F32)
+    run(tail[1:])
+
+    @pl.when(mt + 1 < ts)
+    def _():
+        early_rows.wait_recv()
+        late_rows.wait_recv()
+        gw_ref[...] += take_ref[...].astype(F32)
 
     def own_grad(i, carry):
         rows = pl.ds(pl.multiple_of(i * KB, KB), KB)
@@ -1039,15 +1169,19 @@
         return carry
 
     lax.fori_loop(0, tokens // KB, own_grad, 0)
-    late.end(late_out)
-    net.final(2, sums_ref)
+    write_late(late.end())
+    write_final(2)
     early.finish()
     late.finish()
-    for i, (back, _) in enumerate(parts):
-
-        @pl.when(mt >= back)
-        def _():
-            give(i).wait_send()
+
+    @pl.when(mt >= 2)
+    def _():
+        far_rows.wait_send()
+
+    @pl.when(mt >= 1)
+    def _():
+        early_rows.wait_send()
+        late_rows.wait_send()
 
     net.finish()
 
@@ -1058,7 +1192,6 @@
     window = halo + tokens
     ts, dp, rows = qkvo_all.shape[:3]
     pairs = width // 128
-    n_halo = len(halo_parts(tokens, ts))
     n_far = dp // 2 - 1
     any_spec = pl.BlockSpec(memory_space=pl.ANY)
     vmem = pl.BlockSpec(memory_space=pltpu.VMEM)
@@ -1066,9 +1199,24 @@
     dma = pltpu.SemaphoreType.DMA
     return pl.pallas_call(
         functools.partial(back_kernel, dp, ts),
-        out_shape=[s((tokens, width), F32), s((3, rows, width), F32), s(small.shape, F32), s((8, width), F32)],
+        out_shape=[
+            s((tokens, width), F32),
+            s((1, 1), F32),
+            s((1, rows), F32),
+            s((1, rows), F32),
+            s((3, rows, 3 * HD), F32),
+            s((3, 2, HD // dp), F32),
+            s((3 * HD, rows), F32),
+            s((1, rows), F32),
+            s((1, rows), F32),
+            s((1, rows), F32),
+            s((rows, width), F32),
+            s((width // HD, HD // dp), F32),
+            s((rows, width), F32),
+            s((1, rows), F32),
+        ],
         in_specs=[vmem] * 14 + [any_spec] * 3,
-        out_specs=[vmem] * 4,
+        out_specs=[vmem] * 14,
         scratch_shapes=[
             pltpu.VMEM((pairs, dp, rows, 512), BF16),
             pltpu.VMEM((ts, dp, rows, width), BF16),
@@ -1083,7 +1231,8 @@
             pltpu.VMEM((pairs, tokens, 384), BF16),
             pltpu.VMEM((pairs, halo, 256), BF16),
             pltpu.VMEM((halo, width), BF16),
-            pltpu.VMEM((halo, width), BF16),
+            pltpu.VMEM((tokens, width), BF16),
+            pltpu.VMEM((halo_parts(tokens, ts)[1][1], width), BF16),
             pltpu.VMEM((halo, width), F32),
             pltpu.VMEM((tokens, width), F32),
             pltpu.VMEM((2, ts, dp // 2, rows, width), BF16),
@@ -1102,8 +1251,8 @@
             dma((3, ts, n_far)),
             dma((3, ts)),
             dma((3, ts - 1)),
-            dma((n_halo,)),
-            dma((n_halo,)),
+            dma((3,)),
+            dma((3,)),
             dma((dp + ts,)),
             dma((dp + ts,)),
             dma((dp + ts,)),
@@ -1812,43 +1961,28 @@
         ]
     )
     blocks = lambda g: g.astype(BF16).reshape(ts, dp // 2, 2, width // dp, width)
-    input_grad, sums, small_sums, late_sums = back(
+    grads = back(
         x, halo_x, vec, kseg, qseg, normed_t, q, k, v, ot, lse, mixed, grad_hidden, small_grads,
         blocks(grad_proj_w), blocks(grad_fc_w), qkvo_all,
     )
-    r_proj, r_fc, r_qkvo = sums
-    own = lambda a: lax.dynamic_slice_in_dim(a, me * (width // dp), width // dp, 1)
-    own_late, own_small = own(late_sums), own(small_sums)
-    fc_b = small_sums[4 : 4 + ts].reshape(ts, -1, dp, fc_bias.shape[1])
-    fc_b = lax.dynamic_index_in_dim(lax.dynamic_index_in_dim(fc_b, mt, 0, False), me, 1, False)
-
-    def by_head(v):
-        low = lax.dynamic_slice_in_dim(v, mt * 2 * HD, 2 * HD, 1)
-        last = lax.dynamic_slice_in_dim(v, ts * 2 * HD + mt * HD, HD, 1)
-        v = jnp.concatenate([low, last], axis=1).reshape(2, -1, dp, qv_bias.shape[2])
-        return lax.dynamic_index_in_dim(v, me, 2, False)
-
-    def columns(i):
-        return jnp.concatenate(
-            [r_qkvo[:, i * 128 : (i + 1) * 128], r_qkvo[:, 512 + i * HD : 512 + (i + 1) * HD]], axis=1
-        )
-
+    input_grad, loss, gain_one, bias_one, g_qkv, g_qv_bias, g_out, *others = grads
+    out_bias_, gain_two_, bias_two_, g_fc, g_fc_bias, g_proj, proj_bias_ = others
     return (
         output.astype(BF16)[None],
-        small_sums[4 + ts, 0] / (width * valid_count),
+        loss[0, 0],
         input_grad[None],
-        own_late[0],
-        own_late[1],
-        jnp.stack([columns(i) for i in range(3)]),
-        by_head(late_sums[2:4]),
-        columns(3).T,
-        own_small[0],
-        own_small[1],
-        own_small[2],
-        r_fc,
-        fc_b,
-        r_proj.T,
-        own_small[3],
+        gain_one[0],
+        bias_one[0],
+        g_qkv,
+        g_qv_bias.transpose(1, 0, 2),
+        g_out,
+        out_bias_[0],
+        gain_two_[0],
+        bias_two_[0],
+        g_fc,
+        g_fc_bias,
+        g_proj.T,
+        proj_bias_[0],
     )
 
 
@@ -1874,7 +2008,8 @@
     def fits(qkv_weight, block_input):
         rows = block_input.shape[2] // mesh.shape["dp"]
         wide = qkv_weight.shape[2] // mesh.shape["tensor"]
-        return rows % 16 == 0 and wide == 3 * HD and mesh.shape["tensor"] % 2 == 0
+        parts = halo_parts(block_input.shape[1] // mesh.shape["tensor"], mesh.shape["tensor"])
+        return rows % 16 == 0 and wide == 3 * HD and mesh.shape["tensor"] % 2 == 0 and len(parts) == 2
 
     def step(*args):
         return placed_step(on_device if fits(args[6], args[0]) else plain_device)(*args)

time: 327 us -> 310 us (0.948)
  Pallas kernels: 249 us -> 234 us
    pallas_call x1, Pallas kernels: 145 us -> 134 us  [back(): pl.pallas_call(functools.partial(back_kernel, dp, ts), out_shape=[s((toke...]
    unnamed x29 -> x59, local copies, waits for them, and re-layouts: 4.85 us -> 12.9 us
    pallas_call x1, Pallas kernels: 104 us -> 100 us  [front(): pl.pallas_call(functools.partial(front_kernel, dp, ts), out_shape=[big, b...]
where the time goes in v2:
time: 310 us; the launch traced here: 307 us
  Pallas kernels  234 us (75%)
  matrix products  35.8 us (12%)
  local copies, waits for them, and re-layouts  21.9 us (7%)
  other arithmetic  12 us (4%)
  between operations  3.63 us (1%)
    pallas_call x1, Pallas kernels, back(): pl.pallas_call(functools.partial(back_kernel, dp, ts), out_shape=[s((toke...  134 us
    pallas_call x1, Pallas kernels, front(): pl.pallas_call(functools.partial(front_kernel, dp, ts), out_shape=[big, b...  100 us
    unnamed x59, local copies, waits for them, and re-layouts  12.9 us
    dot_general x1, matrix products, on_device(): jnp.einsum('sd,tdf->stf', low_output, wp, preferred_element_type=F32)  10.7 us
    dot_general x1, matrix products, on_device(): jnp.einsum('sd,stf->tdf', low_output, activated, preferred_element_type=F32)  8.57 us

profile of v2, /device:TPU:0, one launch (start us, length us, event | category | flops | bytes accessed | tf_op | source)
XLA Modules:
  0.0 307.3 jit_solution(8756859419262218992)
XLA Ops:
  0.6 0.7 convert_element_type.71
  1.3 1.3 broadcast_in_dim.125.seg_ref
  2.6 0.7 copy.38
  3.3 0.1 broadcast_in_dim.139
  3.4 0.1 broadcast_in_dim.135
  3.5 0.1 broadcast_in_dim.136
  3.6 1.3 convert_reduce_fusion.1
  4.9 0.7 concatenate.12
  5.7 0.8 copy.37
  6.4 0.1 select_convert_fusion
  6.5 0.1 reshape.116
  6.6 0.8 stack.27
  7.4 0.1 broadcast_in_dim.130
  7.5 0.1 broadcast_in_dim.127
  7.6 0.6 pad_maximum_fusion.small_ref
  8.3 0.9 slice_bitcast_fusion
  9.2 0.9 copy.39
  10.1 0.8 concatenate.14.qkvo_ref
  10.9 100.0 %front.1 = (bf16[4,8,96,768]{3,2,1,0:T(8,128)(2,1)}, bf16[4,8,96,768]{3,2,1,0:T(8,128)(2,1)}, bf16[4,8,96,768]{3,2,1,0:T(8,128)(2,1)}, f32[4,8,768]{2,1,0:T(8,12...) custom-call(bf16[512,768]{1,0:T(8,128)(2,1)} %bitcast.98, ...), custom_call_target="tpu_custom_call" | custom-call | tf_op jit(solution)/shard_map/front/pallas_call | solution.py:545
  110.9 0.9 slice_reduce_fusion.2
  111.8 1.6 reduce_sum.109
  113.4 1.9 multiply_reduce_fusion.1
  115.3 4.9 %fusion.16 = f32[512,4,768]{2,0,1:T(8,128)S(1)} fusion(bf16[4,768,768]{2,1,0:T(8,128)(2,1)} %bitcast.118, f32[512,768]{1,0:T(8,128)S(1)} %copy-done, f32[768]{0:T(1024)S(1)} %get-tuple-element.111, f32[768]{0:T(1024)S(1)} %get-tuple-element.109, f32[512]{0:T(512)S(1)} %add_rsqrt_fusion, f32[512]{0:T(512)S(1)} %broadcast_multiply_fusion.2), kind=kOutput, calls=%fused_computation.58 | convolution fusion | flops 2417885184 | bytes 12593152 | tf_op jit(solution)/shard_map/sd,tdf->stf/dot_general | solution.py:1938
  120.1 1.0 slice.77
  121.2 4.0 %fusion.8 = f32[512,768]{1,0:T(8,128)S(1)} fusion(f32[512,768]{1,0:T(8,128)S(1)} %copy-done, bf16[4,768,768]{2,1,0:T(8,128)(2,1)S(1)} %bitcast.125, f32[768]{0:T(1024)S(1)} %get-tuple-element.110, f32[512,4,768]{2,0,1:T(8,128)S(1)} %fusion.16, f32[4,768]{1,0:T(4,128)S(1)} %bitcast.107), kind=kOutput, calls=%fused_computation.23 | convolution fusion | flops 2432434176 | bytes 14171136 | tf_op jit(solution)/shard_map/stf,tdf->sd/dot_general | solution.py:1940
  125.2 1.3 slice_reduce_fusion.3
  127.2 1.6 fusion.12
  128.8 10.7 %convert_reduce_fusion = (f32[4,768]{1,0:T(4,128)S(1)}, bf16[512,4,768]{2,0,1:T(8,128)(2,1)S(1)}) fusion(bf16[512,768,1]{1,0,2:T(8,128)(2,1)S(1)} %fusion.12, bf16[4,768,768]{2,1,0:T(8,128)(2,1)} %bitcast.122, f32[512,4,768]{2,0,1:T(8,128)} %copy-done.14, f32[4,768]{1,0:T(4,128)S(1)} %bitcast.108), kind=kOutput, calls=%fused_computation.10 | convolution fusion | flops 2458383360 | bytes 14966784 | tf_op jit(solution)/shard_map/sd,tdf->stf/dot_general | solution.py:1945
  139.6 3.0 fusion.7
  142.6 2.9 fusion.6
  145.6 0.7 broadcast_in_dim.149
  146.3 1.3 concatenate.15.small_ref
  147.5 8.6 %convolution_convert_fusion.1 = bf16[4,768,768]{1,2,0:T(8,128)(2,1)} fusion(bf16[512,768,1]{1,0,2:T(8,128)(2,1)} %copy-done.2, f32[512,4,768]{2,0,1:T(8,128)} %copy-done.14, f32[4,768]{1,0:T(4,128)S(1)} %bitcast.109), kind=kOutput, calls=%fused_computation.13 | convolution fusion | flops 2434007040 | bytes 11808768 | tf_op jit(solution)/shard_map/sd,stf->tdf/dot_general | solution.py:1946
  156.1 4.7 %convolution_convert_fusion = bf16[4,768,768]{1,2,0:T(8,128)(2,1)} fusion(bf16[512,4,768]{2,0,1:T(8,128)(2,1)S(1)} %copy-done.16, f32[512,768]{1,0:T(8,128)S(1)} %copy-done, f32[768]{0:T(1024)S(1)} %get-tuple-element.111, f32[768]{0:T(1024)S(1)} %get-tuple-element.109, f32[512]{0:T(512)S(1)} %add_rsqrt_fusion, f32[512]{0:T(512)S(1)} %broadcast_multiply_fusion.2), kind=kOutput, calls=%fused_computation.12 | convolution fusion | flops 2420244480 | bytes 9447424 | tf_op jit(solution)/shard_map/sd,stf->tdf/dot_general | solution.py:1949
  160.8 134.0 %back.1 = (f32[512,768]{1,0:T(8,128)}, f32[1,1]{1,0:T(1,128)}, f32[1,96]{1,0:T(1,128)}, f32[1,96]{1,0:T(1,128)}, f32[3,96,192]{2,1,0:T(8,128)}, /*index=5*/f32[3...) custom-call(bf16[512,768]{1,0:T(8,128)(2,1)} %bitcast.99, ...), custom_call_target="tpu_custom_call" | custom-call | tf_op jit(solution)/shard_map/back/pallas_call | solution.py:1200
  294.9 1.4 copy.42
  297.1 2.7 copy.64
  299.7 0.5 copy.65
  300.2 0.5 copy.66
  300.7 0.7 copy.67
  301.5 0.6 copy.68
  302.0 0.6 copy.69
  302.7 0.5 copy.70
  303.2 0.5 copy.71
  303.7 0.5 copy.72
  304.2 0.7 copy.73
  304.9 0.7 copy.74
  305.7 0.5 copy.75
  (71 shorter events, 0.3 us)
Async XLA Ops:
  110.9 4.4 %copy-start = (f32[512,768]{1,0:T(8,128)S(1)}, f32[512,768]{1,0:T(8,128)}, u32[]{:S(2)}) copy-start(f32[512,768]{1,0:T(8,128)} %get-tuple-element.44) | copy-start | bytes 4718596
  113.4 7.8 %slice-start.2 = ((s8[4718592]{0:T(1024)(128)(4,1)}), s8[4194304]{0:T(1024)(128)(4,1)S(1)}, s32[]{:S(2)}) async-start(s8[4718592]{0:T(1024)(128)(4,1)} %bitcast.123), calls=%async_computation.2 | async-start | bytes 8388608
  115.2 5.9 %slice-start.3 = ((s8[4718592]{0:T(1024)(128)(4,1)}), s8[524288]{0:T(1024)(128)(4,1)S(1)}, s32[]{:S(2)}) async-start(s8[4718592]{0:T(1024)(128)(4,1)} %bitcast.123), calls=%async_computation.3 | async-start | bytes 1048576
  120.1 5.0 %copy-start.14 = (f32[512,4,768]{2,0,1:T(8,128)}, f32[512,4,768]{2,0,1:T(8,128)S(1)}, u32[]{:S(2)}) copy-start(f32[512,4,768]{2,0,1:T(8,128)S(1)} %fusion.16) | copy-start | bytes 18874372
  127.2 12.4 %slice-start = ((s8[4718592]{0:T(1024)(128)(4,1)}), s8[4194304]{0:T(1024)(128)(4,1)S(1)}, s32[]{:S(2)}) async-start(s8[4718592]{0:T(1024)(128)(4,1)} %bitcast.119), calls=%async_computation | async-start | bytes 8388608
  128.8 10.8 %copy-start.2 = (bf16[512,768,1]{1,0,2:T(8,128)(2,1)}, bf16[512,768,1]{1,0,2:T(8,128)(2,1)S(1)}, u32[]{:S(2)}) copy-start(bf16[512,768,1]{1,0,2:T(8,128)(2,1)S(1)} %fusion.12) | copy-start | bytes 2359300
  128.8 10.8 %slice-start.1 = ((s8[4718592]{0:T(1024)(128)(4,1)}), s8[524288]{0:T(1024)(128)(4,1)S(1)}, s32[]{:S(2)}) async-start(s8[4718592]{0:T(1024)(128)(4,1)} %bitcast.119), calls=%async_computation.1 | async-start | bytes 1048576
  139.5 3.1 copy-start.15
  139.6 3.1 copy-start.1
  147.5 8.6 %copy-start.16 = (bf16[512,4,768]{2,0,1:T(8,128)(2,1)S(1)}, bf16[512,4,768]{2,0,1:T(8,128)(2,1)}, u32[]{:S(2)}) copy-start(bf16[512,4,768]{2,0,1:T(8,128)(2,1)} %copy-done.15) | copy-start | bytes 9437188
  294.8 4.9 %copy-start.13 = (f32[1,96]{1,0:T(1,128)S(1)}, f32[1,96]{1,0:T(1,128)}, u32[]{:S(2)}) copy-start(f32[1,96]{1,0:T(1,128)} %get-tuple-element.61) | copy-start | bytes 1156
  294.8 5.4 %copy-start.12 = (f32[1,96]{1,0:T(1,128)S(1)}, f32[1,96]{1,0:T(1,128)}, u32[]{:S(2)}) copy-start(f32[1,96]{1,0:T(1,128)} %get-tuple-element.62) | copy-start | bytes 1156
  294.8 5.9 %copy-start.5 = (f32[3,96,192]{2,1,0:T(8,128)S(1)}, f32[3,96,192]{2,1,0:T(8,128)}, u32[]{:S(2)}) copy-start(f32[3,96,192]{2,1,0:T(8,128)} %get-tuple-element.149) | copy-start | bytes 663556
  294.8 6.6 %copy-start.7 = (f32[3,2,8]{2,1,0:T(2,128)S(1)}, f32[3,2,8]{2,1,0:T(2,128)}, u32[]{:S(2)}) copy-start(f32[3,2,8]{2,1,0:T(2,128)} %get-tuple-element.64) | copy-start | bytes 580
  294.9 7.2 %copy-start.6 = (f32[192,96]{1,0:T(8,128)S(1)}, f32[192,96]{1,0:T(8,128)}, u32[]{:S(2)}) copy-start(f32[192,96]{1,0:T(8,128)} %get-tuple-element.151) | copy-start | bytes 221188
  294.9 7.8 %copy-start.11 = (f32[1,96]{1,0:T(1,128)S(1)}, f32[1,96]{1,0:T(1,128)}, u32[]{:S(2)}) copy-start(f32[1,96]{1,0:T(1,128)} %get-tuple-element.66) | copy-start | bytes 1156
  294.9 8.3 %copy-start.10 = (f32[1,96]{1,0:T(1,128)S(1)}, f32[1,96]{1,0:T(1,128)}, u32[]{:S(2)}) copy-start(f32[1,96]{1,0:T(1,128)} %get-tuple-element.67) | copy-start | bytes 1156
  294.9 8.8 %copy-start.9 = (f32[1,96]{1,0:T(1,128)S(1)}, f32[1,96]{1,0:T(1,128)}, u32[]{:S(2)}) copy-start(f32[1,96]{1,0:T(1,128)} %get-tuple-element.68) | copy-start | bytes 1156
  294.9 9.3 %copy-start.4 = (f32[96,768]{1,0:T(8,128)S(1)}, f32[96,768]{1,0:T(8,128)}, u32[]{:S(2)}) copy-start(f32[96,768]{1,0:T(8,128)} %get-tuple-element.155) | copy-start | bytes 884740
  294.9 10.0 %copy-start.3 = (f32[96,768]{1,0:T(8,128)S(1)}, f32[96,768]{1,0:T(8,128)}, u32[]{:S(2)}) copy-start(f32[96,768]{1,0:T(8,128)} %get-tuple-element.71) | copy-start | bytes 884740
  294.9 10.7 %copy-start.8 = (f32[1,96]{1,0:T(1,128)S(1)}, f32[1,96]{1,0:T(1,128)}, u32[]{:S(2)}) copy-start(f32[1,96]{1,0:T(1,128)} %get-tuple-element.72) | copy-start | bytes 1156

commit v3 on v2

--- a/solution.py
+++ b/solution.py
@@ -311,7 +311,7 @@
         c.start()
     for k in range(1, ts):
         net.z_step(0, k)
-    for k in range(1, ts - 1):
+    for k in range(1, ts):
         net.z_step(1, k)
     for i, (back, _) in enumerate(parts):
 
@@ -324,7 +324,6 @@
         late_rows.start()
         early_rows.start()
 
-    net.z_step(1, ts - 1)
     for i in range(stages):
         for k in range(ts):
             net.far_step(0, k, i)
@@ -567,7 +566,7 @@
             pltpu.VMEM((ts, dp, 8, width), F32),
             pltpu.VMEM((pairs, dp, rows, 512), BF16),
             pltpu.VMEM((ts, dp, rows, 256), BF16),
-            pltpu.VMEM((n_halo, 8, tokens), jnp.int32),
+            pltpu.VMEM((n_halo, 1, tokens), jnp.int32),
             pltpu.VMEM((window, width), BF16),
             pltpu.VMEM((2, window, 128), BF16),
             pltpu.VMEM((128, window), BF16),
@@ -1923,9 +1922,8 @@
             )[None],
         ]
     )
-    seg_rows = jnp.broadcast_to(segment_ids, (8, tokens))
     qkvo_all, w_fc, w_proj, vec, kseg, qseg, normed_t, halo_x, q, k, v, ot, lse, mixed, hidden = front(
-        x, seg_rows, small, qkvo, fc_weight, proj_weight.T, dp, ts, HALO
+        x, segment_ids, small, qkvo, fc_weight, proj_weight.T, dp, ts, HALO
     )
     gain_two, bias_two, b_proj = [vec[0, i] for i in (3, 4, 5)]
     b_fc = vec[:, 6]

time: 310 us -> 296 us (0.955)
  Pallas kernels: 234 us -> 221 us
    pallas_call x1, Pallas kernels: 134 us -> 123 us  [back(): pl.pallas_call(functools.partial(back_kernel, dp, ts), out_shape=[s((toke...]
where the time goes in v3:
time: 296 us; the launch traced here: 293 us
  Pallas kernels  221 us (75%)
  matrix products  35.8 us (12%)
  local copies, waits for them, and re-layouts  20.6 us (7%)
  other arithmetic  12 us (4%)
  between operations  3.63 us (1%)
    pallas_call x1, Pallas kernels, back(): pl.pallas_call(functools.partial(back_kernel, dp, ts), out_shape=[s((toke...  123 us
    pallas_call x1, Pallas kernels, front(): pl.pallas_call(functools.partial(front_kernel, dp, ts), out_shape=[big, b...  98.8 us
    unnamed x59, local copies, waits for them, and re-layouts  12.9 us
    dot_general x1, matrix products, on_device(): jnp.einsum('sd,tdf->stf', low_output, wp, preferred_element_type=F32)  10.7 us
    dot_general x1, matrix products, on_device(): jnp.einsum('sd,stf->tdf', low_output, activated, preferred_element_type=F32)  8.57 us

profile of v3, /device:TPU:0, one launch (start us, length us, event | category | flops | bytes accessed | tf_op | source)
XLA Modules:
  0.0 293.4 jit_solution(13332177435593760765)
XLA Ops:
  0.6 0.7 convert_element_type.71
  1.3 0.7 copy.38
  2.0 0.1 broadcast_in_dim.130
  2.1 0.1 broadcast_in_dim.126
  2.2 0.1 broadcast_in_dim.127
  2.3 1.3 convert_reduce_fusion.1
  3.6 0.7 concatenate.12
  4.4 0.8 copy.37
  5.1 0.1 select_convert_fusion
  5.2 0.1 reshape.116
  5.3 0.8 stack.27
  6.1 0.1 broadcast_in_dim.121
  6.2 0.1 broadcast_in_dim.117
  6.3 0.1 broadcast_in_dim.118
  6.4 0.6 pad_maximum_fusion.small_ref
  7.0 0.9 slice_bitcast_fusion
  7.9 0.9 copy.39
  8.8 0.8 concatenate.14.qkvo_ref
  9.6 98.8 %front.1 = (bf16[4,8,96,768]{3,2,1,0:T(8,128)(2,1)}, bf16[4,8,96,768]{3,2,1,0:T(8,128)(2,1)}, bf16[4,8,96,768]{3,2,1,0:T(8,128)(2,1)}, f32[4,8,768]{2,1,0:T(8,12...) custom-call(bf16[512,768]{1,0:T(8,128)(2,1)} %bitcast.97, ...), custom_call_target="tpu_custom_call" | custom-call | tf_op jit(solution)/shard_map/front/pallas_call | solution.py:544
  108.4 0.9 slice_reduce_fusion.2
  109.3 1.6 reduce_sum.109
  110.9 1.9 multiply_reduce_fusion.1
  112.8 4.9 %fusion.16 = f32[512,4,768]{2,0,1:T(8,128)S(1)} fusion(bf16[4,768,768]{2,1,0:T(8,128)(2,1)} %bitcast.116, f32[512,768]{1,0:T(8,128)S(1)} %copy-done, f32[768]{0:T(1024)S(1)} %get-tuple-element.111, f32[768]{0:T(1024)S(1)} %get-tuple-element.109, f32[512]{0:T(512)S(1)} %add_rsqrt_fusion, f32[512]{0:T(512)S(1)} %broadcast_multiply_fusion.2), kind=kOutput, calls=%fused_computation.58 | convolution fusion | flops 2417885184 | bytes 12593152 | tf_op jit(solution)/shard_map/sd,tdf->stf/dot_general | solution.py:1936
  117.7 1.0 slice.77
  118.7 4.0 %fusion.8 = f32[512,768]{1,0:T(8,128)S(1)} fusion(f32[512,768]{1,0:T(8,128)S(1)} %copy-done, bf16[4,768,768]{2,1,0:T(8,128)(2,1)S(1)} %bitcast.123, f32[768]{0:T(1024)S(1)} %get-tuple-element.110, f32[512,4,768]{2,0,1:T(8,128)S(1)} %fusion.16, f32[4,768]{1,0:T(4,128)S(1)} %bitcast.106), kind=kOutput, calls=%fused_computation.23 | convolution fusion | flops 2432434176 | bytes 14171136 | tf_op jit(solution)/shard_map/stf,tdf->sd/dot_general | solution.py:1938
  122.7 1.3 slice_reduce_fusion.3
  124.8 1.6 fusion.12
  126.4 10.7 %convert_reduce_fusion = (f32[4,768]{1,0:T(4,128)S(1)}, bf16[512,4,768]{2,0,1:T(8,128)(2,1)S(1)}) fusion(bf16[512,768,1]{1,0,2:T(8,128)(2,1)S(1)} %fusion.12, bf16[4,768,768]{2,1,0:T(8,128)(2,1)} %bitcast.120, f32[512,4,768]{2,0,1:T(8,128)} %copy-done.14, f32[4,768]{1,0:T(4,128)S(1)} %bitcast.107), kind=kOutput, calls=%fused_computation.10 | convolution fusion | flops 2458383360 | bytes 14966784 | tf_op jit(solution)/shard_map/sd,tdf->stf/dot_general | solution.py:1943
  137.1 3.0 %fusion.7 = (f32[768]{0:T(1024)S(1)}, f32[512]{0:T(512)S(1)}, f32[512]{0:T(512)S(1)}, f32[768]{0:T(1024)S(1)}, f32[512,768,1]{1,0,2:T(8,128)S(1)}) fusion(f32[512,768]{1,0:T(8,128)S(1)} %copy-done, f32[512]{0:T(512)S(1)} %add_rsqrt_fusion, f32[512]{0:T(512)S(1)} %broadcast_multiply_fusion.2, f32[768]{0:T(1024)S(1)} %get-tuple-element.109, ...), kind=kOutput, calls=%fused_computation.21 | convolution fusion | flops 2419455488 | bytes 11027456 | tf_op jit(solution)/shard_map/stf,tdf->sd/dot_general | solution.py:1948
  140.2 2.9 %fusion.6 = (f32[]{:T(128)}, f32[768]{0:T(1024)S(1)}, f32[768]{0:T(1024)S(1)}, f32[512,768]{1,0:T(8,128)}, bf16[1,512,768]{2,1,0:T(8,128)(2,1)}) fusion(f32[512]{0:T(512)S(1)} %bitcast.105, f32[512,768]{1,0:T(8,128)S(1)} %fusion.8, bf16[1,512,768]{2,1,0:T(8,128)(2,1)S(1)} %copy-done.1, f32[]{:T(128)S(6)} %div.17, f32[512]{0:T(512)S(1)} %get-tuple-element.127, ...), kind=kLoop, calls=%fused_computation.16 | loop fusion | flops 6683135 | bytes 7883784 | tf_op jit(solution)/shard_map/reduce_sum | solution.py:1940
  143.1 0.7 broadcast_in_dim.140
  143.8 1.3 concatenate.15.small_ref
  145.1 8.6 %convolution_convert_fusion.1 = bf16[4,768,768]{1,2,0:T(8,128)(2,1)} fusion(bf16[512,768,1]{1,0,2:T(8,128)(2,1)} %copy-done.2, f32[512,4,768]{2,0,1:T(8,128)} %copy-done.14, f32[4,768]{1,0:T(4,128)S(1)} %bitcast.108), kind=kOutput, calls=%fused_computation.13 | convolution fusion | flops 2434007040 | bytes 11808768 | tf_op jit(solution)/shard_map/sd,stf->tdf/dot_general | solution.py:1944
  153.7 4.7 %convolution_convert_fusion = bf16[4,768,768]{1,2,0:T(8,128)(2,1)} fusion(bf16[512,4,768]{2,0,1:T(8,128)(2,1)S(1)} %copy-done.16, f32[512,768]{1,0:T(8,128)S(1)} %copy-done, f32[768]{0:T(1024)S(1)} %get-tuple-element.111, f32[768]{0:T(1024)S(1)} %get-tuple-element.109, f32[512]{0:T(512)S(1)} %add_rsqrt_fusion, f32[512]{0:T(512)S(1)} %broadcast_multiply_fusion.2), kind=kOutput, calls=%fused_computation.12 | convolution fusion | flops 2420244480 | bytes 9447424 | tf_op jit(solution)/shard_map/sd,stf->tdf/dot_general | solution.py:1947
  158.3 122.6 %back.1 = (f32[512,768]{1,0:T(8,128)}, f32[1,1]{1,0:T(1,128)}, f32[1,96]{1,0:T(1,128)}, f32[1,96]{1,0:T(1,128)}, f32[3,96,192]{2,1,0:T(8,128)}, /*index=5*/f32[3...) custom-call(bf16[512,768]{1,0:T(8,128)(2,1)} %bitcast.98, ...), custom_call_target="tpu_custom_call" | custom-call | tf_op jit(solution)/shard_map/back/pallas_call | solution.py:1199
  281.0 1.4 copy.42
  283.2 2.7 copy.64
  285.8 0.5 copy.65
  286.3 0.5 copy.66
  286.9 0.7 copy.67
  287.6 0.6 copy.68
  288.1 0.6 copy.69
  288.8 0.5 copy.70
  289.3 0.5 copy.71
  289.8 0.5 copy.72
  290.3 0.7 copy.73
  291.1 0.7 copy.74
  291.8 0.5 copy.75
  (70 shorter events, 0.2 us)
Async XLA Ops:
  108.4 4.4 %copy-start = (f32[512,768]{1,0:T(8,128)S(1)}, f32[512,768]{1,0:T(8,128)}, u32[]{:S(2)}) copy-start(f32[512,768]{1,0:T(8,128)} %get-tuple-element.44) | copy-start | bytes 4718596
  110.9 7.8 %slice-start.2 = ((s8[4718592]{0:T(1024)(128)(4,1)}), s8[4194304]{0:T(1024)(128)(4,1)S(1)}, s32[]{:S(2)}) async-start(s8[4718592]{0:T(1024)(128)(4,1)} %bitcast.121), calls=%async_computation.2 | async-start | bytes 8388608
  112.8 5.9 %slice-start.3 = ((s8[4718592]{0:T(1024)(128)(4,1)}), s8[524288]{0:T(1024)(128)(4,1)S(1)}, s32[]{:S(2)}) async-start(s8[4718592]{0:T(1024)(128)(4,1)} %bitcast.121), calls=%async_computation.3 | async-start | bytes 1048576
  117.7 5.0 %copy-start.14 = (f32[512,4,768]{2,0,1:T(8,128)}, f32[512,4,768]{2,0,1:T(8,128)S(1)}, u32[]{:S(2)}) copy-start(f32[512,4,768]{2,0,1:T(8,128)S(1)} %fusion.16) | copy-start | bytes 18874372
  124.8 12.3 %slice-start = ((s8[4718592]{0:T(1024)(128)(4,1)}), s8[4194304]{0:T(1024)(128)(4,1)S(1)}, s32[]{:S(2)}) async-start(s8[4718592]{0:T(1024)(128)(4,1)} %bitcast.117), calls=%async_computation | async-start | bytes 8388608
  126.3 10.7 %copy-start.2 = (bf16[512,768,1]{1,0,2:T(8,128)(2,1)}, bf16[512,768,1]{1,0,2:T(8,128)(2,1)S(1)}, u32[]{:S(2)}) copy-start(bf16[512,768,1]{1,0,2:T(8,128)(2,1)S(1)} %fusion.12) | copy-start | bytes 2359300
  126.3 10.8 %slice-start.1 = ((s8[4718592]{0:T(1024)(128)(4,1)}), s8[524288]{0:T(1024)(128)(4,1)S(1)}, s32[]{:S(2)}) async-start(s8[4718592]{0:T(1024)(128)(4,1)} %bitcast.117), calls=%async_computation.1 | async-start | bytes 1048576
  137.1 3.1 %copy-start.15 = (bf16[512,4,768]{2,0,1:T(8,128)(2,1)}, bf16[512,4,768]{2,0,1:T(8,128)(2,1)S(1)}, u32[]{:S(2)}) copy-start(bf16[512,4,768]{2,0,1:T(8,128)(2,1)S(1)} %get-tuple-element.126) | copy-start | bytes 9437188
  137.1 3.1 %copy-start.1 = (bf16[1,512,768]{2,1,0:T(8,128)(2,1)S(1)}, bf16[1,512,768]{2,1,0:T(8,128)(2,1)}, u32[]{:S(2)}) copy-start(bf16[1,512,768]{2,1,0:T(8,128)(2,1)} %param.17) | copy-start | bytes 2359300
  145.1 8.6 %copy-start.16 = (bf16[512,4,768]{2,0,1:T(8,128)(2,1)S(1)}, bf16[512,4,768]{2,0,1:T(8,128)(2,1)}, u32[]{:S(2)}) copy-start(bf16[512,4,768]{2,0,1:T(8,128)(2,1)} %copy-done.15) | copy-start | bytes 9437188
  280.9 4.9 %copy-start.13 = (f32[1,96]{1,0:T(1,128)S(1)}, f32[1,96]{1,0:T(1,128)}, u32[]{:S(2)}) copy-start(f32[1,96]{1,0:T(1,128)} %get-tuple-element.61) | copy-start | bytes 1156
  280.9 5.4 %copy-start.12 = (f32[1,96]{1,0:T(1,128)S(1)}, f32[1,96]{1,0:T(1,128)}, u32[]{:S(2)}) copy-start(f32[1,96]{1,0:T(1,128)} %get-tuple-element.62) | copy-start | bytes 1156
  280.9 5.9 %copy-start.5 = (f32[3,96,192]{2,1,0:T(8,128)S(1)}, f32[3,96,192]{2,1,0:T(8,128)}, u32[]{:S(2)}) copy-start(f32[3,96,192]{2,1,0:T(8,128)} %get-tuple-element.149) | copy-start | bytes 663556
  281.0 6.6 %copy-start.7 = (f32[3,2,8]{2,1,0:T(2,128)S(1)}, f32[3,2,8]{2,1,0:T(2,128)}, u32[]{:S(2)}) copy-start(f32[3,2,8]{2,1,0:T(2,128)} %get-tuple-element.64) | copy-start | bytes 580
  281.0 7.2 %copy-start.6 = (f32[192,96]{1,0:T(8,128)S(1)}, f32[192,96]{1,0:T(8,128)}, u32[]{:S(2)}) copy-start(f32[192,96]{1,0:T(8,128)} %get-tuple-element.151) | copy-start | bytes 221188
  281.0 7.8 %copy-start.11 = (f32[1,96]{1,0:T(1,128)S(1)}, f32[1,96]{1,0:T(1,128)}, u32[]{:S(2)}) copy-start(f32[1,96]{1,0:T(1,128)} %get-tuple-element.66) | copy-start | bytes 1156
  281.0 8.3 %copy-start.10 = (f32[1,96]{1,0:T(1,128)S(1)}, f32[1,96]{1,0:T(1,128)}, u32[]{:S(2)}) copy-start(f32[1,96]{1,0:T(1,128)} %get-tuple-element.67) | copy-start | bytes 1156
  281.0 8.8 %copy-start.9 = (f32[1,96]{1,0:T(1,128)S(1)}, f32[1,96]{1,0:T(1,128)}, u32[]{:S(2)}) copy-start(f32[1,96]{1,0:T(1,128)} %get-tuple-element.68) | copy-start | bytes 1156
  281.0 9.3 %copy-start.4 = (f32[96,768]{1,0:T(8,128)S(1)}, f32[96,768]{1,0:T(8,128)}, u32[]{:S(2)}) copy-start(f32[96,768]{1,0:T(8,128)} %get-tuple-element.155) | copy-start | bytes 884740
  281.0 10.0 %copy-start.3 = (f32[96,768]{1,0:T(8,128)S(1)}, f32[96,768]{1,0:T(8,128)}, u32[]{:S(2)}) copy-start(f32[96,768]{1,0:T(8,128)} %get-tuple-element.71) | copy-start | bytes 884740
  281.0 10.7 %copy-start.8 = (f32[1,96]{1,0:T(1,128)S(1)}, f32[1,96]{1,0:T(1,128)}, u32[]{:S(2)}) copy-start(f32[1,96]{1,0:T(1,128)} %get-tuple-element.72) | copy-start | bytes 1156

commit v4 on v3

--- a/solution.py
+++ b/solution.py
@@ -237,7 +237,8 @@
     ts,
     x_ref,
     seg_ref,
-    small_ref,
+    valid_ref,
+    small_in,
     qkvo_ref,
     fc_ref,
     proj_ref,
@@ -256,6 +257,7 @@
     lse_ref,
     mixed_ref,
     hidden_ref,
+    small_ref,
     small_all,
     w_ref,
     h2_ref,
@@ -279,6 +281,10 @@
     outs = [small_all, qkvo_all, fc_all, proj_all]
     halo_ref[...] = jnp.zeros_like(halo_ref)
     hseg_ref[...] = jnp.full_like(hseg_ref, -1)
+    row = lax.broadcasted_iota(jnp.int32, small_ref.shape, 0)
+    lane = lax.broadcasted_iota(jnp.int32, small_ref.shape, 1)
+    count = jnp.sum(valid_ref[...].astype(F32), axis=1, keepdims=True)
+    small_ref[...] = jnp.where((row == 7) & (lane == 6 * HD), count, small_in[...])
     meet(dp, ts)
     net = Gather(dp, ts, ins, outs, z_send, z_recv, send_sem, recv_sem)
     stages = len(net.far)
@@ -529,7 +535,7 @@
     net.finish()
 
 
-def front(x, seg, small, qkvo, fc, proj, dp, ts, halo):
+def front(x, seg, valid, small, qkvo, fc, proj, dp, ts, halo):
     tokens, width = x.shape
     rows = fc.shape[0]
     window = halo + tokens
@@ -560,9 +566,10 @@
             s((tokens, width), BF16),
             s((tokens, width), F32),
         ],
-        in_specs=[vmem, vmem] + [any_spec] * 4,
+        in_specs=[vmem] * 4 + [any_spec] * 3,
         out_specs=[any_spec] * 3 + [vmem] * 12,
         scratch_shapes=[
+            pltpu.VMEM((8, width), F32),
             pltpu.VMEM((ts, dp, 8, width), F32),
             pltpu.VMEM((pairs, dp, rows, 512), BF16),
             pltpu.VMEM((ts, dp, rows, 256), BF16),
@@ -583,7 +590,7 @@
             collective_id=1, has_side_effects=True, vmem_limit_bytes=62 << 20
         ),
         name="front",
-    )(x, seg, small, qkvo, fc, proj)
+    )(x, seg, valid, small, qkvo, fc, proj)
 
 
 class Scatter:
@@ -1917,13 +1924,12 @@
             spread(vectors).reshape(6, width),
             spread(fc_bias).reshape(1, -1),
             jnp.concatenate(
-                [qv[0, : 2 * HD], qv[1, : 2 * HD], qv[0, 2 * HD :], qv[1, 2 * HD :], jnp.sum(valid_rows)[None]]
-                + [jnp.zeros((width - 2 * e - 1,), F32)]
+                [qv[0, : 2 * HD], qv[1, : 2 * HD], qv[0, 2 * HD :], qv[1, 2 * HD :], jnp.zeros((width - 2 * e,), F32)]
             )[None],
         ]
     )
     qkvo_all, w_fc, w_proj, vec, kseg, qseg, normed_t, halo_x, q, k, v, ot, lse, mixed, hidden = front(
-        x, segment_ids, small, qkvo, fc_weight, proj_weight.T, dp, ts, HALO
+        x, segment_ids, valid_mask, small, qkvo, fc_weight, proj_weight.T, dp, ts, HALO
     )
     gain_two, bias_two, b_proj = [vec[0, i] for i in (3, 4, 5)]
     b_fc = vec[:, 6]

time: 296 us -> 294 us (level)
  no operation moved by 1% of the time
where the time goes in v4:
time: 294 us; the launch traced here: 291 us
  Pallas kernels  221 us (75%)
  matrix products  35.6 us (12%)
  local copies, waits for them, and re-layouts  19.9 us (7%)
  other arithmetic  10.7 us (4%)
  between operations  3.64 us (1%)
    pallas_call x1, Pallas kernels, back(): pl.pallas_call(functools.partial(back_kernel, dp, ts), out_shape=[s((toke...  122 us
    pallas_call x1, Pallas kernels, front(): pl.pallas_call(functools.partial(front_kernel, dp, ts), out_shape=[big, b...  98.6 us
    unnamed x59, local copies, waits for them, and re-layouts  12.9 us
    dot_general x1, matrix products, on_device(): jnp.einsum('sd,tdf->stf', low_output, wp, preferred_element_type=F32)  10.6 us
    dot_general x1, matrix products, on_device(): jnp.einsum('sd,stf->tdf', low_output, activated, preferred_element_type=F32)  8.57 us

profile of v4, /device:TPU:0, one launch (start us, length us, event | category | flops | bytes accessed | tf_op | source)
XLA Modules:
  0.0 290.9 jit_solution(18363986251878343940)
XLA Ops:
  0.6 0.7 convert_element_type.74
  1.3 0.7 copy.38
  2.0 0.1 broadcast_in_dim.127
  2.1 0.1 broadcast_in_dim.123
  2.2 0.1 broadcast_in_dim.124
  2.4 0.1 concatenate.12
  2.4 0.8 copy.37
  3.2 0.1 select_convert_fusion
  3.3 0.1 reshape.116
  3.4 0.8 stack.27
  4.2 0.1 broadcast_in_dim.118
  4.3 0.1 broadcast_in_dim.114
  4.3 0.1 broadcast_in_dim.115
  4.4 0.6 pad_maximum_fusion.small_in
  5.1 0.9 slice_bitcast_fusion
  5.9 0.9 copy.39
  6.9 0.8 concatenate.14.qkvo_ref
  7.7 98.6 %front.1 = (bf16[4,8,96,768]{3,2,1,0:T(8,128)(2,1)}, bf16[4,8,96,768]{3,2,1,0:T(8,128)(2,1)}, bf16[4,8,96,768]{3,2,1,0:T(8,128)(2,1)}, f32[4,8,768]{2,1,0:T(8,12...) custom-call(bf16[512,768]{1,0:T(8,128)(2,1)} %bitcast.96, ...), custom_call_target="tpu_custom_call" | custom-call | tf_op jit(solution)/shard_map/front/pallas_call | solution.py:550
  106.3 0.9 slice_reduce_fusion.2
  107.2 1.6 reduce_sum.99
  108.8 1.9 multiply_reduce_fusion.1
  110.7 4.8 %fusion.16 = f32[512,4,768]{2,0,1:T(8,128)S(1)} fusion(bf16[4,768,768]{2,1,0:T(8,128)(2,1)} %bitcast.115, f32[512,768]{1,0:T(8,128)S(1)} %copy-done, f32[768]{0:T(1024)S(1)} %get-tuple-element.111, f32[768]{0:T(1024)S(1)} %get-tuple-element.109, f32[512]{0:T(512)S(1)} %add_rsqrt_fusion, f32[512]{0:T(512)S(1)} %broadcast_multiply_fusion.2), kind=kOutput, calls=%fused_computation.57 | convolution fusion | flops 2417885184 | bytes 12593152 | tf_op jit(solution)/shard_map/sd,tdf->stf/dot_general | solution.py:1942
  115.5 1.0 slice.77
  116.5 4.0 %fusion.8 = f32[512,768]{1,0:T(8,128)S(1)} fusion(f32[512,768]{1,0:T(8,128)S(1)} %copy-done, bf16[4,768,768]{2,1,0:T(8,128)(2,1)S(1)} %bitcast.122, f32[768]{0:T(1024)S(1)} %get-tuple-element.110, f32[512,4,768]{2,0,1:T(8,128)S(1)} %fusion.16, f32[4,768]{1,0:T(4,128)S(1)} %bitcast.105), kind=kOutput, calls=%fused_computation.23 | convolution fusion | flops 2432434176 | bytes 14171136 | tf_op jit(solution)/shard_map/stf,tdf->sd/dot_general | solution.py:1944
  120.5 1.3 slice_reduce_fusion.3
  122.6 1.5 fusion.12
  124.1 10.6 %convert_reduce_fusion = (f32[4,768]{1,0:T(4,128)S(1)}, bf16[512,4,768]{2,0,1:T(8,128)(2,1)S(1)}) fusion(bf16[512,768,1]{1,0,2:T(8,128)(2,1)S(1)} %fusion.12, bf16[4,768,768]{2,1,0:T(8,128)(2,1)} %bitcast.119, f32[512,4,768]{2,0,1:T(8,128)} %copy-done.14, f32[4,768]{1,0:T(4,128)S(1)} %bitcast.106), kind=kOutput, calls=%fused_computation.10 | convolution fusion | flops 2458383360 | bytes 14966784 | tf_op jit(solution)/shard_map/sd,tdf->stf/dot_general | solution.py:1949
  134.8 0.0 copy-start.1
  134.8 3.0 %fusion.7 = (f32[768]{0:T(1024)S(1)}, f32[512]{0:T(512)S(1)}, f32[512]{0:T(512)S(1)}, f32[768]{0:T(1024)S(1)}, f32[512,768,1]{1,0,2:T(8,128)S(1)}) fusion(f32[512,768]{1,0:T(8,128)S(1)} %copy-done, f32[512]{0:T(512)S(1)} %add_rsqrt_fusion, f32[512]{0:T(512)S(1)} %broadcast_multiply_fusion.2, f32[768]{0:T(1024)S(1)} %get-tuple-element.109, ...), kind=kOutput, calls=%fused_computation.21 | convolution fusion | flops 2419455488 | bytes 11027456 | tf_op jit(solution)/shard_map/stf,tdf->sd/dot_general | solution.py:1954
  137.9 3.0 %fusion.6 = (f32[]{:T(128)}, f32[768]{0:T(1024)S(1)}, f32[768]{0:T(1024)S(1)}, f32[512,768]{1,0:T(8,128)}, bf16[1,512,768]{2,1,0:T(8,128)(2,1)}) fusion(f32[512]{0:T(512)S(1)} %bitcast.104, f32[512,768]{1,0:T(8,128)S(1)} %fusion.8, bf16[1,512,768]{2,1,0:T(8,128)(2,1)S(1)} %copy-done.1, f32[]{:T(128)S(6)} %div.17, f32[512]{0:T(512)S(1)} %get-tuple-element.127, ...), kind=kLoop, calls=%fused_computation.16 | loop fusion | flops 6683135 | bytes 7883784 | tf_op jit(solution)/shard_map/reduce_sum | solution.py:1946
  140.8 0.7 broadcast_in_dim.136
  141.5 1.3 concatenate.15.small_ref
  142.8 8.6 %convolution_convert_fusion.1 = bf16[4,768,768]{1,2,0:T(8,128)(2,1)} fusion(bf16[512,768,1]{1,0,2:T(8,128)(2,1)} %copy-done.2, f32[512,4,768]{2,0,1:T(8,128)} %copy-done.14, f32[4,768]{1,0:T(4,128)S(1)} %bitcast.107), kind=kOutput, calls=%fused_computation.13 | convolution fusion | flops 2434007040 | bytes 11808768 | tf_op jit(solution)/shard_map/sd,stf->tdf/dot_general | solution.py:1950
  151.4 4.6 %convolution_convert_fusion = bf16[4,768,768]{1,2,0:T(8,128)(2,1)} fusion(bf16[512,4,768]{2,0,1:T(8,128)(2,1)S(1)} %copy-done.16, f32[512,768]{1,0:T(8,128)S(1)} %copy-done, f32[768]{0:T(1024)S(1)} %get-tuple-element.111, f32[768]{0:T(1024)S(1)} %get-tuple-element.109, f32[512]{0:T(512)S(1)} %add_rsqrt_fusion, f32[512]{0:T(512)S(1)} %broadcast_multiply_fusion.2), kind=kOutput, calls=%fused_computation.12 | convolution fusion | flops 2420244480 | bytes 9447424 | tf_op jit(solution)/shard_map/sd,stf->tdf/dot_general | solution.py:1953
  156.0 122.4 %back.1 = (f32[512,768]{1,0:T(8,128)}, f32[1,1]{1,0:T(1,128)}, f32[1,96]{1,0:T(1,128)}, f32[1,96]{1,0:T(1,128)}, f32[3,96,192]{2,1,0:T(8,128)}, /*index=5*/f32[3...) custom-call(bf16[512,768]{1,0:T(8,128)(2,1)} %bitcast.97, ...), custom_call_target="tpu_custom_call" | custom-call | tf_op jit(solution)/shard_map/back/pallas_call | solution.py:1206
  278.5 1.4 copy.42
  280.7 2.7 copy.64
  283.3 0.5 copy.65
  283.8 0.5 copy.66
  284.3 0.7 copy.67
  285.1 0.6 copy.68
  285.6 0.6 copy.69
  286.3 0.5 copy.70
  286.8 0.5 copy.71
  287.3 0.5 copy.72
  287.8 0.7 copy.73
  288.5 0.7 copy.74
  289.3 0.5 copy.75
  (69 shorter events, 0.2 us)
Async XLA Ops:
  106.3 4.4 %copy-start = (f32[512,768]{1,0:T(8,128)S(1)}, f32[512,768]{1,0:T(8,128)}, u32[]{:S(2)}) copy-start(f32[512,768]{1,0:T(8,128)} %get-tuple-element.44) | copy-start | bytes 4718596
  108.8 7.8 %slice-start.2 = ((s8[4718592]{0:T(1024)(128)(4,1)}), s8[4194304]{0:T(1024)(128)(4,1)S(1)}, s32[]{:S(2)}) async-start(s8[4718592]{0:T(1024)(128)(4,1)} %bitcast.120), calls=%async_computation.2 | async-start | bytes 8388608
  110.7 5.9 %slice-start.3 = ((s8[4718592]{0:T(1024)(128)(4,1)}), s8[524288]{0:T(1024)(128)(4,1)S(1)}, s32[]{:S(2)}) async-start(s8[4718592]{0:T(1024)(128)(4,1)} %bitcast.120), calls=%async_computation.3 | async-start | bytes 1048576
  115.5 5.0 %copy-start.14 = (f32[512,4,768]{2,0,1:T(8,128)}, f32[512,4,768]{2,0,1:T(8,128)S(1)}, u32[]{:S(2)}) copy-start(f32[512,4,768]{2,0,1:T(8,128)S(1)} %fusion.16) | copy-start | bytes 18874372
  122.5 12.2 %slice-start = ((s8[4718592]{0:T(1024)(128)(4,1)}), s8[4194304]{0:T(1024)(128)(4,1)S(1)}, s32[]{:S(2)}) async-start(s8[4718592]{0:T(1024)(128)(4,1)} %bitcast.116), calls=%async_computation | async-start | bytes 8388608
  124.1 10.7 %copy-start.2 = (bf16[512,768,1]{1,0,2:T(8,128)(2,1)}, bf16[512,768,1]{1,0,2:T(8,128)(2,1)S(1)}, u32[]{:S(2)}) copy-start(bf16[512,768,1]{1,0,2:T(8,128)(2,1)S(1)} %fusion.12) | copy-start | bytes 2359300
  124.1 10.7 %slice-start.1 = ((s8[4718592]{0:T(1024)(128)(4,1)}), s8[524288]{0:T(1024)(128)(4,1)S(1)}, s32[]{:S(2)}) async-start(s8[4718592]{0:T(1024)(128)(4,1)} %bitcast.116), calls=%async_computation.1 | async-start | bytes 1048576
  134.8 3.1 %copy-start.15 = (bf16[512,4,768]{2,0,1:T(8,128)(2,1)}, bf16[512,4,768]{2,0,1:T(8,128)(2,1)S(1)}, u32[]{:S(2)}) copy-start(bf16[512,4,768]{2,0,1:T(8,128)(2,1)S(1)} %get-tuple-element.126) | copy-start | bytes 9437188
  134.8 3.0 %copy-start.1 = (bf16[1,512,768]{2,1,0:T(8,128)(2,1)S(1)}, bf16[1,512,768]{2,1,0:T(8,128)(2,1)}, u32[]{:S(2)}) copy-start(bf16[1,512,768]{2,1,0:T(8,128)(2,1)} %param.17) | copy-start | bytes 2359300
  142.8 8.6 %copy-start.16 = (bf16[512,4,768]{2,0,1:T(8,128)(2,1)S(1)}, bf16[512,4,768]{2,0,1:T(8,128)(2,1)}, u32[]{:S(2)}) copy-start(bf16[512,4,768]{2,0,1:T(8,128)(2,1)} %copy-done.15) | copy-start | bytes 9437188
  278.4 4.9 %copy-start.13 = (f32[1,96]{1,0:T(1,128)S(1)}, f32[1,96]{1,0:T(1,128)}, u32[]{:S(2)}) copy-start(f32[1,96]{1,0:T(1,128)} %get-tuple-element.61) | copy-start | bytes 1156
  278.4 5.4 %copy-start.12 = (f32[1,96]{1,0:T(1,128)S(1)}, f32[1,96]{1,0:T(1,128)}, u32[]{:S(2)}) copy-start(f32[1,96]{1,0:T(1,128)} %get-tuple-element.62) | copy-start | bytes 1156
  278.4 5.9 %copy-start.5 = (f32[3,96,192]{2,1,0:T(8,128)S(1)}, f32[3,96,192]{2,1,0:T(8,128)}, u32[]{:S(2)}) copy-start(f32[3,96,192]{2,1,0:T(8,128)} %get-tuple-element.149) | copy-start | bytes 663556
  278.4 6.6 %copy-start.7 = (f32[3,2,8]{2,1,0:T(2,128)S(1)}, f32[3,2,8]{2,1,0:T(2,128)}, u32[]{:S(2)}) copy-start(f32[3,2,8]{2,1,0:T(2,128)} %get-tuple-element.64) | copy-start | bytes 580
  278.4 7.2 %copy-start.6 = (f32[192,96]{1,0:T(8,128)S(1)}, f32[192,96]{1,0:T(8,128)}, u32[]{:S(2)}) copy-start(f32[192,96]{1,0:T(8,128)} %get-tuple-element.151) | copy-start | bytes 221188
  278.5 7.8 %copy-start.11 = (f32[1,96]{1,0:T(1,128)S(1)}, f32[1,96]{1,0:T(1,128)}, u32[]{:S(2)}) copy-start(f32[1,96]{1,0:T(1,128)} %get-tuple-element.66) | copy-start | bytes 1156
  278.5 8.3 %copy-start.10 = (f32[1,96]{1,0:T(1,128)S(1)}, f32[1,96]{1,0:T(1,128)}, u32[]{:S(2)}) copy-start(f32[1,96]{1,0:T(1,128)} %get-tuple-element.67) | copy-start | bytes 1156
  278.5 8.8 %copy-start.9 = (f32[1,96]{1,0:T(1,128)S(1)}, f32[1,96]{1,0:T(1,128)}, u32[]{:S(2)}) copy-start(f32[1,96]{1,0:T(1,128)} %get-tuple-element.68) | copy-start | bytes 1156
  278.5 9.3 %copy-start.4 = (f32[96,768]{1,0:T(8,128)S(1)}, f32[96,768]{1,0:T(8,128)}, u32[]{:S(2)}) copy-start(f32[96,768]{1,0:T(8,128)} %get-tuple-element.155) | copy-start | bytes 884740
  278.5 10.0 %copy-start.3 = (f32[96,768]{1,0:T(8,128)S(1)}, f32[96,768]{1,0:T(8,128)}, u32[]{:S(2)}) copy-start(f32[96,768]{1,0:T(8,128)} %get-tuple-element.71) | copy-start | bytes 884740
  278.5 10.7 %copy-start.8 = (f32[1,96]{1,0:T(1,128)S(1)}, f32[1,96]{1,0:T(1,128)}, u32[]{:S(2)}) copy-start(f32[1,96]{1,0:T(1,128)} %get-tuple-element.72) | copy-start | bytes 1156
